TPU v7x, 32 devices: a whole 2x2x4 slice. The times are simulated.
32 devices in a mesh: dp: 8 (over z, x), sub: 4 (over y, core).
Axes of the slice: x: 2, y: 2, z: 4, core: 2. Of those that a mesh axis runs over, the one named last changes fastest.
Arguments:
- queries: bfloat16 [1024, 4096], P('dp', 'sub'), may hold values from -1 to 1
- passages: bfloat16 [48, 4096], P('dp', 'sub'), may hold values from -1 to 1
- positive_bank: bfloat16 [2048, 4096], P('dp', 'sub'), may hold values from -1 to 1
- positive_ids: int32 [1024, 16], P('dp'), may hold values from -1 to 2047, as said below
- positive_counts: int32 [1024], P('dp'), may hold values from 1 to 16
Outputs:
- losses: float32 [1024], P('dp')
- query_grad: float32 [1024, 4096], P('dp', 'sub')
- passage_grad: float32 [48, 4096], P('dp', 'sub')
- bank_grad: float32 [2048, 4096], P('dp', 'sub')
Inputs may be any that keep to these rules, and one draw needn't show every extreme that they name: `positive_ids`: entries of row i before position positive_counts[i] are rows of positive_bank, the rest are -1. The valid entries of the 128 queries of one index of dp name rows held by any one index of dp at most 32 times in all (repeats counted), a bound that is reached. In each aligned block of 16 queries at most one query has more than one valid entry.
All inputs are finite; a program needn't handle non-finite values.
Results may differ from a plain program's by a relative error of at most 0.0019.
Values may be sent and summed in bfloat16 or wider, within the bound.
No kernel may reach another device: no remote copies, remote signals or barrier semaphores. Data moves between devices by JAX's collectives and lax.ppermute only.
A program may use at most 64 MiB of HBM per device.

v0:
```python
import jax
import jax.numpy as jnp
from jax import lax
from jax.sharding import PartitionSpec as P


def softmax_terms(score_sums, pos_sums, counts):
    scores = score_sums * 50.0
    pos_scores = pos_sums * 50.0
    is_valid = jnp.arange(pos_scores.shape[1])[None, :] < counts[:, None]
    row_max = jnp.maximum(jnp.max(scores, 1), jnp.max(jnp.where(is_valid, pos_scores, -jnp.inf), 1))
    row_total = jnp.sum(jnp.exp(scores - row_max[:, None]), 1)
    row_total = row_total + jnp.sum(
        jnp.exp(jnp.where(is_valid, pos_scores - row_max[:, None], -jnp.inf)), 1
    )
    log_total = row_max + jnp.log(row_total)
    inv_count = 1.0 / counts.astype(jnp.float32)
    query_loss = log_total - jnp.sum(jnp.where(is_valid, pos_scores, 0.0), 1) * inv_count
    weights = jnp.exp(scores - log_total[:, None]).astype(jnp.bfloat16)
    coeffs = jnp.where(
        is_valid,
        jnp.exp(jnp.where(is_valid, pos_scores - log_total[:, None], -jnp.inf))
        - inv_count[:, None],
        0.0,
    )
    return (query_loss, weights, coeffs)


def body(queries, passages, positive_bank, positive_ids, positive_counts):
    peer_count = lax.axis_size("dp")
    query_count, col_width = queries.shape
    bank_rows = positive_bank.shape[0]
    capacity = bank_rows // 8
    max_pos = positive_ids.shape[1]
    slot_total = peer_count * capacity
    flat_ids = positive_ids.reshape(-1)
    is_live = (jnp.arange(max_pos)[None, :] < positive_counts[:, None]).reshape(-1)
    owner_dev = jnp.where(is_live, flat_ids // bank_rows, 0)
    onehot = ((owner_dev[:, None] == jnp.arange(peer_count)[None, :]) & is_live[:, None]).astype(
        jnp.int32
    )
    slot_rank = jnp.sum(jnp.cumsum(onehot, 0) * onehot, 1) - 1
    slot_of = jnp.where(is_live, owner_dev * capacity + slot_rank, slot_total)
    local_ids = jnp.where(is_live, flat_ids % bank_rows, -1)
    send_ids = jnp.full((slot_total + 1,), -1, jnp.int32).at[slot_of].set(local_ids)[:slot_total]
    slot_request = (
        jnp.zeros((slot_total + 1,), jnp.int32)
        .at[slot_of]
        .set(jnp.arange(flat_ids.shape[0], dtype=jnp.int32))[:slot_total]
    )
    slot_live = send_ids >= 0
    slot_query = slot_request // max_pos
    wanted = lax.all_to_all(
        send_ids.reshape(peer_count, capacity), "dp", split_axis=0, concat_axis=0, tiled=True
    ).reshape(-1)
    served = wanted >= 0
    picked = jnp.where(
        served[:, None],
        positive_bank[jnp.clip(wanted, 0, bank_rows - 1)],
        jnp.zeros((), jnp.bfloat16),
    )
    fetched = lax.all_to_all(
        picked.reshape(peer_count, capacity, col_width),
        "dp",
        split_axis=0,
        concat_axis=0,
        tiled=True,
    ).reshape(slot_total, col_width)
    query_slots = queries[slot_query]
    slot_scores = jnp.einsum("sd,sd->s", query_slots, fetched, preferred_element_type=jnp.float32)
    pos_part = jnp.concatenate([slot_scores, jnp.zeros((1,), jnp.float32)])[slot_of].reshape(
        query_count, max_pos
    )
    all_passages = lax.all_gather(passages, "dp", axis=0, tiled=True)
    score_part = lax.dot_general(
        queries, all_passages, (((1,), (1,)), ((), ())), preferred_element_type=jnp.float32
    )
    score_sums, pos_sums = lax.psum((score_part, pos_part), "sub")
    losses, weights, coeffs = softmax_terms(score_sums, pos_sums, positive_counts)
    slot_coeff = jnp.where(slot_live, coeffs.reshape(-1)[slot_request], 0.0)
    pos_grad = jax.ops.segment_sum(
        slot_coeff[:, None] * fetched.astype(jnp.float32), slot_query, query_count
    )
    query_grad = 50.0 * (
        jnp.dot(weights, all_passages, preferred_element_type=jnp.float32) + pos_grad
    )
    passage_grad = 50.0 * lax.psum_scatter(
        lax.dot_general(
            weights, queries, (((0,), (0,)), ((), ())), preferred_element_type=jnp.float32
        ),
        "dp",
        scatter_dimension=0,
        tiled=True,
    )
    grad_rows = (slot_coeff[:, None] * query_slots.astype(jnp.float32)).reshape(
        peer_count, capacity, col_width
    )
    bank_terms = lax.all_to_all(grad_rows, "dp", split_axis=0, concat_axis=0, tiled=True).reshape(
        slot_total, col_width
    )
    member = (
        jnp.where(served, wanted, bank_rows)[None, :] == jnp.arange(bank_rows)[:, None]
    ).astype(jnp.float32)
    bank_grad = 50.0 * jnp.dot(member, bank_terms, precision=lax.Precision.HIGHEST)
    return (losses, query_grad, passage_grad, bank_grad)


def solution(mesh):
    placed = (P("dp", "sub"), P("dp", "sub"), P("dp", "sub"), P("dp", None), P("dp"))
    return jax.shard_map(
        body,
        mesh=mesh,
        in_specs=placed,
        out_specs=(P("dp"), P("dp", "sub"), P("dp", "sub"), P("dp", "sub")),
        check_vma=False,
    )
```

profile of v0, /device:TPU:0, one launch (start us, length us, event | category | flops | bytes accessed | tf_op | source)
XLA Modules:
  0.0 160.7 jit_solution(311845607783761699)
XLA Ops:
  0.7 0.8 lt.93
  1.8 0.6 copy-done.4
  3.0 2.3 %reduce-window.6 = s32[8,16,128]{2,1,0:T(8,128)S(1)} reduce-window(s32[8,16,128]{2,1,0:T(8,128)S(1)} %fusion.9, s32[]{:T(128)} %constant.33.clone.1), window={size=1x1x128 pad=0_0x0_0x127_0}, to_apply=%region_2.3 | reduce-window | flops 2080768 | bytes 131076 | tf_op jit(solution)/shard_map/reduce-window
  5.3 0.3 slice_reduce_fusion
  6.0 8.0 %scatter_custom_fusion.1 = s32[257]{0:T(512)S(1)} fusion(s32[2048]{0:T(1024)S(1)} %bitcast.47, s32[2048]{0:T(1024)S(1)} %get-tuple-element.15, s32[]{:T(128)} %constant.68.clone.1), kind=kCustom, calls=%fused_computation.79 | custom fusion | bytes 1032 | tf_op jit(solution)/shard_map/scatter | solution.py:45
  14.2 13.6 %all_to_all.19 = s32[8,1,32]{2,1,0:T(1,128)S(1)} all-to-all(s32[8,1,32]{2,1,0:T(1,128)S(1)} %all_to_all.12), channel_id=1, replica_groups=mesh['dp'=8,'sub'=4] {'dp'}, dimensions={0} | all-to-all | bytes 2048 | tf_op jit(solution)/shard_map/all_to_all | solution.py:53
  27.8 1.2 gather_fusion.1
  29.0 0.9 broadcast_select_fusion
  29.9 3.6 %all-to-all-start.1 = ((bf16[8,32,1024]{2,1,0:T(8,128)(2,1)}), bf16[8,32,1024]{2,1,0:T(8,128)(2,1)S(1)}, u32[]{:S(2)}, u32[]{:S(2)}) async-start(bf16[8,32,1024]{2,1,0:T(8,128)(2,1)} %broadcast_select_fusion), calls=%async_computation.1 | async-start | bytes 1048576 | tf_op jit(solution)/shard_map/all_to_all | solution.py:62
  33.6 36.1 %all-gather = bf16[8,6,1024]{2,1,0:T(8,128)(2,1)S(1)} all-gather(bf16[1,6,1024]{2,1,0:T(8,128)(2,1)S(1)} %bitcast.51), channel_id=1, replica_groups=mesh['dp'=8,'sub'=4] {'dp'}, dimensions={0}, use_global_device_ids=true | all-gather | bytes 110592 | tf_op jit(solution)/shard_map/all_gather | solution.py:74
  69.7 8.0 %scatter_custom_fusion = s32[257]{0:T(512)S(1)} fusion(s32[2048]{0:T(1024)S(1)} %bitcast.48, s32[2048]{0:T(1024)S(1)} %iota.22, s32[]{:T(128)} %constant.33.clone.1), kind=kCustom, calls=%fused_computation.81 | custom fusion | bytes 1032 | tf_op jit(solution)/shard_map/scatter | solution.py:49
  77.8 1.2 gather_fusion
  79.2 0.2 fusion.1
  79.5 13.2 %gather_fusion.2 = f32[2048]{0:T(1024)S(1)} fusion(f32[257]{0:T(512)S(1)} %pad_maximum_fusion, s32[2048]{0:T(1024)S(1)} %broadcast_clamp_fusion), kind=kCustom, calls=%fused_computation.2 | custom fusion | bytes 24576 | tf_op jit(solution)/shard_map/gather | solution.py:71
  92.8 11.1 %all-reduce.2 = (f32[128,48]{0,1:T(8,128)S(1)}, f32[128,16]{1,0:T(8,128)S(1)}) all-reduce(f32[128,48]{0,1:T(8,128)S(1)} %fusion.25, f32[128,16]{1,0:T(8,128)S(1)} %reshape.300), channel_id=1, replica_groups=mesh['dp'=8,'sub'=4] {'sub'}, use_global_device_ids=true, to_apply=%region_0.1 | all-reduce | flops 8192 | bytes 65536 | tf_op jit(solution)/shard_map/psum | solution.py:78
  104.3 0.5 multiply_subtract_fusion
  105.1 1.7 %gather_fusion.3 = f32[256]{0:T(256)S(1)} fusion(f32[2048]{0:T(1024)S(1)} %reshape.301, s32[1024]{0:T(1024)S(1)} %pad_clamp_fusion), kind=kCustom, calls=%fused_computation.3 | custom fusion | bytes 3072 | tf_op jit(solution)/shard_map/gather | solution.py:80
  106.9 1.1 convert_multiply_fusion.3
  108.0 3.6 %all-to-all-start.2 = ((f32[8,32,1024]{2,1,0:T(8,128)}), f32[8,32,1024]{2,1,0:T(8,128)S(1)}, u32[]{:S(2)}, u32[]{:S(2)}) async-start(f32[8,32,1024]{2,1,0:T(8,128)} %convert_multiply_fusion.3), calls=%async_computation.2 | async-start | bytes 2097152 | tf_op jit(solution)/shard_map/all_to_all | solution.py:98
  111.6 0.6 copy-done.5
  112.2 0.6 dynamic-slice.4
  113.5 0.5 broadcast.285
  114.0 0.7 reduce.7
  114.9 31.8 %fusion = f32[8,1024]{1,0:T(8,128)S(1)} fusion(f32[48,1024]{1,0:T(8,128)S(1)} %fusion.17), kind=kCustom, calls=%all-reduce-scatter | all-reduce-scatter fusion | flops 65537 | bytes 229888
  146.7 3.2 %collective-permute-start = (f32[8,1024]{1,0:T(8,128)S(1)}, f32[8,1024]{1,0:T(8,128)S(1)}, u32[]{:S(2)}, u32[]{:S(2)}) collective-permute-start(f32[8,1024]{1,0:T(8,128)S(1)} %fusion), channel_id=1, source_target_pairs={{0,4},{4,8},{8,12},{12,16},{16,20},{20,24},{24,28},{1,5},{5,9},{9,... | collective-permute-start | bytes 98312
  149.9 4.2 %collective-permute-start.1 = (f32[6,1024]{1,0:T(8,128)S(1)}, f32[6,1024]{1,0:T(8,128)S(1)}, u32[]{:S(2)}, u32[]{:S(2)}) collective-permute-start(f32[6,1024]{1,0:T(8,128)S(1)} %slice.25), channel_id=1, source_target_pairs={{0,8},{4,12},{8,16},{12,20},{16,24},{20,28},{1,9},{5,13},{9,17},{1... | collective-permute-start | bytes 73736
  154.1 0.2 fusion.18
  154.3 3.0 %scatter_custom_fusion.2 = f32[128,1024]{1,0:T(8,128)S(1)} fusion(f32[128,1024]{1,0:T(8,128)S(1)} %fusion.18, s32[256]{0:T(256)S(1)} %get-tuple-element.12, bf16[256,1024]{1,0:T(8,128)(2,1)S(1)} %bitcast.42, f32[256]{0:T(256)S(1)} %compare_select_fusion.7), kind=kCustom, calls=%fused_computation.11 | custom fusion | flops 786432 | bytes 1049600 | tf_op jit(solution)/shard_map/scatter-add | solution.py:81
  157.3 0.8 broadcast_multiply_fusion
  158.2 0.2 concatenate.4
  158.4 0.6 dynamic-slice_multiply_fusion
  159.0 1.7 %convolution_multiply_fusion = f32[256,1024]{1,0:T(8,128)} fusion(f32[256,1024]{1,0:T(8,128)S(1)} %bitcast.43, s32[256]{0:T(256)S(1)} %compare_select_fusion.5), kind=kOutput, calls=%fused_computation.7 | convolution fusion | flops 805634048 | bytes 2098176 | tf_op jit(solution)/shard_map/dot_general | solution.py:104
  (62 shorter events, 2.8 us)
Async XLA Ops:
  0.6 27.2 %copy-start = (bf16[256,1024]{1,0:T(8,128)(2,1)S(1)}, bf16[256,1024]{1,0:T(8,128)(2,1)}, u32[]{:S(2)}) copy-start(bf16[256,1024]{1,0:T(8,128)(2,1)} %param.7) | copy-start | bytes 1572868
  0.6 0.8 copy-start.2
  1.7 0.7 copy-start.4
  29.9 3.6 %copy-start.3 = (bf16[6,1024]{1,0:T(8,128)(2,1)S(1)}, bf16[6,1024]{1,0:T(8,128)(2,1)}, u32[]{:S(2)}) copy-start(bf16[6,1024]{1,0:T(8,128)(2,1)} %param.6) | copy-start | bytes 36868
  29.9 49.3 %all-to-all-start.1 = ((bf16[8,32,1024]{2,1,0:T(8,128)(2,1)}), bf16[8,32,1024]{2,1,0:T(8,128)(2,1)S(1)}, u32[]{:S(2)}, u32[]{:S(2)}) async-start(bf16[8,32,1024]{2,1,0:T(8,128)(2,1)} %broadcast_select_fusion), calls=%async_computation.1 | async-start | bytes 1048576 | tf_op jit(solution)/shard_map/all_to_all | solution.py:62
  33.5 44.3 %copy-start.1 = (bf16[128,1024]{1,0:T(8,128)(2,1)S(1)}, bf16[128,1024]{1,0:T(8,128)(2,1)}, u32[]{:S(2)}) copy-start(bf16[128,1024]{1,0:T(8,128)(2,1)} %param.5) | copy-start | bytes 786436
  108.0 51.0 %all-to-all-start.2 = ((f32[8,32,1024]{2,1,0:T(8,128)}), f32[8,32,1024]{2,1,0:T(8,128)S(1)}, u32[]{:S(2)}, u32[]{:S(2)}) async-start(f32[8,32,1024]{2,1,0:T(8,128)} %convert_multiply_fusion.3), calls=%async_computation.2 | async-start | bytes 2097152 | tf_op jit(solution)/shard_map/all_to_all | solution.py:98
  111.6 0.7 copy-start.5
  146.7 11.5 %collective-permute-start = (f32[8,1024]{1,0:T(8,128)S(1)}, f32[8,1024]{1,0:T(8,128)S(1)}, u32[]{:S(2)}, u32[]{:S(2)}) collective-permute-start(f32[8,1024]{1,0:T(8,128)S(1)} %fusion), channel_id=1, source_target_pairs={{0,4},{4,8},{8,12},{12,16},{16,20},{20,24},{24,28},{1,5},{5,9},{9,... | collective-permute-start | bytes 98312
  149.9 8.3 %collective-permute-start.1 = (f32[6,1024]{1,0:T(8,128)S(1)}, f32[6,1024]{1,0:T(8,128)S(1)}, u32[]{:S(2)}, u32[]{:S(2)}) collective-permute-start(f32[6,1024]{1,0:T(8,128)S(1)} %slice.25), channel_id=1, source_target_pairs={{0,8},{4,12},{8,16},{12,20},{16,24},{20,28},{1,9},{5,13},{9,17},{1... | collective-permute-start | bytes 73736
where the time goes:
time: 161 us
  blocking collectives  92.6 us (58%)
  local copies, waits for them, and re-layouts  38.3 us (24%)
  starting transfers between devices  14.5 us (9%)
  other arithmetic  11.3 us (7%)
  matrix products  2.25 us (1%)
  between operations  1.68 us (1%)
    all_gather x1, blocking collectives, body(): all_passages = lax.all_gather(passages, 'dp', axis=0, tiled=True)  36.1 us
    unnamed x1, blocking collectives  31.8 us
    all_to_all x1, blocking collectives, body(): lax.all_to_all(send_ids.reshape(peer_count, capacity), 'dp', split_axis=0...  13.6 us
    gather x1, local copies, waits for them, and re-layouts, body(): jnp.concatenate([slot_scores, jnp.zeros((1,), jnp.float32)])[slot_of]  13.2 us
    psum x1, blocking collectives, body(): score_sums, pos_sums = lax.psum((score_part, pos_part), 'sub')  11.1 us
    scatter x1, local copies, waits for them, and re-layouts, body(): jnp.full((slot_total + 1,), -1, jnp.int32).at[slot_of].set(local_ids)  8.04 us
    scatter x1, local copies, waits for them, and re-layouts, body(): slot_request = jnp.zeros((slot_total + 1,), jnp.int32).at[slot_of].set(jn...  8.03 us
    unnamed x2, starting transfers between devices  7.36 us
  transfers between devices with their start and end apart: 4, of which 0 were waited for; matrix products, arithmetic and copies ran while one was open for 30% of the time, Pallas kernels for 0%

commit v1 on v0

v1 whole, which is shorter than its diff:
```python
import jax
import jax.numpy as jnp
from jax import lax
from jax.sharding import PartitionSpec as P

BF = jnp.bfloat16
F32 = jnp.float32


def exchange(x):
    return lax.all_to_all(x, "dp", split_axis=0, concat_axis=0, tiled=True)


def sub_sum(x):
    size = lax.axis_size("sub")
    step = 1
    while step < size:
        x = x + lax.ppermute(x, "sub", [(i, i ^ step) for i in range(size)])
        step *= 2
    return x


def split(x):
    hi = lax.reduce_precision(x, 8, 7)
    return hi.astype(BF), (x - hi).astype(BF)


def dot(a, b, ca, cb):
    return lax.dot_general(a, b, (((ca,), (cb,)), ((), ())), preferred_element_type=F32)


def body(queries, passages, bank, ids, counts):
    peers = lax.axis_size("dp")
    q_rows, width = queries.shape
    bank_rows = bank.shape[0]
    cap = bank_rows // 8
    places = peers * cap
    pas = passages.shape[0]
    pad = -(-(pas + 1) // 8) * 8
    blocks = q_rows // 16
    max_pos = ids.shape[1]

    first = ids[:, 0]
    rest = jnp.max(ids.reshape(blocks, 16, max_pos), 1)
    rest = jnp.where(jnp.arange(max_pos)[None, :] > 0, rest, -1).reshape(-1)
    sid = jnp.concatenate([first, rest])
    slots = sid.shape[0]
    valid = sid >= 0
    owner = jnp.where(valid, sid // bank_rows, -1)
    at = jnp.arange(slots)
    rank = jnp.sum(
        ((owner[:, None] == owner[None, :]) & (at[:, None] < at[None, :])).astype(F32), 0
    ).astype(jnp.int32)
    place = jnp.where(valid, owner * cap + rank, places)
    perm = jnp.arange(places)[:, None] == place[None, :]
    send_ids = jnp.max(jnp.where(perm, (sid % bank_rows)[None, :], -1), 1)
    q_at = jnp.arange(q_rows)
    owns = jnp.concatenate(
        [
            q_at[:, None] == q_at[None, :],
            (jnp.arange(blocks * max_pos)[:, None] // max_pos == q_at[None, :] // 16)
            & (counts[None, :] > 1),
        ]
    )
    asks = dot(perm.astype(BF), owns.astype(BF), 1, 0)
    asked = asks > 0.5

    head = jnp.broadcast_to(passages[None], (peers, pas, width))
    id_row = jnp.pad(
        send_ids.reshape(peers, 1, cap).astype(BF), ((0, 0), (0, pad - pas - 1), (0, width - cap))
    )
    heads = exchange(jnp.concatenate([head, id_row], 1))
    all_pas = heads.reshape(peers * pad, width)
    wanted = heads[:, pas, :cap].astype(F32).reshape(-1)
    pick = (wanted[:, None] == jnp.arange(bank_rows).astype(F32)[None, :]).astype(BF)
    picked = dot(pick, bank, 1, 0).astype(BF)
    fetched = exchange(picked.reshape(peers, cap, width)).reshape(places, width)
    q_send = dot(asks.astype(BF), queries, 1, 0).astype(BF)
    q_send, fetched = lax.optimization_barrier((q_send, fetched))
    q_got = exchange(q_send.reshape(peers, cap, width)).reshape(places, width)

    part = dot(all_pas, queries, 1, 1)
    pos_part = jnp.sum(jnp.where(asked, dot(fetched, queries, 1, 1), 0.0), 1)
    sums = sub_sum(jnp.concatenate([part, pos_part.reshape(-1, q_rows)])) * 50.0
    real = (jnp.arange(peers * pad) % pad < pas)[:, None]
    scores = jnp.where(real, sums[: peers * pad], -jnp.inf)
    pos = sums[peers * pad :].reshape(places, 1)
    pos_or = jnp.where(asked, pos, -jnp.inf)
    row_max = jnp.maximum(jnp.max(scores, 0), jnp.max(pos_or, 0))
    total = jnp.sum(jnp.exp(scores - row_max), 0) + jnp.sum(jnp.exp(pos_or - row_max), 0)
    log_total = row_max + jnp.log(total)
    inv_count = 1.0 / counts.astype(F32)
    losses = log_total - jnp.sum(jnp.where(asked, pos, 0.0), 0) * inv_count
    weights = jnp.exp(scores - log_total).astype(BF)
    coeffs = jnp.where(asked, jnp.exp(pos_or - log_total) - inv_count, 0.0)
    coeff = jnp.sum(coeffs, 1).reshape(peers, 1, cap)

    pas_part = dot(weights, queries, 1, 0).reshape(peers, pad, width)
    sent = jnp.where(
        jnp.arange(pad)[None, :, None] == pas,
        jnp.pad(coeff, ((0, 0), (0, 0), (0, width - cap))),
        pas_part,
    )
    sent, q_got = lax.optimization_barrier((sent, q_got))
    got = exchange(sent)

    hi, lo = split(coeffs)
    query_grad = 50.0 * (dot(weights, all_pas, 0, 0) + dot(hi, fetched, 0, 0) + dot(lo, fetched, 0, 0))
    passage_grad = 50.0 * jnp.sum(got[:, :pas], 0)
    back = got[:, pas, :cap].reshape(1, -1)
    member = jnp.where(
        wanted[None, :] == jnp.arange(bank_rows).astype(F32)[:, None], back, 0.0
    )
    hi, lo = split(member)
    bank_grad = 50.0 * (dot(hi, q_got, 1, 0) + dot(lo, q_got, 1, 0))
    return (losses, query_grad, passage_grad, bank_grad)


def solution(mesh):
    placed = (P("dp", "sub"), P("dp", "sub"), P("dp", "sub"), P("dp", None), P("dp"))
    return jax.shard_map(
        body,
        mesh=mesh,
        in_specs=placed,
        out_specs=(P("dp"), P("dp", "sub"), P("dp", "sub"), P("dp", "sub")),
        check_vma=False,
    )
```

time: 161 us -> 73.9 us (0.46)
  blocking collectives: 92.6 us -> 0 us
  waiting for transfers between devices: 0.01 us -> 38.4 us
  local copies, waits for them, and re-layouts: 38.3 us -> 3.66 us
  other arithmetic: 11.3 us -> 3.37 us
  matrix products: 2.25 us -> 7.41 us
  starting transfers between devices: 14.5 us -> 19.6 us
    all_to_all x2 -> x4, waiting for transfers between devices: 0.01 us -> 37.2 us  [exchange(): return lax.all_to_all(x, 'dp', split_axis=0, concat_axis=0, tiled=True)]
    all_gather x1 -> x0, blocking collectives: 36.1 us -> none  [body(): all_passages = lax.all_gather(passages, 'dp', axis=0, tiled=True)]
    unnamed x1 -> x0, blocking collectives: 31.8 us -> none
    gather x4 -> x0, local copies, waits for them, and re-layouts: 17.3 us -> none  [the longest x1 13.2 us: body(): jnp.concatenate([slot_scores, jnp.zeros((1,), jnp.float32)])[slot_of]]
    scatter x2 -> x0, local copies, waits for them, and re-layouts: 16.1 us -> none  [the longest x1 8.04 us: body(): jnp.full((slot_total + 1,), -1, jnp.int32).at[slot_of].set(local_ids)]
    all_to_all x1 -> x0, blocking collectives: 13.6 us -> none  [body(): lax.all_to_all(send_ids.reshape(peer_count, capacity), 'dp', split_axis=0...]
    psum x1 -> x0, blocking collectives: 11.1 us -> none  [body(): score_sums, pos_sums = lax.psum((score_part, pos_part), 'sub')]
    all_to_all x2 -> x4, starting transfers between devices: 7.18 us -> 18.1 us  [exchange(): return lax.all_to_all(x, 'dp', split_axis=0, concat_axis=0, tiled=True)]
  transfers between devices with their start and end apart: 4 -> 6, of which waited for: 0 -> 5; matrix products, arithmetic and copies ran while one was open for 30% -> 8% of each run, Pallas kernels for 0% -> 0%
where the time goes in v1:
time: 73.9 us; the launch traced here: 73.3 us
  waiting for transfers between devices  38.4 us (52%)
  starting transfers between devices  19.6 us (27%)
  matrix products  7.41 us (10%)
  local copies, waits for them, and re-layouts  3.66 us (5%)
  other arithmetic  3.37 us (5%)
  between operations  0.82 us (1%)
    all_to_all x4, waiting for transfers between devices, exchange(): return lax.all_to_all(x, 'dp', split_axis=0, concat_axis=0, tiled=True)  37.2 us
    all_to_all x4, starting transfers between devices, exchange(): return lax.all_to_all(x, 'dp', split_axis=0, concat_axis=0, tiled=True)  18.1 us
    dot_general x11, matrix products, dot(): lax.dot_general(a, b, (((ca,), (cb,)), ((), ())), preferred_element_type=...  7.41 us
    unnamed x8, local copies, waits for them, and re-layouts  1.64 us
    ppermute x2, starting transfers between devices, sub_sum(): x = x + lax.ppermute(x, 'sub', [(i, i ^ step) for i in range(size)])  1.59 us
  transfers between devices with their start and end apart: 6, of which 5 were waited for; matrix products, arithmetic and copies ran while one was open for 8% of the time, Pallas kernels for 0%

profile of v1, /device:TPU:0, one launch (start us, length us, event | category | flops | bytes accessed | tf_op | source)
XLA Modules:
  0.0 73.3 jit_solution(1875479057728305689)
XLA Ops:
  0.7 0.7 %slice_bitcast_fusion.1 = s32[128]{0:T(128)S(1)} fusion(s32[128,16]{0,1:T(8,128)} %param.8), kind=kLoop, calls=%fused_computation.107 | loop fusion | bytes 1024 | tf_op jit(solution)/shard_map/concatenate | solution.py:46
  1.4 0.8 %reshape.444 = s32[8,16,16]{1,0,2:T(8,128)S(1)} reshape(s32[128,16]{0,1:T(8,128)} %param.8) | data formatting | bytes 16384 | tf_op jit(solution)/shard_map/reshape | solution.py:44
  2.2 0.3 reduce_max.36
  3.1 0.3 copy-done.2
  3.4 0.7 fusion.16
  4.1 7.3 %all-to-all-start = ((bf16[8,8,1024]{2,1,0:T(8,128)(2,1)}), bf16[8,8,1024]{2,1,0:T(8,128)(2,1)S(1)}, u32[]{:S(2)}, u32[]{:S(2)}) async-start(bf16[8,8,1024]{2,1,0:T(8,128)(2,1)} %fusion.16), calls=%async_computation | async-start | bytes 262144 | tf_op jit(solution)/shard_map/all_to_all | solution.py:11
  11.4 0.6 copy-done.3
  12.2 6.6 %all-to-all-done = bf16[8,8,1024]{2,1,0:T(8,128)(2,1)S(1)} async-done(((bf16[8,8,1024]{2,1,0:T(8,128)(2,1)}), bf16[8,8,1024]{2,1,0:T(8,128)(2,1)S(1)}, u32[]{:S(2)}, u32[]{:S(2)}) %all-to-all-start) | async-done | bytes 131104 | tf_op jit(solution)/shard_map/all_to_all | solution.py:11
  18.8 1.1 %convolution_convert_fusion = bf16[256,1024]{1,0:T(8,128)(2,1)} fusion(bf16[256,1024]{1,0:T(8,128)(2,1)S(1)} %copy-done, f32[256]{0:T(256)S(1)} %iota_convert_fusion, f32[256]{0:T(256)S(1)} %reshape.453), kind=kOutput, calls=%fused_computation.2 | convolution fusion | flops 134545408 | bytes 1050624 | tf_op jit(solution)/shard_map/dot_general | solution.py:29
  20.0 3.5 %all-to-all-start.1 = ((bf16[8,32,1024]{2,1,0:T(8,128)(2,1)}), bf16[8,32,1024]{2,1,0:T(8,128)(2,1)S(1)}, u32[]{:S(2)}, u32[]{:S(2)}) async-start(bf16[8,32,1024]{2,1,0:T(8,128)(2,1)} %bitcast.2), calls=%async_computation.1 | async-start | bytes 1048576 | tf_op jit(solution)/shard_map/all_to_all | solution.py:11
  23.5 0.2 broadcast_compare_fusion
  23.7 0.7 copy-done.1
  24.4 1.1 %convolution_convert_fusion.1 = bf16[256,1024]{1,0:T(8,128)(2,1)} fusion(bf16[128,1024]{1,0:T(8,128)(2,1)S(1)} %copy-done.1, bf16[256,128]{1,0:T(8,128)(2,1)S(1)} %get-tuple-element.17), kind=kOutput, calls=%fused_computation.3 | convolution fusion | flops 67371008 | bytes 851968 | tf_op jit(solution)/shard_map/dot_general | solution.py:29
  25.5 0.2 fusion.20
  25.7 11.0 %all-to-all-done.1 = bf16[8,32,1024]{2,1,0:T(8,128)(2,1)S(1)} async-done(((bf16[8,32,1024]{2,1,0:T(8,128)(2,1)}), bf16[8,32,1024]{2,1,0:T(8,128)(2,1)S(1)}, u32[]{:S(2)}, u32[]{:S(2)}) %all-to-all-start.1) | async-done | bytes 524320 | tf_op jit(solution)/shard_map/all_to_all | solution.py:11
  36.7 0.4 fusion.3
  37.2 1.2 %collective-permute-done = f32[66,128]{1,0:T(8,128)S(1)} collective-permute-done((f32[66,128]{1,0:T(8,128)S(1)}, f32[66,128]{1,0:T(8,128)S(1)}, u32[]{:S(2)}, u32[]{:S(2)}) %collective-permute-start) | collective-permute-done | bytes 33824 | tf_op jit(solution)/shard_map/ppermute | solution.py:18
  38.4 1.5 %collective-permute-start.1 = (f32[66,128]{1,0:T(8,128)S(1)}, f32[66,128]{1,0:T(8,128)S(1)}, u32[]{:S(2)}, u32[]{:S(2)}) collective-permute-start(f32[66,128]{1,0:T(8,128)S(1)} %fusion.60), channel_id=1, source_target_pairs={{0,2},{1,3},{2,0},{3,1},{4,6},{5,7},{6,4},{7,5},{8,10},{9,11},{10,... | collective-permute-start | bytes 101384 | tf_op jit(solution)/shard_map/ppermute | solution.py:18
  39.9 3.7 %all-to-all-start.2 = ((bf16[8,32,1024]{2,1,0:T(8,128)(2,1)}), bf16[8,32,1024]{2,1,0:T(8,128)(2,1)S(1)}, u32[]{:S(2)}, u32[]{:S(2)}) async-start(bf16[8,32,1024]{2,1,0:T(8,128)(2,1)} %bitcast.8), calls=%async_computation.2 | async-start | bytes 1048576 | tf_op jit(solution)/shard_map/all_to_all | solution.py:11
  43.9 0.1 fusion.11
  44.1 0.2 fusion.15
  44.4 0.9 %fusion.2 = f32[8,8,1024]{2,1,0:T(8,128)} fusion(bf16[128,1024]{1,0:T(8,128)(2,1)S(1)} %copy-done.1, f32[8,1024]{1,0:T(8,128)S(1)} %pad_bitcast_fusion, pred[8]{0:T(512)(128)(4,1)S(1)} %iota_compare_fusion.5, f32[66,128]{1,0:T(8,128)S(1)} %add_multiply_fusion, f32[128]{0:T(128)S(1)} %log_add_fusion, pred[64]{0:T(512)(128)(4,1)S(1)} %fusion.52), kind=kOutput, calls=%fused_computation.8 | convolution fusion | flops 16867328 | bytes 591360 | tf_op jit(solution)/shard_map/dot_general | solution.py:29
  45.3 0.3 fusion.37
  45.7 0.3 convolution_add_fusion.1
  46.0 12.2 %all-to-all-done.2 = bf16[8,32,1024]{2,1,0:T(8,128)(2,1)S(1)} async-done(((bf16[8,32,1024]{2,1,0:T(8,128)(2,1)}), bf16[8,32,1024]{2,1,0:T(8,128)(2,1)S(1)}, u32[]{:S(2)}, u32[]{:S(2)}) %all-to-all-start.2) | async-done | bytes 524320 | tf_op jit(solution)/shard_map/all_to_all | solution.py:11
  58.2 3.6 %all-to-all-start.3 = ((f32[8,8,1024]{2,1,0:T(8,128)}), f32[8,8,1024]{2,1,0:T(8,128)S(1)}, u32[]{:S(2)}, u32[]{:S(2)}) async-start(f32[8,8,1024]{2,1,0:T(8,128)} %fusion.2), calls=%async_computation.3 | async-start | bytes 524288 | tf_op jit(solution)/shard_map/all_to_all | solution.py:11
  61.8 0.5 multiply_subtract_fusion
  62.3 1.2 %fusion.1 = f32[128,1024]{1,0:T(8,128)} fusion(f32[128,1024]{1,0:T(8,128)S(1)} %convolution_add_fusion.1, bf16[256,1024]{1,0:T(8,128)(2,1)S(1)} %bitcast.35, pred[256,128]{1,0:T(32,128)(4,1)S(1)} %get-tuple-element.16, f32[128]{0:T(128)S(1)} %convert_divide_fusion, f32[128]{0:T(128)S(1)} %log_add_fusion, f32[256]{0:T(256)S(1)} %slice_bitcast_fusion), kind=kOutput, calls=%fused_computation.6 | convolution fusion | flops 67600384 | bytes 1607680 | tf_op jit(solution)/shard_map/dot_general | solution.py:29
  63.5 7.4 %all-to-all-done.3 = f32[8,8,1024]{2,1,0:T(8,128)S(1)} async-done(((f32[8,8,1024]{2,1,0:T(8,128)}), f32[8,8,1024]{2,1,0:T(8,128)S(1)}, u32[]{:S(2)}, u32[]{:S(2)}) %all-to-all-start.3) | async-done | bytes 262176 | tf_op jit(solution)/shard_map/all_to_all | solution.py:11
  71.0 0.6 broadcast_multiply_fusion
  71.6 0.3 fusion.18
  72.0 1.3 %fusion = f32[256,1024]{1,0:T(8,128)} fusion(f32[256,1024]{1,0:T(8,128)S(1)} %fusion.18, bf16[256,1024]{1,0:T(8,128)(2,1)S(1)} %bitcast.37, f32[256]{0:T(256)S(1)} %broadcast_in_dim.139, f32[256]{0:T(256)S(1)} %reshape.453, f32[256]{0:T(256)S(1)} %iota_convert_fusion), kind=kOutput, calls=%fused_computation.1 | convolution fusion | flops 135069696 | bytes 2624512 | tf_op jit(solution)/shard_map/dot_general | solution.py:29
  (41 shorter events, 1.5 us)
Async XLA Ops:
  0.6 18.2 %copy-start = (bf16[256,1024]{1,0:T(8,128)(2,1)S(1)}, bf16[256,1024]{1,0:T(8,128)(2,1)}, u32[]{:S(2)}) copy-start(bf16[256,1024]{1,0:T(8,128)(2,1)} %param.7) | copy-start | bytes 1572868
  2.7 0.7 copy-start.2
  4.1 14.6 %all-to-all-start = ((bf16[8,8,1024]{2,1,0:T(8,128)(2,1)}), bf16[8,8,1024]{2,1,0:T(8,128)(2,1)S(1)}, u32[]{:S(2)}, u32[]{:S(2)}) async-start(bf16[8,8,1024]{2,1,0:T(8,128)(2,1)} %fusion.16), calls=%async_computation | async-start | bytes 262144 | tf_op jit(solution)/shard_map/all_to_all | solution.py:11
  11.4 0.7 copy-start.3
  20.0 16.8 %all-to-all-start.1 = ((bf16[8,32,1024]{2,1,0:T(8,128)(2,1)}), bf16[8,32,1024]{2,1,0:T(8,128)(2,1)S(1)}, u32[]{:S(2)}, u32[]{:S(2)}) async-start(bf16[8,32,1024]{2,1,0:T(8,128)(2,1)} %bitcast.2), calls=%async_computation.1 | async-start | bytes 1048576 | tf_op jit(solution)/shard_map/all_to_all | solution.py:11
  23.5 1.0 %copy-start.1 = (bf16[128,1024]{1,0:T(8,128)(2,1)S(1)}, bf16[128,1024]{1,0:T(8,128)(2,1)}, u32[]{:S(2)}) copy-start(bf16[128,1024]{1,0:T(8,128)(2,1)} %param.5) | copy-start | bytes 786436
  37.1 1.3 %collective-permute-start = (f32[66,128]{1,0:T(8,128)S(1)}, f32[66,128]{1,0:T(8,128)S(1)}, u32[]{:S(2)}, u32[]{:S(2)}) collective-permute-start(f32[66,128]{1,0:T(8,128)S(1)} %pad_maximum_fusion), channel_id=1, source_target_pairs={{0,1},{1,0},{2,3},{3,2},{4,5},{5,4},{6,7},{7,6},{8,9},{9,8},{10,11... | collective-permute-start | bytes 101384 | tf_op jit(solution)/shard_map/ppermute | solution.py:18
  38.4 5.2 %collective-permute-start.1 = (f32[66,128]{1,0:T(8,128)S(1)}, f32[66,128]{1,0:T(8,128)S(1)}, u32[]{:S(2)}, u32[]{:S(2)}) collective-permute-start(f32[66,128]{1,0:T(8,128)S(1)} %fusion.60), channel_id=1, source_target_pairs={{0,2},{1,3},{2,0},{3,1},{4,6},{5,7},{6,4},{7,5},{8,10},{9,11},{10,... | collective-permute-start | bytes 101384 | tf_op jit(solution)/shard_map/ppermute | solution.py:18
  39.9 18.2 %all-to-all-start.2 = ((bf16[8,32,1024]{2,1,0:T(8,128)(2,1)}), bf16[8,32,1024]{2,1,0:T(8,128)(2,1)S(1)}, u32[]{:S(2)}, u32[]{:S(2)}) async-start(bf16[8,32,1024]{2,1,0:T(8,128)(2,1)} %bitcast.8), calls=%async_computation.2 | async-start | bytes 1048576 | tf_op jit(solution)/shard_map/all_to_all | solution.py:11
  58.2 12.7 %all-to-all-start.3 = ((f32[8,8,1024]{2,1,0:T(8,128)}), f32[8,8,1024]{2,1,0:T(8,128)S(1)}, u32[]{:S(2)}, u32[]{:S(2)}) async-start(f32[8,8,1024]{2,1,0:T(8,128)} %fusion.2), calls=%async_computation.3 | async-start | bytes 524288 | tf_op jit(solution)/shard_map/all_to_all | solution.py:11

commit v2 on v1

--- a/solution.py
+++ b/solution.py
@@ -27,6 +27,27 @@
 
 def dot(a, b, ca, cb):
     return lax.dot_general(a, b, (((ca,), (cb,)), ((), ())), preferred_element_type=F32)
+
+
+def scatter_sum(x):
+    size = lax.axis_size("dp")
+    if size > 8 or size % 2:
+        return jnp.sum(exchange(x), 0)
+    me = lax.axis_index("dp")
+    odd = me % 2 == 1
+    even_half, odd_half = x[0::2], x[1::2]
+    other = lax.ppermute(
+        jnp.where(odd, even_half, odd_half), "dp", [(i, i ^ 1) for i in range(size)]
+    )
+    half = jnp.where(odd, odd_half, even_half) + other
+    total = lax.dynamic_index_in_dim(half, me // 2, 0, False)
+    parts = []
+    for k in range(1, size // 2):
+        part = lax.dynamic_index_in_dim(half, (me // 2) ^ k, 0, False)
+        parts.append(lax.ppermute(part, "dp", [(i, i ^ (2 * k)) for i in range(size)]))
+    for part in parts:
+        total = total + part
+    return total
 
 
 def body(queries, passages, bank, ids, counts):
@@ -94,20 +115,21 @@
     weights = jnp.exp(scores - log_total).astype(BF)
     coeffs = jnp.where(asked, jnp.exp(pos_or - log_total) - inv_count, 0.0)
     coeff = jnp.sum(coeffs, 1).reshape(peers, 1, cap)
+    mine = (jnp.arange(peers) == lax.axis_index("dp"))[None, :, None]
+    coeff = jnp.where(mine, coeff, 0.0).reshape(peers, 1, places)
 
     pas_part = dot(weights, queries, 1, 0).reshape(peers, pad, width)
     sent = jnp.where(
         jnp.arange(pad)[None, :, None] == pas,
-        jnp.pad(coeff, ((0, 0), (0, 0), (0, width - cap))),
+        jnp.pad(coeff, ((0, 0), (0, 0), (0, width - places))),
         pas_part,
     )
-    sent, q_got = lax.optimization_barrier((sent, q_got))
-    got = exchange(sent)
+    got = scatter_sum(sent)
 
     hi, lo = split(coeffs)
     query_grad = 50.0 * (dot(weights, all_pas, 0, 0) + dot(hi, fetched, 0, 0) + dot(lo, fetched, 0, 0))
-    passage_grad = 50.0 * jnp.sum(got[:, :pas], 0)
-    back = got[:, pas, :cap].reshape(1, -1)
+    passage_grad = 50.0 * got[:pas]
+    back = got[pas : pas + 1, :places]
     member = jnp.where(
         wanted[None, :] == jnp.arange(bank_rows).astype(F32)[:, None], back, 0.0
     )

time: 73.9 us -> 66.2 us (0.90)
  waiting for transfers between devices: 38.4 us -> 28.1 us
  starting transfers between devices: 19.6 us -> 22.8 us
    all_to_all x4 -> x3, waiting for transfers between devices: 37.2 us -> 17.6 us  [exchange(): return lax.all_to_all(x, 'dp', split_axis=0, concat_axis=0, tiled=True)]
    ppermute x0 -> x4, waiting for transfers between devices: none -> 9.29 us  [the longest x1 5.49 us: scatter_sum(): lax.ppermute(jnp.where(odd, even_half, odd_half), 'dp', [(i, i ^ 1) for i...]
    ppermute x0 -> x4, starting transfers between devices: none -> 6.74 us  [the longest x3 4.66 us: scatter_sum(): lax.ppermute(part, 'dp', [(i, i ^ 2 * k) for i in range(size)])]
    all_to_all x4 -> x3, starting transfers between devices: 18.1 us -> 14.4 us  [exchange(): return lax.all_to_all(x, 'dp', split_axis=0, concat_axis=0, tiled=True)]
  transfers between devices with their start and end apart: 6 -> 9, of which waited for: 5 -> 6; matrix products, arithmetic and copies ran while one was open for 8% -> 9% of each run, Pallas kernels for 0% -> 0%
where the time goes in v2:
time: 66.2 us; the launch traced here: 65.7 us
  waiting for transfers between devices  28.1 us (42%)
  starting transfers between devices  22.8 us (34%)
  matrix products  6.72 us (10%)
  local copies, waits for them, and re-layouts  3.84 us (6%)
  other arithmetic  3.42 us (5%)
  between operations  0.87 us (1%)
    all_to_all x3, waiting for transfers between devices, exchange(): return lax.all_to_all(x, 'dp', split_axis=0, concat_axis=0, tiled=True)  17.6 us
    all_to_all x3, starting transfers between devices, exchange(): return lax.all_to_all(x, 'dp', split_axis=0, concat_axis=0, tiled=True)  14.4 us
    dot_general x11, matrix products, dot(): lax.dot_general(a, b, (((ca,), (cb,)), ((), ())), preferred_element_type=...  6.72 us
    ppermute x1, waiting for transfers between devices, scatter_sum(): lax.ppermute(jnp.where(odd, even_half, odd_half), 'dp', [(i, i ^ 1) for i...  5.49 us
    ppermute x3, starting transfers between devices, scatter_sum(): lax.ppermute(part, 'dp', [(i, i ^ 2 * k) for i in range(size)])  4.66 us
    ppermute x3, waiting for transfers between devices, scatter_sum(): lax.ppermute(part, 'dp', [(i, i ^ 2 * k) for i in range(size)])  3.8 us
    ppermute x1, starting transfers between devices, scatter_sum(): lax.ppermute(jnp.where(odd, even_half, odd_half), 'dp', [(i, i ^ 1) for i...  2.08 us
    unnamed x8, local copies, waits for them, and re-layouts  1.64 us
  transfers between devices with their start and end apart: 9, of which 6 were waited for; matrix products, arithmetic and copies ran while one was open for 9% of the time, Pallas kernels for 0%

profile of v2, /device:TPU:0, one launch (start us, length us, event | category | flops | bytes accessed | tf_op | source)
XLA Modules:
  0.0 65.7 jit_solution(6200932983593210401)
XLA Ops:
  0.7 0.7 %slice_bitcast_fusion.1 = s32[128]{0:T(128)S(1)} fusion(s32[128,16]{0,1:T(8,128)} %param.8), kind=kLoop, calls=%fused_computation.115 | loop fusion | bytes 1024 | tf_op jit(solution)/shard_map/concatenate | solution.py:67
  1.4 0.8 %reshape.481 = s32[8,16,16]{1,0,2:T(8,128)S(1)} reshape(s32[128,16]{0,1:T(8,128)} %param.8) | data formatting | bytes 16384 | tf_op jit(solution)/shard_map/reshape | solution.py:65
  2.2 0.3 reduce_max.36
  3.1 0.3 copy-done.2
  3.4 0.7 %fusion.16 = bf16[8,8,1024]{2,1,0:T(8,128)(2,1)} fusion(bf16[8,1,32]{2,1,0:T(2,128)(2,1)S(1)} %convert_element_type.103, bf16[8,6,1024]{2,1,0:T(8,128)(2,1)S(1)} %broadcast_in_dim.154), kind=kLoop, calls=%fused_computation.35 | loop fusion | flops 393216 | bytes 229888 | tf_op jit(solution)/shard_map/concatenate | solution.py:93
  4.1 7.3 %all-to-all-start = ((bf16[8,8,1024]{2,1,0:T(8,128)(2,1)}), bf16[8,8,1024]{2,1,0:T(8,128)(2,1)S(1)}, u32[]{:S(2)}, u32[]{:S(2)}) async-start(bf16[8,8,1024]{2,1,0:T(8,128)(2,1)} %fusion.16), calls=%async_computation | async-start | bytes 262144 | tf_op jit(solution)/shard_map/all_to_all | solution.py:11
  11.4 0.6 copy-done.3
  12.2 6.6 %all-to-all-done = bf16[8,8,1024]{2,1,0:T(8,128)(2,1)S(1)} async-done(((bf16[8,8,1024]{2,1,0:T(8,128)(2,1)}), bf16[8,8,1024]{2,1,0:T(8,128)(2,1)S(1)}, u32[]{:S(2)}, u32[]{:S(2)}) %all-to-all-start) | async-done | bytes 131104 | tf_op jit(solution)/shard_map/all_to_all | solution.py:11
  18.8 1.1 %convolution_convert_fusion = bf16[256,1024]{1,0:T(8,128)(2,1)} fusion(bf16[256,1024]{1,0:T(8,128)(2,1)S(1)} %copy-done, f32[256]{0:T(256)S(1)} %iota_convert_fusion, f32[256]{0:T(256)S(1)} %reshape.489), kind=kOutput, calls=%fused_computation.2 | convolution fusion | flops 134545408 | bytes 1050624 | tf_op jit(solution)/shard_map/dot_general | solution.py:29
  20.0 3.5 %all-to-all-start.1 = ((bf16[8,32,1024]{2,1,0:T(8,128)(2,1)}), bf16[8,32,1024]{2,1,0:T(8,128)(2,1)S(1)}, u32[]{:S(2)}, u32[]{:S(2)}) async-start(bf16[8,32,1024]{2,1,0:T(8,128)(2,1)} %bitcast.2), calls=%async_computation.1 | async-start | bytes 1048576 | tf_op jit(solution)/shard_map/all_to_all | solution.py:11
  23.7 0.7 %copy-done.1 = bf16[128,1024]{1,0:T(8,128)(2,1)S(1)} copy-done((bf16[128,1024]{1,0:T(8,128)(2,1)S(1)}, bf16[128,1024]{1,0:T(8,128)(2,1)}, u32[]{:S(2)}) %copy-start.1) | copy-done | bytes 262168
  24.4 1.1 %convolution_convert_fusion.1 = bf16[256,1024]{1,0:T(8,128)(2,1)} fusion(bf16[128,1024]{1,0:T(8,128)(2,1)S(1)} %copy-done.1, bf16[256,128]{1,0:T(8,128)(2,1)S(1)} %get-tuple-element.16), kind=kOutput, calls=%fused_computation.3 | convolution fusion | flops 67371008 | bytes 851968 | tf_op jit(solution)/shard_map/dot_general | solution.py:29
  25.7 11.0 %all-to-all-done.1 = bf16[8,32,1024]{2,1,0:T(8,128)(2,1)S(1)} async-done(((bf16[8,32,1024]{2,1,0:T(8,128)(2,1)}), bf16[8,32,1024]{2,1,0:T(8,128)(2,1)S(1)}, u32[]{:S(2)}, u32[]{:S(2)}) %all-to-all-start.1) | async-done | bytes 524320 | tf_op jit(solution)/shard_map/all_to_all | solution.py:11
  36.7 0.4 fusion.3
  37.2 1.2 %collective-permute-done = f32[66,128]{1,0:T(8,128)S(1)} collective-permute-done((f32[66,128]{1,0:T(8,128)S(1)}, f32[66,128]{1,0:T(8,128)S(1)}, u32[]{:S(2)}, u32[]{:S(2)}) %collective-permute-start) | collective-permute-done | bytes 33824 | tf_op jit(solution)/shard_map/ppermute | solution.py:18
  38.4 1.5 %collective-permute-start.1 = (f32[66,128]{1,0:T(8,128)S(1)}, f32[66,128]{1,0:T(8,128)S(1)}, u32[]{:S(2)}, u32[]{:S(2)}) collective-permute-start(f32[66,128]{1,0:T(8,128)S(1)} %fusion.62), channel_id=1, source_target_pairs={{0,2},{1,3},{2,0},{3,1},{4,6},{5,7},{6,4},{7,5},{8,10},{9,11},{10,... | collective-permute-start | bytes 101384 | tf_op jit(solution)/shard_map/ppermute | solution.py:18
  40.1 3.7 %all-to-all-start.2 = ((bf16[8,32,1024]{2,1,0:T(8,128)(2,1)}), bf16[8,32,1024]{2,1,0:T(8,128)(2,1)S(1)}, u32[]{:S(2)}, u32[]{:S(2)}) async-start(bf16[8,32,1024]{2,1,0:T(8,128)(2,1)} %bitcast.13), calls=%async_computation.2 | async-start | bytes 1048576 | tf_op jit(solution)/shard_map/all_to_all | solution.py:11
  44.5 0.3 fusion.37
  45.0 0.2 fusion.2
  45.3 2.1 %collective-permute-start.2 = (f32[4,8,1024]{2,1,0:T(8,128)S(1)}, f32[4,8,1024]{2,1,0:T(8,128)S(1)}, u32[]{:S(2)}, u32[]{:S(2)}) collective-permute-start(f32[4,8,1024]{2,1,0:T(8,128)S(1)} %slice_select_fusion), channel_id=1, source_target_pairs={{0,4},{4,0},{8,12},{12,8},{16,20},{20,16},{24,28},{28,24},{1,5},{5... | collective-permute-start | bytes 393224 | tf_op jit(solution)/shard_map/ppermute | solution.py:39
  47.4 0.3 convolution_add_fusion.1
  47.7 1.2 %fusion.1 = f32[128,1024]{1,0:T(8,128)} fusion(f32[128,1024]{1,0:T(8,128)S(1)} %convolution_add_fusion.1, bf16[256,1024]{1,0:T(8,128)(2,1)S(1)} %bitcast.48, pred[256,128]{1,0:T(32,128)(4,1)S(1)} %get-tuple-element.15, f32[128]{0:T(128)S(1)} %convert_divide_fusion, f32[128]{0:T(128)S(1)} %log_add_fusion, f32[256]{0:T(256)S(1)} %slice_bitcast_fusion), kind=kOutput, calls=%fused_computation.6 | convolution fusion | flops 67600384 | bytes 1607680 | tf_op jit(solution)/shard_map/dot_general | solution.py:29
  48.8 5.5 %collective-permute-done.2 = f32[4,8,1024]{2,1,0:T(8,128)S(1)} collective-permute-done((f32[4,8,1024]{2,1,0:T(8,128)S(1)}, f32[4,8,1024]{2,1,0:T(8,128)S(1)}, u32[]{:S(2)}, u32[]{:S(2)}) %collective-permute-start.2) | collective-permute-done | bytes 131104 | tf_op jit(solution)/shard_map/ppermute | solution.py:39
  54.4 1.8 %collective-permute-start.3 = (f32[8,1024]{1,0:T(8,128)S(1)}, f32[8,1024]{1,0:T(8,128)S(1)}, u32[]{:S(2)}, u32[]{:S(2)}) collective-permute-start(f32[8,1024]{1,0:T(8,128)S(1)} %get-tuple-element.10), channel_id=1, source_target_pairs={{0,8},{4,12},{8,0},{12,4},{16,24},{20,28},{24,16},{28,20},{1,9},{5... | collective-permute-start | bytes 98312 | tf_op jit(solution)/shard_map/ppermute | solution.py:47
  56.1 2.4 %collective-permute-start.5 = (f32[8,1024]{1,0:T(8,128)S(1)}, f32[8,1024]{1,0:T(8,128)S(1)}, u32[]{:S(2)}, u32[]{:S(2)}) collective-permute-start(f32[8,1024]{1,0:T(8,128)S(1)} %get-tuple-element.11), channel_id=1, source_target_pairs={{0,24},{4,28},{8,16},{12,20},{16,8},{20,12},{24,0},{28,4},{1,25},{... | collective-permute-start | bytes 98312 | tf_op jit(solution)/shard_map/ppermute | solution.py:47
  58.6 0.5 collective-permute-start.4
  59.0 0.5 multiply_subtract_fusion
  59.6 2.6 %collective-permute-done.5 = f32[8,1024]{1,0:T(8,128)S(1)} collective-permute-done((f32[8,1024]{1,0:T(8,128)S(1)}, f32[8,1024]{1,0:T(8,128)S(1)}, u32[]{:S(2)}, u32[]{:S(2)}) %collective-permute-start.5) | collective-permute-done | bytes 32800 | tf_op jit(solution)/shard_map/ppermute | solution.py:47
  62.1 1.2 %collective-permute-done.4 = f32[8,1024]{1,0:T(8,128)S(1)} collective-permute-done((f32[8,1024]{1,0:T(8,128)S(1)}, f32[8,1024]{1,0:T(8,128)S(1)}, u32[]{:S(2)}, u32[]{:S(2)}) %collective-permute-start.4) | collective-permute-done | bytes 32800 | tf_op jit(solution)/shard_map/ppermute | solution.py:47
  63.4 0.6 slice_multiply_fusion
  64.0 0.3 fusion.18
  64.4 1.3 %fusion = f32[256,1024]{1,0:T(8,128)} fusion(f32[256,1024]{1,0:T(8,128)S(1)} %fusion.18, bf16[256,1024]{1,0:T(8,128)(2,1)S(1)} %bitcast.50, f32[256]{0:T(256)S(1)} %bitcast.54, f32[256]{0:T(256)S(1)} %reshape.489, f32[256]{0:T(256)S(1)} %iota_convert_fusion), kind=kOutput, calls=%fused_computation.1 | convolution fusion | flops 135069696 | bytes 2624512 | tf_op jit(solution)/shard_map/dot_general | solution.py:29
  (55 shorter events, 2.4 us)
Async XLA Ops:
  0.6 18.2 %copy-start = (bf16[256,1024]{1,0:T(8,128)(2,1)S(1)}, bf16[256,1024]{1,0:T(8,128)(2,1)}, u32[]{:S(2)}) copy-start(bf16[256,1024]{1,0:T(8,128)(2,1)} %param.7) | copy-start | bytes 1572868
  2.7 0.7 %copy-start.2 = (bf16[6,1024]{1,0:T(8,128)(2,1)S(1)}, bf16[6,1024]{1,0:T(8,128)(2,1)}, u32[]{:S(2)}) copy-start(bf16[6,1024]{1,0:T(8,128)(2,1)} %param.6) | copy-start | bytes 36868
  4.1 14.6 %all-to-all-start = ((bf16[8,8,1024]{2,1,0:T(8,128)(2,1)}), bf16[8,8,1024]{2,1,0:T(8,128)(2,1)S(1)}, u32[]{:S(2)}, u32[]{:S(2)}) async-start(bf16[8,8,1024]{2,1,0:T(8,128)(2,1)} %fusion.16), calls=%async_computation | async-start | bytes 262144 | tf_op jit(solution)/shard_map/all_to_all | solution.py:11
  11.4 0.7 %copy-start.3 = (s32[128]{0:T(128)S(1)}, s32[128]{0:T(128)}, u32[]{:S(2)}) copy-start(s32[128]{0:T(128)} %param.9) | copy-start | bytes 1540
  20.0 16.8 %all-to-all-start.1 = ((bf16[8,32,1024]{2,1,0:T(8,128)(2,1)}), bf16[8,32,1024]{2,1,0:T(8,128)(2,1)S(1)}, u32[]{:S(2)}, u32[]{:S(2)}) async-start(bf16[8,32,1024]{2,1,0:T(8,128)(2,1)} %bitcast.2), calls=%async_computation.1 | async-start | bytes 1048576 | tf_op jit(solution)/shard_map/all_to_all | solution.py:11
  23.5 1.0 %copy-start.1 = (bf16[128,1024]{1,0:T(8,128)(2,1)S(1)}, bf16[128,1024]{1,0:T(8,128)(2,1)}, u32[]{:S(2)}) copy-start(bf16[128,1024]{1,0:T(8,128)(2,1)} %param.5) | copy-start | bytes 786436
  37.1 1.3 %collective-permute-start = (f32[66,128]{1,0:T(8,128)S(1)}, f32[66,128]{1,0:T(8,128)S(1)}, u32[]{:S(2)}, u32[]{:S(2)}) collective-permute-start(f32[66,128]{1,0:T(8,128)S(1)} %pad_maximum_fusion), channel_id=1, source_target_pairs={{0,1},{1,0},{2,3},{3,2},{4,5},{5,4},{6,7},{7,6},{8,9},{9,8},{10,11... | collective-permute-start | bytes 101384 | tf_op jit(solution)/shard_map/ppermute | solution.py:18
  38.4 5.4 %collective-permute-start.1 = (f32[66,128]{1,0:T(8,128)S(1)}, f32[66,128]{1,0:T(8,128)S(1)}, u32[]{:S(2)}, u32[]{:S(2)}) collective-permute-start(f32[66,128]{1,0:T(8,128)S(1)} %fusion.62), channel_id=1, source_target_pairs={{0,2},{1,3},{2,0},{3,1},{4,6},{5,7},{6,4},{7,5},{8,10},{9,11},{10,... | collective-permute-start | bytes 101384 | tf_op jit(solution)/shard_map/ppermute | solution.py:18
  40.1 23.9 %all-to-all-start.2 = ((bf16[8,32,1024]{2,1,0:T(8,128)(2,1)}), bf16[8,32,1024]{2,1,0:T(8,128)(2,1)S(1)}, u32[]{:S(2)}, u32[]{:S(2)}) async-start(bf16[8,32,1024]{2,1,0:T(8,128)(2,1)} %bitcast.13), calls=%async_computation.2 | async-start | bytes 1048576 | tf_op jit(solution)/shard_map/all_to_all | solution.py:11
  45.3 9.1 %collective-permute-start.2 = (f32[4,8,1024]{2,1,0:T(8,128)S(1)}, f32[4,8,1024]{2,1,0:T(8,128)S(1)}, u32[]{:S(2)}, u32[]{:S(2)}) collective-permute-start(f32[4,8,1024]{2,1,0:T(8,128)S(1)} %slice_select_fusion), channel_id=1, source_target_pairs={{0,4},{4,0},{8,12},{12,8},{16,20},{20,16},{24,28},{28,24},{1,5},{5... | collective-permute-start | bytes 393224 | tf_op jit(solution)/shard_map/ppermute | solution.py:39
  54.4 5.2 %collective-permute-start.3 = (f32[8,1024]{1,0:T(8,128)S(1)}, f32[8,1024]{1,0:T(8,128)S(1)}, u32[]{:S(2)}, u32[]{:S(2)}) collective-permute-start(f32[8,1024]{1,0:T(8,128)S(1)} %get-tuple-element.10), channel_id=1, source_target_pairs={{0,8},{4,12},{8,0},{12,4},{16,24},{20,28},{24,16},{28,20},{1,9},{5... | collective-permute-start | bytes 98312 | tf_op jit(solution)/shard_map/ppermute | solution.py:47
  56.1 6.0 %collective-permute-start.5 = (f32[8,1024]{1,0:T(8,128)S(1)}, f32[8,1024]{1,0:T(8,128)S(1)}, u32[]{:S(2)}, u32[]{:S(2)}) collective-permute-start(f32[8,1024]{1,0:T(8,128)S(1)} %get-tuple-element.11), channel_id=1, source_target_pairs={{0,24},{4,28},{8,16},{12,20},{16,8},{20,12},{24,0},{28,4},{1,25},{... | collective-permute-start | bytes 98312 | tf_op jit(solution)/shard_map/ppermute | solution.py:47
  58.6 4.8 %collective-permute-start.4 = (f32[8,1024]{1,0:T(8,128)S(1)}, f32[8,1024]{1,0:T(8,128)S(1)}, u32[]{:S(2)}, u32[]{:S(2)}) collective-permute-start(f32[8,1024]{1,0:T(8,128)S(1)} %get-tuple-element.12), channel_id=1, source_target_pairs={{0,16},{4,20},{8,24},{12,28},{16,0},{20,4},{24,8},{28,12},{1,17},{... | collective-permute-start | bytes 98312 | tf_op jit(solution)/shard_map/ppermute | solution.py:47

commit v3 on v2

v3 whole, which is shorter than its diff:
```python
import jax
import jax.numpy as jnp
from jax import lax
from jax.sharding import PartitionSpec as P


BF = jnp.bfloat16
F32 = jnp.float32


def exchange(x, groups=None):
    return lax.all_to_all(
        x, "dp", split_axis=0, concat_axis=0, tiled=True, axis_index_groups=groups
    )


def split(x):
    hi = lax.reduce_precision(x, 8, 7)
    return hi.astype(BF), (x - hi).astype(BF)


def dot(a, b, ca, cb):
    return lax.dot_general(a, b, (((ca,), (cb,)), ((), ())), preferred_element_type=F32)


def to_pair(x):
    return lax.ppermute(x, "dp", [(i, i ^ 1) for i in range(lax.axis_size("dp"))])


def sub_sums(x):
    size, peers = lax.axis_size("sub"), lax.axis_size("dp")
    step = 1
    while 2 * step < size:
        x = x + lax.ppermute(x, "sub", [(i, i ^ step) for i in range(size)])
        step *= 2
    mine = x + lax.ppermute(x, "sub", [(i, i ^ step) for i in range(size)])
    cross = [
        (d * size + s, (d ^ 1) * size + (s ^ step)) for d in range(peers) for s in range(size)
    ]
    pair = to_pair(x)
    pair = pair + lax.ppermute(x, ("dp", "sub"), cross)
    return mine, pair


def line_groups():
    peers = lax.axis_size("dp")
    return [list(range(odd, peers, 2)) for odd in range(2)]


def scatter_sum(x):
    size = lax.axis_size("dp")
    lines = size // 2
    if lines > 4 or lines & (lines - 1):
        return jnp.sum(exchange(x, line_groups()), 0)
    line = lax.axis_index("dp") // 2
    total = lax.dynamic_index_in_dim(x, line, 0, False)
    parts = []
    for k in range(1, lines):
        part = lax.dynamic_index_in_dim(x, line ^ k, 0, False)
        parts.append(lax.ppermute(part, "dp", [(i, i ^ (2 * k)) for i in range(size)]))
    for part in parts:
        total = total + part
    return total


def owns_of(counts, max_pos):
    q_rows = counts.shape[0]
    q_at = jnp.arange(q_rows)
    return jnp.concatenate(
        [
            q_at[:, None] == q_at[None, :],
            (jnp.arange(q_rows // 16 * max_pos)[:, None] // max_pos == q_at[None, :] // 16)
            & (counts[None, :] > 1),
        ]
    )


def body(queries, passages, bank, ids, counts):
    peers = lax.axis_size("dp")
    lines = peers // 2
    me = lax.axis_index("dp")
    odd = me % 2 == 1
    q_rows, width = queries.shape
    bank_rows = bank.shape[0]
    cap = bank_rows // 8
    places = peers * cap
    pas = passages.shape[0]
    pad = -(-(pas + 1) // 8) * 8
    blocks = q_rows // 16
    max_pos = ids.shape[1]
    near = lambda x: jnp.where(odd, x[:, 1], x[:, 0])

    first = ids[:, 0]
    rest = jnp.max(ids.reshape(blocks, 16, max_pos), 1)
    rest = jnp.where(jnp.arange(max_pos)[None, :] > 0, rest, -1).reshape(-1)
    sid = jnp.concatenate([first, rest])
    slots = sid.shape[0]
    valid = sid >= 0
    owner = jnp.where(valid, sid // bank_rows, -1)
    at = jnp.arange(slots)
    rank = jnp.sum(
        ((owner[:, None] == owner[None, :]) & (at[:, None] < at[None, :])).astype(F32), 0
    ).astype(jnp.int32)
    place = jnp.where(valid, owner * cap + rank, places)
    perm = jnp.arange(places)[:, None] == place[None, :]
    send_ids = jnp.max(jnp.where(perm, (sid % bank_rows)[None, :], -1), 1)

    head = jnp.broadcast_to(passages[None], (peers, pas, width))
    id_row = jnp.pad(
        send_ids.reshape(peers, 1, cap).astype(BF), ((0, 0), (0, pad - pas - 1), (0, width - cap))
    )
    heads = exchange(jnp.concatenate([head, id_row], 1))

    notes = jnp.concatenate([place.astype(BF), counts.astype(BF)])
    notes = jnp.pad(notes[None], ((0, 7), (0, width - notes.shape[0])))
    pair_in = to_pair(jnp.concatenate([queries, notes]))
    pair_q = pair_in[:q_rows]
    pair_place = pair_in[q_rows, :slots].astype(jnp.int32)
    pair_counts = pair_in[q_rows, slots : slots + q_rows].astype(jnp.int32)
    pair_perm = jnp.arange(places)[:, None] == pair_place[None, :]
    asks = dot(perm.astype(BF), owns_of(counts, max_pos).astype(BF), 1, 0)
    pair_asks = dot(pair_perm.astype(BF), owns_of(pair_counts, max_pos).astype(BF), 1, 0)
    asks = jnp.stack([asks, pair_asks])
    asked = asks > 0.5
    both_counts = jnp.stack([counts, pair_counts]).astype(F32)[:, None, :]

    all_pas = heads.reshape(peers * pad, width)
    wanted = heads[:, pas, :cap].astype(F32).reshape(-1)
    pick = (wanted[:, None] == jnp.arange(bank_rows).astype(F32)[None, :]).astype(BF)
    picked = dot(pick, bank, 1, 0).astype(BF)
    fetched = exchange(picked.reshape(peers, cap, width)).reshape(places, width)

    send = []
    for k, rows in enumerate((queries, pair_q)):
        ask = near(asks[k].astype(BF).reshape(lines, 2, cap, q_rows)).reshape(-1, q_rows)
        send.append(dot(ask, rows, 1, 0).astype(BF).reshape(lines, 1, cap, width))
    even_send = jnp.where(odd, send[1], send[0])
    odd_send = jnp.where(odd, send[0], send[1])
    q_send = jnp.concatenate([even_send, odd_send], 1).reshape(lines, 2 * cap, width)
    q_send, fetched = lax.optimization_barrier((q_send, fetched))
    q_got = exchange(q_send, line_groups())
    q_got = q_got.reshape(places, width)

    part = dot(all_pas, queries, 1, 1)
    pos_part = jnp.sum(jnp.where(asked[0], dot(fetched, queries, 1, 1), 0.0), 1)
    mine, pair = sub_sums(jnp.concatenate([part, pos_part.reshape(-1, q_rows)]))
    sums = jnp.stack([mine, pair]) * 50.0
    real = (jnp.arange(peers * pad) % pad < pas)[None, :, None]
    scores = jnp.where(real, sums[:, : peers * pad], -jnp.inf)
    pos = sums[:, peers * pad :].reshape(2, places, 1)
    pos_or = jnp.where(asked, pos, -jnp.inf)
    row_max = jnp.maximum(jnp.max(scores, 1, keepdims=True), jnp.max(pos_or, 1, keepdims=True))
    total = jnp.sum(jnp.exp(scores - row_max), 1, keepdims=True)
    total = total + jnp.sum(jnp.exp(pos_or - row_max), 1, keepdims=True)
    log_total = row_max + jnp.log(total)
    inv_count = 1.0 / both_counts
    losses = log_total[0, 0] - jnp.sum(jnp.where(asked[0], pos[0], 0.0), 0) * inv_count[0, 0]
    weights = jnp.exp(scores - log_total).astype(BF)
    coeffs = jnp.where(asked, jnp.exp(pos_or - log_total) - inv_count, 0.0)

    pas_part = jnp.zeros((lines * pad, width), F32)
    rows = jnp.zeros((lines, peers, cap), F32)
    for k, q in enumerate((queries, pair_q)):
        near_w = near(weights[k].reshape(lines, 2, pad, q_rows)).reshape(lines * pad, q_rows)
        pas_part = pas_part + dot(near_w, q, 1, 0)
        coeff = near(jnp.sum(coeffs[k], 1).reshape(lines, 2, cap))
        source = (jnp.arange(peers) == me ^ k)[None, :, None]
        rows = jnp.where(source, coeff[:, None, :], rows)
    sent = jnp.where(
        jnp.arange(pad)[None, :, None] == pas,
        jnp.pad(rows.reshape(lines, 1, places), ((0, 0), (0, 0), (0, width - places))),
        pas_part.reshape(lines, pad, width),
    )
    got = scatter_sum(sent)

    hi, lo = split(coeffs[0])
    query_grad = 50.0 * (
        dot(weights[0], all_pas, 0, 0) + dot(hi, fetched, 0, 0) + dot(lo, fetched, 0, 0)
    )
    passage_grad = 50.0 * got[:pas]
    back = got[pas : pas + 1, :places]
    member = jnp.where(
        wanted[None, :] == jnp.arange(bank_rows).astype(F32)[:, None], back, 0.0
    )
    hi, lo = split(member)
    bank_grad = 50.0 * (dot(hi, q_got, 1, 0) + dot(lo, q_got, 1, 0))
    return (losses, query_grad, passage_grad, bank_grad)


def solution(mesh):
    placed = (P("dp", "sub"), P("dp", "sub"), P("dp", "sub"), P("dp", None), P("dp"))
    return jax.shard_map(
        body,
        mesh=mesh,
        in_specs=placed,
        out_specs=(P("dp"), P("dp", "sub"), P("dp", "sub"), P("dp", "sub")),
        check_vma=False,
    )
```

time: 66.2 us -> 65.8 us (level)
  other arithmetic: 3.42 us -> 5.69 us
  waiting for transfers between devices: 28.1 us -> 26.8 us
  local copies, waits for them, and re-layouts: 3.84 us -> 2.58 us
    ppermute x3 -> x5, starting transfers between devices: 3.67 us -> 6.66 us  [the longest x2 4.57 us: to_pair(): lax.ppermute(x, 'dp', [(i, i ^ 1) for i in range(lax.axis_size('dp'))])]
    all_to_all x3, starting transfers between devices: 14.4 us -> 12 us  [exchange(): lax.all_to_all(x, 'dp', split_axis=0, concat_axis=0, tiled=True, axis_ind...]
    concatenate x1 -> x4, other arithmetic: 0.01 us -> 1.83 us  [the longest x1 0.98 us: body(): pair_in = to_pair(jnp.concatenate([queries, notes]))]
    unnamed x8 -> x10, local copies, waits for them, and re-layouts: 1.64 us -> 0.03 us
    ppermute x3 -> x5, waiting for transfers between devices: 6.67 us -> 5.54 us  [the longest x2 2.33 us: to_pair(): lax.ppermute(x, 'dp', [(i, i ^ 1) for i in range(lax.axis_size('dp'))])]
    dot_general x11 -> x14, matrix products: 6.72 us -> 6.06 us  [dot(): lax.dot_general(a, b, (((ca,), (cb,)), ((), ())), preferred_element_type=...]
  transfers between devices with their start and end apart: 9 -> 11, of which waited for: 6 -> 7; matrix products, arithmetic and copies ran while one was open for 9% -> 14% of each run, Pallas kernels for 0% -> 0%
where the time goes in v3:
time: 65.8 us; the launch traced here: 65.3 us
  waiting for transfers between devices  26.8 us (41%)
  starting transfers between devices  23.1 us (35%)
  matrix products  6.06 us (9%)
  other arithmetic  5.69 us (9%)
  local copies, waits for them, and re-layouts  2.58 us (4%)
  between operations  1.09 us (2%)
    all_to_all x3, waiting for transfers between devices, exchange(): lax.all_to_all(x, 'dp', split_axis=0, concat_axis=0, tiled=True, axis_ind...  17.7 us
    all_to_all x3, starting transfers between devices, exchange(): lax.all_to_all(x, 'dp', split_axis=0, concat_axis=0, tiled=True, axis_ind...  12 us
    dot_general x14, matrix products, dot(): lax.dot_general(a, b, (((ca,), (cb,)), ((), ())), preferred_element_type=...  6.06 us
    ppermute x2, starting transfers between devices, to_pair(): lax.ppermute(x, 'dp', [(i, i ^ 1) for i in range(lax.axis_size('dp'))])  4.57 us
    ppermute x3, starting transfers between devices, scatter_sum(): lax.ppermute(part, 'dp', [(i, i ^ 2 * k) for i in range(size)])  4.45 us
    ppermute x3, waiting for transfers between devices, scatter_sum(): lax.ppermute(part, 'dp', [(i, i ^ 2 * k) for i in range(size)])  3.51 us
    ppermute x2, waiting for transfers between devices, to_pair(): lax.ppermute(x, 'dp', [(i, i ^ 1) for i in range(lax.axis_size('dp'))])  2.33 us
    ppermute x1, waiting for transfers between devices, sub_sums(): pair = pair + lax.ppermute(x, ('dp', 'sub'), cross)  2.02 us
  transfers between devices with their start and end apart: 11, of which 7 were waited for; matrix products, arithmetic and copies ran while one was open for 14% of the time, Pallas kernels for 0%

profile of v3, /device:TPU:0, one launch (start us, length us, event | category | flops | bytes accessed | tf_op | source)
XLA Modules:
  0.0 65.3 jit_solution(14375721054699140583)
XLA Ops:
  0.7 0.8 %reshape.662 = s32[8,16,16]{1,0,2:T(8,128)S(1)} reshape(s32[128,16]{0,1:T(8,128)} %param.8) | data formatting | bytes 16384 | tf_op jit(solution)/shard_map/reshape | solution.py:94
  1.5 0.7 %slice_bitcast_fusion.3 = s32[128]{0:T(128)S(1)} fusion(s32[128,16]{0,1:T(8,128)} %param.8), kind=kLoop, calls=%fused_computation.147 | loop fusion | bytes 1024 | tf_op jit(solution)/shard_map/concatenate | solution.py:96
  2.2 0.3 reduce_max.36
  3.0 1.0 %fusion.6 = bf16[136,1024]{1,0:T(8,128)(2,1)S(1)} fusion(bf16[1,384]{1,0:T(2,128)(2,1)S(1)} %broadcast_in_dim.201, bf16[128,1024]{1,0:T(8,128)(2,1)} %param.5), kind=kLoop, calls=%fused_computation.21 | loop fusion | flops 835584 | bytes 541440 | tf_op jit(solution)/shard_map/concatenate | solution.py:116
  4.0 3.0 %collective-permute-start = (bf16[136,1024]{1,0:T(8,128)(2,1)S(1)}, bf16[136,1024]{1,0:T(8,128)(2,1)S(1)}, u32[]{:S(2)}, u32[]{:S(2)}) collective-permute-start(bf16[136,1024]{1,0:T(8,128)(2,1)S(1)} %fusion.6), channel_id=1, source_target_pairs={{0,4},{4,0},{8,12},{12,8},{16,20},{20,16},{24,28},{28,24},{1,5},{5... | collective-permute-start | bytes 835592 | tf_op jit(solution)/shard_map/ppermute | solution.py:27
  7.2 0.7 %fusion.21 = bf16[8,8,1024]{2,1,0:T(8,128)(2,1)} fusion(bf16[8,1,32]{2,1,0:T(2,128)(2,1)S(1)} %convert_element_type.142, bf16[8,6,1024]{2,1,0:T(8,128)(2,1)S(1)} %broadcast_in_dim.195), kind=kLoop, calls=%fused_computation.49 | loop fusion | flops 393216 | bytes 229888 | tf_op jit(solution)/shard_map/concatenate | solution.py:112
  7.9 4.9 %all-to-all-start = ((bf16[8,8,1024]{2,1,0:T(8,128)(2,1)}), bf16[8,8,1024]{2,1,0:T(8,128)(2,1)S(1)}, u32[]{:S(2)}, u32[]{:S(2)}) async-start(bf16[8,8,1024]{2,1,0:T(8,128)(2,1)} %fusion.21), calls=%async_computation | async-start | bytes 262144 | tf_op jit(solution)/shard_map/all_to_all | solution.py:12
  13.3 6.9 %all-to-all-done = bf16[8,8,1024]{2,1,0:T(8,128)(2,1)S(1)} async-done(((bf16[8,8,1024]{2,1,0:T(8,128)(2,1)}), bf16[8,8,1024]{2,1,0:T(8,128)(2,1)S(1)}, u32[]{:S(2)}, u32[]{:S(2)}) %all-to-all-start) | async-done | bytes 131104 | tf_op jit(solution)/shard_map/all_to_all | solution.py:12
  20.3 1.1 %convolution_convert_fusion = bf16[256,1024]{1,0:T(8,128)(2,1)} fusion(bf16[256,1024]{1,0:T(8,128)(2,1)S(1)} %copy-done, f32[256]{0:T(256)S(1)} %iota_convert_fusion, f32[256]{0:T(256)S(1)} %reshape.675), kind=kOutput, calls=%fused_computation.2 | convolution fusion | flops 134545408 | bytes 1050624 | tf_op jit(solution)/shard_map/dot_general | solution.py:23
  21.4 3.6 %all-to-all-start.1 = ((bf16[8,32,1024]{2,1,0:T(8,128)(2,1)}), bf16[8,32,1024]{2,1,0:T(8,128)(2,1)S(1)}, u32[]{:S(2)}, u32[]{:S(2)}) async-start(bf16[8,32,1024]{2,1,0:T(8,128)(2,1)} %bitcast.16), calls=%async_computation.1 | async-start | bytes 1048576 | tf_op jit(solution)/shard_map/all_to_all | solution.py:12
  26.1 0.2 broadcast_select_fusion.1
  26.3 0.8 %pad_maximum_fusion = bf16[4,2,32,1024]{3,2,1,0:T(8,128)(2,1)} fusion(bf16[4,1,32,1024]{3,2,1,0:T(8,128)(2,1)S(1)} %bitcast.119, bf16[4,1,32,1024]{3,2,1,0:T(8,128)(2,1)S(1)} %bitcast.118), kind=kLoop, calls=%fused_computation.15 | loop fusion | flops 262144 | bytes 1048576 | tf_op jit(solution)/shard_map/concatenate | solution.py:139
  27.1 10.9 %all-to-all-done.1 = bf16[8,32,1024]{2,1,0:T(8,128)(2,1)S(1)} async-done(((bf16[8,32,1024]{2,1,0:T(8,128)(2,1)}), bf16[8,32,1024]{2,1,0:T(8,128)(2,1)S(1)}, u32[]{:S(2)}, u32[]{:S(2)}) %all-to-all-start.1) | async-done | bytes 524320 | tf_op jit(solution)/shard_map/all_to_all | solution.py:12
  38.0 0.4 fusion.4
  38.5 1.2 %collective-permute-done.1 = f32[66,128]{1,0:T(8,128)S(1)} collective-permute-done((f32[66,128]{1,0:T(8,128)S(1)}, f32[66,128]{1,0:T(8,128)S(1)}, u32[]{:S(2)}, u32[]{:S(2)}) %collective-permute-start.1) | collective-permute-done | bytes 33824 | tf_op jit(solution)/shard_map/ppermute | solution.py:34
  39.7 1.5 %collective-permute-start.2 = (f32[66,128]{1,0:T(8,128)S(1)}, f32[66,128]{1,0:T(8,128)S(1)}, u32[]{:S(2)}, u32[]{:S(2)}) collective-permute-start(f32[66,128]{1,0:T(8,128)S(1)} %fusion.69), channel_id=1, source_target_pairs={{0,2},{1,3},{2,0},{3,1},{4,6},{5,7},{6,4},{7,5},{8,10},{9,11},{10,... | collective-permute-start | bytes 101384 | tf_op jit(solution)/shard_map/ppermute | solution.py:36
  41.2 3.5 %all-to-all-start.2 = ((bf16[4,64,1024]{2,1,0:T(8,128)(2,1)}), bf16[4,64,1024]{2,1,0:T(8,128)(2,1)S(1)}, u32[]{:S(2)}, u32[]{:S(2)}) async-start(bf16[4,64,1024]{2,1,0:T(8,128)(2,1)} %bitcast.15), calls=%async_computation.2 | async-start | bytes 1048576 | tf_op jit(solution)/shard_map/all_to_all | solution.py:12
  44.7 1.5 %collective-permute-start.3 = (f32[66,128]{1,0:T(8,128)S(1)}, f32[66,128]{1,0:T(8,128)S(1)}, u32[]{:S(2)}, u32[]{:S(2)}) collective-permute-start(f32[66,128]{1,0:T(8,128)S(1)} %fusion.69), channel_id=1, source_target_pairs={{0,4},{4,0},{8,12},{12,8},{16,20},{20,16},{24,28},{28,24},{1,5},{5... | collective-permute-start | bytes 101384 | tf_op jit(solution)/shard_map/ppermute | solution.py:27
  46.2 0.5 collective-permute-start.4
  46.8 2.3 %collective-permute-done.3 = f32[66,128]{1,0:T(8,128)S(1)} collective-permute-done((f32[66,128]{1,0:T(8,128)S(1)}, f32[66,128]{1,0:T(8,128)S(1)}, u32[]{:S(2)}, u32[]{:S(2)}) %collective-permute-start.3) | collective-permute-done | bytes 33824 | tf_op jit(solution)/shard_map/ppermute | solution.py:27
  49.1 2.0 %collective-permute-done.4 = f32[66,128]{1,0:T(8,128)S(1)} collective-permute-done((f32[66,128]{1,0:T(8,128)S(1)}, f32[66,128]{1,0:T(8,128)S(1)}, u32[]{:S(2)}, u32[]{:S(2)}) %collective-permute-start.4) | collective-permute-done | bytes 33824 | tf_op jit(solution)/shard_map/ppermute | solution.py:41
  51.9 0.3 fusion.42
  52.3 0.2 convolution_add_fusion.1
  52.6 1.1 %fusion.1 = f32[128,1024]{1,0:T(8,128)} fusion(f32[128,1024]{1,0:T(8,128)S(1)} %convolution_add_fusion.1, bf16[256,1024]{1,0:T(8,128)(2,1)S(1)} %bitcast.107, f32[2,256,128]{2,1,0:T(8,128)S(1)} %fusion.12), kind=kOutput, calls=%fused_computation.5 | convolution fusion | flops 67469312 | bytes 1703936 | tf_op jit(solution)/shard_map/dot_general | solution.py:23
  54.4 3.8 %collective-permute-start.7 = (f32[8,1024]{1,0:T(8,128)S(1)}, f32[8,1024]{1,0:T(8,128)S(1)}, u32[]{:S(2)}, u32[]{:S(2)}) collective-permute-start(f32[8,1024]{1,0:T(8,128)S(1)} %get-tuple-element.17), channel_id=1, source_target_pairs={{0,24},{4,28},{8,16},{12,20},{16,8},{20,12},{24,0},{28,4},{1,25},{... | collective-permute-start | bytes 98312 | tf_op jit(solution)/shard_map/ppermute | solution.py:60
  58.2 0.7 %collective-permute-start.5 = (f32[8,1024]{1,0:T(8,128)S(1)}, f32[8,1024]{1,0:T(8,128)S(1)}, u32[]{:S(2)}, u32[]{:S(2)}) collective-permute-start(f32[8,1024]{1,0:T(8,128)S(1)} %get-tuple-element.16), channel_id=1, source_target_pairs={{0,8},{4,12},{8,0},{12,4},{16,24},{20,28},{24,16},{28,20},{1,9},{5... | collective-permute-start | bytes 98312 | tf_op jit(solution)/shard_map/ppermute | solution.py:60
  59.0 0.5 fusion.62
  59.5 0.8 %collective-permute-done.7 = f32[8,1024]{1,0:T(8,128)S(1)} collective-permute-done((f32[8,1024]{1,0:T(8,128)S(1)}, f32[8,1024]{1,0:T(8,128)S(1)}, u32[]{:S(2)}, u32[]{:S(2)}) %collective-permute-start.7) | collective-permute-done | bytes 32800 | tf_op jit(solution)/shard_map/ppermute | solution.py:60
  60.3 2.7 %collective-permute-done.6 = f32[8,1024]{1,0:T(8,128)S(1)} collective-permute-done((f32[8,1024]{1,0:T(8,128)S(1)}, f32[8,1024]{1,0:T(8,128)S(1)}, u32[]{:S(2)}, u32[]{:S(2)}) %collective-permute-start.6) | collective-permute-done | bytes 32800 | tf_op jit(solution)/shard_map/ppermute | solution.py:60
  63.0 0.6 slice_multiply_fusion
  63.6 0.3 fusion.23
  64.0 1.3 %fusion = f32[256,1024]{1,0:T(8,128)} fusion(f32[256,1024]{1,0:T(8,128)S(1)} %fusion.23, bf16[256,1024]{1,0:T(8,128)(2,1)S(1)} %bitcast.109, f32[256]{0:T(256)S(1)} %bitcast.130, f32[256]{0:T(256)S(1)} %reshape.675, f32[256]{0:T(256)S(1)} %iota_convert_fusion), kind=kOutput, calls=%fused_computation.1 | convolution fusion | flops 135069696 | bytes 2624512 | tf_op jit(solution)/shard_map/dot_general | solution.py:23
  (87 shorter events, 3.9 us)
Async XLA Ops:
  0.6 19.6 %copy-start = (bf16[256,1024]{1,0:T(8,128)(2,1)S(1)}, bf16[256,1024]{1,0:T(8,128)(2,1)}, u32[]{:S(2)}) copy-start(bf16[256,1024]{1,0:T(8,128)(2,1)} %param.7) | copy-start | bytes 1572868
  1.5 0.7 %copy-start.3 = (s32[128]{0:T(128)S(1)}, s32[128]{0:T(128)}, u32[]{:S(2)}) copy-start(s32[128]{0:T(128)} %param.9) | copy-start | bytes 1540
  3.0 4.2 %copy-start.2 = (bf16[6,1024]{1,0:T(8,128)(2,1)S(1)}, bf16[6,1024]{1,0:T(8,128)(2,1)}, u32[]{:S(2)}) copy-start(bf16[6,1024]{1,0:T(8,128)(2,1)} %param.6) | copy-start | bytes 36868
  4.0 21.3 %collective-permute-start = (bf16[136,1024]{1,0:T(8,128)(2,1)S(1)}, bf16[136,1024]{1,0:T(8,128)(2,1)S(1)}, u32[]{:S(2)}, u32[]{:S(2)}) collective-permute-start(bf16[136,1024]{1,0:T(8,128)(2,1)S(1)} %fusion.6), channel_id=1, source_target_pairs={{0,4},{4,0},{8,12},{12,8},{16,20},{20,16},{24,28},{28,24},{1,5},{5... | collective-permute-start | bytes 835592 | tf_op jit(solution)/shard_map/ppermute | solution.py:27
  7.9 12.2 %all-to-all-start = ((bf16[8,8,1024]{2,1,0:T(8,128)(2,1)}), bf16[8,8,1024]{2,1,0:T(8,128)(2,1)S(1)}, u32[]{:S(2)}, u32[]{:S(2)}) async-start(bf16[8,8,1024]{2,1,0:T(8,128)(2,1)} %fusion.21), calls=%async_computation | async-start | bytes 262144 | tf_op jit(solution)/shard_map/all_to_all | solution.py:12
  21.4 3.6 %copy-start.1 = (bf16[128,1024]{1,0:T(8,128)(2,1)S(1)}, bf16[128,1024]{1,0:T(8,128)(2,1)}, u32[]{:S(2)}) copy-start(bf16[128,1024]{1,0:T(8,128)(2,1)} %param.5) | copy-start | bytes 786436
  21.4 16.6 %all-to-all-start.1 = ((bf16[8,32,1024]{2,1,0:T(8,128)(2,1)}), bf16[8,32,1024]{2,1,0:T(8,128)(2,1)S(1)}, u32[]{:S(2)}, u32[]{:S(2)}) async-start(bf16[8,32,1024]{2,1,0:T(8,128)(2,1)} %bitcast.16), calls=%async_computation.1 | async-start | bytes 1048576 | tf_op jit(solution)/shard_map/all_to_all | solution.py:12
  38.4 1.3 %collective-permute-start.1 = (f32[66,128]{1,0:T(8,128)S(1)}, f32[66,128]{1,0:T(8,128)S(1)}, u32[]{:S(2)}, u32[]{:S(2)}) collective-permute-start(f32[66,128]{1,0:T(8,128)S(1)} %pad_maximum_fusion.1), channel_id=1, source_target_pairs={{0,1},{1,0},{2,3},{3,2},{4,5},{5,4},{6,7},{7,6},{8,9},{9,8},{10,11... | collective-permute-start | bytes 101384 | tf_op jit(solution)/shard_map/ppermute | solution.py:34
  39.7 7.1 %collective-permute-start.2 = (f32[66,128]{1,0:T(8,128)S(1)}, f32[66,128]{1,0:T(8,128)S(1)}, u32[]{:S(2)}, u32[]{:S(2)}) collective-permute-start(f32[66,128]{1,0:T(8,128)S(1)} %fusion.69), channel_id=1, source_target_pairs={{0,2},{1,3},{2,0},{3,1},{4,6},{5,7},{6,4},{7,5},{8,10},{9,11},{10,... | collective-permute-start | bytes 101384 | tf_op jit(solution)/shard_map/ppermute | solution.py:36
  41.2 22.4 %all-to-all-start.2 = ((bf16[4,64,1024]{2,1,0:T(8,128)(2,1)}), bf16[4,64,1024]{2,1,0:T(8,128)(2,1)S(1)}, u32[]{:S(2)}, u32[]{:S(2)}) async-start(bf16[4,64,1024]{2,1,0:T(8,128)(2,1)} %bitcast.15), calls=%async_computation.2 | async-start | bytes 1048576 | tf_op jit(solution)/shard_map/all_to_all | solution.py:12
  44.7 4.4 %collective-permute-start.3 = (f32[66,128]{1,0:T(8,128)S(1)}, f32[66,128]{1,0:T(8,128)S(1)}, u32[]{:S(2)}, u32[]{:S(2)}) collective-permute-start(f32[66,128]{1,0:T(8,128)S(1)} %fusion.69), channel_id=1, source_target_pairs={{0,4},{4,0},{8,12},{12,8},{16,20},{20,16},{24,28},{28,24},{1,5},{5... | collective-permute-start | bytes 101384 | tf_op jit(solution)/shard_map/ppermute | solution.py:27
  46.2 4.9 %collective-permute-start.4 = (f32[66,128]{1,0:T(8,128)S(1)}, f32[66,128]{1,0:T(8,128)S(1)}, u32[]{:S(2)}, u32[]{:S(2)}) collective-permute-start(f32[66,128]{1,0:T(8,128)S(1)} %fusion.69), channel_id=1, source_target_pairs={{0,6},{1,7},{2,4},{3,5},{4,2},{5,3},{6,0},{7,1},{8,14},{9,15},{10,... | collective-permute-start | bytes 101384 | tf_op jit(solution)/shard_map/ppermute | solution.py:41
  54.4 5.9 %collective-permute-start.7 = (f32[8,1024]{1,0:T(8,128)S(1)}, f32[8,1024]{1,0:T(8,128)S(1)}, u32[]{:S(2)}, u32[]{:S(2)}) collective-permute-start(f32[8,1024]{1,0:T(8,128)S(1)} %get-tuple-element.17), channel_id=1, source_target_pairs={{0,24},{4,28},{8,16},{12,20},{16,8},{20,12},{24,0},{28,4},{1,25},{... | collective-permute-start | bytes 98312 | tf_op jit(solution)/shard_map/ppermute | solution.py:60
  58.2 4.8 %collective-permute-start.6 = (f32[8,1024]{1,0:T(8,128)S(1)}, f32[8,1024]{1,0:T(8,128)S(1)}, u32[]{:S(2)}, u32[]{:S(2)}) collective-permute-start(f32[8,1024]{1,0:T(8,128)S(1)} %get-tuple-element.18), channel_id=1, source_target_pairs={{0,16},{4,20},{8,24},{12,28},{16,0},{20,4},{24,8},{28,12},{1,17},{... | collective-permute-start | bytes 98312 | tf_op jit(solution)/shard_map/ppermute | solution.py:60
  58.2 4.8 %collective-permute-start.5 = (f32[8,1024]{1,0:T(8,128)S(1)}, f32[8,1024]{1,0:T(8,128)S(1)}, u32[]{:S(2)}, u32[]{:S(2)}) collective-permute-start(f32[8,1024]{1,0:T(8,128)S(1)} %get-tuple-element.16), channel_id=1, source_target_pairs={{0,8},{4,12},{8,0},{12,4},{16,24},{20,28},{24,16},{28,20},{1,9},{5... | collective-permute-start | bytes 98312 | tf_op jit(solution)/shard_map/ppermute | solution.py:60

commit v4 on v3

v4 whole, which is shorter than its diff:
```python
import jax
import jax.numpy as jnp
from jax import lax
from jax.experimental import pallas as pl
from jax.experimental.pallas import tpu as pltpu
from jax.sharding import PartitionSpec as P


BF = jnp.bfloat16
F32 = jnp.float32


def exchange(x, groups=None):
    return lax.all_to_all(
        x, "dp", split_axis=0, concat_axis=0, tiled=True, axis_index_groups=groups
    )


def dot(a, b, ca, cb):
    return lax.dot_general(a, b, (((ca,), (cb,)), ((), ())), preferred_element_type=F32)


def to_pair(x):
    return lax.ppermute(x, "dp", [(i, i ^ 1) for i in range(lax.axis_size("dp"))])


def sub_sum(x):
    size = lax.axis_size("sub")
    step = 1
    while step < size:
        x = x + lax.ppermute(x, "sub", [(i, i ^ step) for i in range(size)])
        step *= 2
    return x


def line_groups():
    peers = lax.axis_size("dp")
    return [list(range(odd, peers, 2)) for odd in range(2)]


def scatter_sum(x):
    size = lax.axis_size("dp")
    lines = size // 2
    if lines > 4 or lines & (lines - 1):
        return [jnp.sum(exchange(x, line_groups()), 0)]
    line = lax.axis_index("dp") // 2
    total = lax.dynamic_index_in_dim(x, line, 0, False)
    parts = []
    for k in range(1, lines):
        part = lax.dynamic_index_in_dim(x, line ^ k, 0, False)
        parts.append(lax.ppermute(part, "dp", [(i, i ^ (2 * k)) for i in range(size)]))
    return [total] + parts


def iota(shape, dim):
    return lax.broadcasted_iota(jnp.int32, shape, dim)


def call(kernel, outs, flops, *args, **kw):
    size = sum(a.size * a.dtype.itemsize for a in (*args, *outs))
    cost = pl.CostEstimate(flops=flops, bytes_accessed=size, transcendentals=0)
    return pl.pallas_call(kernel, out_shape=outs, cost_estimate=cost, **kw)(*args)


VMEM = pl.BlockSpec(memory_space=pltpu.VMEM)
ROOMY = pltpu.CompilerParams(vmem_limit_bytes=16 * 2**20)


def plan(ids, passages, peers, bank_rows, pad):
    max_pos, q_rows = ids.shape
    pas, width = passages.shape
    cap = bank_rows // 8
    slots, places = 2 * q_rows, peers * cap

    def kernel(ids_ref, pas_ref, block_ref, place_ref):
        ident = (ids_ref[...] + 1).astype(F32)
        high = jnp.floor(ident / 64)
        parts = jnp.concatenate([high, ident - 64 * high]).astype(BF)
        same = (iota((q_rows, q_rows), 0) // 16 == iota((q_rows, q_rows), 1) // 16).astype(BF)
        group = jnp.dot(parts, same, preferred_element_type=F32)
        group = 64 * group[:max_pos] + group[max_pos:]
        row = iota((max_pos, q_rows), 0)
        here = (row == iota((max_pos, q_rows), 1) % max_pos) & (row > 0)
        rest = jnp.sum(jnp.where(here, group, 0.0), 0, keepdims=True)
        sid = jnp.concatenate([ident[:1], rest], 1)
        owner = jnp.floor((sid - 0.5) / bank_rows)
        local = sid - owner * bank_rows
        down, along = iota((slots, slots), 0), iota((slots, slots), 1)
        owner_col = jnp.sum(jnp.where(down == along, owner, 0.0), 1, keepdims=True)
        before = (owner_col == owner) & (down < along)
        rank = jnp.sum(before.astype(F32), 0, keepdims=True)
        place = jnp.where(sid > 0, owner * cap + rank, float(places))
        place_ref[...] = place
        perm = iota((places, slots), 0).astype(F32) == place
        id_col = jnp.sum(jnp.where(perm, local, 0.0), 1, keepdims=True) - 1
        turn = iota((places, places), 0) == iota((places, places), 1)
        id_row = jnp.sum(jnp.where(turn, id_col, 0.0), 0, keepdims=True)
        top = jnp.concatenate([pas_ref[...].astype(F32), jnp.zeros((pad - pas, width), F32)])
        below = iota((pad, width), 0) == pas
        for d in range(peers):
            tail = jnp.concatenate(
                [id_row[:, d * cap : (d + 1) * cap], jnp.zeros((1, width - cap), F32)], 1
            )
            block_ref[d] = jnp.where(below, tail, top).astype(BF)

    outs = (
        jax.ShapeDtypeStruct((peers, pad, width), BF),
        jax.ShapeDtypeStruct((1, slots), F32),
    )
    block, place = call(
        kernel,
        outs,
        10**7,
        ids,
        passages,
        in_specs=[VMEM, VMEM],
        out_specs=(VMEM, VMEM),
        name="plan",
    )
    return block, place[0].astype(jnp.int32)


def soften(sums, asks, counts, rows, where, pas, base=None):
    places, q_rows = asks.shape
    width = rows.shape[1]
    heads = sums.shape[0] - places // q_rows
    pad = -(-(pas + 1) // 8) * 8
    peers = heads // pad
    lines, cap = peers // 2, places // peers

    def kernel(where_ref, sums_ref, asks_ref, counts_ref, rows_ref, *refs):
        odd, source = where_ref[0] == 1, where_ref[1]
        total = 50.0 * sums_ref[...]
        asked = asks_ref[...] > 0.5
        real = iota((heads, q_rows), 0) % pad < pas
        scores = jnp.where(real, total[:heads], -jnp.inf)
        eye = iota((q_rows, q_rows), 0) == iota((q_rows, q_rows), 1)
        pos = jnp.concatenate(
            [
                jnp.sum(jnp.where(eye, total[j : j + 1], 0.0), 1, keepdims=True)
                for j in range(heads, heads + places // q_rows)
            ]
        )
        pos_or = jnp.where(asked, pos, -jnp.inf)
        top = jnp.maximum(
            jnp.max(scores, 0, keepdims=True), jnp.max(pos_or, 0, keepdims=True)
        )
        mass = jnp.sum(jnp.exp(scores - top), 0, keepdims=True)
        mass = mass + jnp.sum(jnp.exp(pos_or - top), 0, keepdims=True)
        log_total = top + jnp.log(mass)
        inv_count = 1.0 / counts_ref[...]
        weights = jnp.exp(scores - log_total)
        coeffs = jnp.where(asked, jnp.exp(pos_or - log_total) - inv_count, 0.0)
        if base is None:
            losses_ref, weights_ref, hi_ref, lo_ref, sent_ref = refs
            own = jnp.sum(jnp.where(asked, pos, 0.0), 0, keepdims=True)
            losses_ref[...] = log_total - own * inv_count
            weights_ref[...] = weights.astype(BF)
            hi = coeffs.astype(BF)
            hi_ref[...] = hi
            lo_ref[...] = (coeffs - hi.astype(F32)).astype(BF)
        else:
            base_ref, sent_ref = refs
        split_w = weights.reshape(lines, 2, pad, q_rows)
        near_w = jnp.where(odd, split_w[:, 1], split_w[:, 0]).reshape(lines * pad, q_rows)
        part = jnp.dot(near_w.astype(BF), rows_ref[...], preferred_element_type=F32)
        part = part.reshape(lines, pad, width)
        coeff = jnp.sum(coeffs, 1, keepdims=True)
        down, lane = iota((places, places), 0), iota((places, places), 1)
        left = jnp.where(down % cap == lane - source * cap, coeff, 0.0)
        line, at = iota((lines, places), 0), iota((lines, places), 1) // cap
        pick = (at == 2 * line + where_ref[0]).astype(BF)
        row = jnp.zeros((lines, places), F32)
        for _ in range(3):
            piece = left.astype(BF)
            left = left - piece.astype(F32)
            row = row + jnp.dot(pick, piece, preferred_element_type=F32)
        if base is not None:
            part = part + base_ref[...]
            row = row + base_ref[:, pas, :places]
        sent_ref[...] = part
        for i in range(lines):
            sent_ref[i, pas : pas + 1, :places] = row[i : i + 1]

    outs = (jax.ShapeDtypeStruct((lines, pad, width), F32),)
    args = (where, sums, asks, counts, rows)
    if base is None:
        outs = (
            jax.ShapeDtypeStruct((1, q_rows), F32),
            jax.ShapeDtypeStruct((heads, q_rows), BF),
            jax.ShapeDtypeStruct((places, q_rows), BF),
            jax.ShapeDtypeStruct((places, q_rows), BF),
        ) + outs
    else:
        args += (base,)
    return call(
        kernel,
        outs,
        10**7,
        *args,
        in_specs=[pl.BlockSpec(memory_space=pltpu.SMEM)] + [VMEM] * (len(args) - 1),
        out_specs=(VMEM,) * len(outs),
        compiler_params=ROOMY,
        name="soften" if base is None else "soften_pair",
    )


def close(parts, wanted, q_got, pas, bank_rows):
    places, width = q_got.shape
    steps = 4
    cols = width // steps
    n = len(parts)

    def kernel(*refs):
        wanted_ref, q_ref, pas_out, bank_out, pas_vmem, bank_vmem, sems = refs[n:]
        total = sum(r[...] for r in refs[:n])
        pas_vmem[...] = 50.0 * total[:pas]
        copies = [pltpu.make_async_copy(pas_vmem, pas_out, sems.at[steps])]
        copies[0].start()
        back = 50.0 * total[pas : pas + 1, :places]
        row = iota((bank_rows, places), 0).astype(F32)
        member = jnp.where(row == wanted_ref[...], back, 0.0)
        hi = member.astype(BF)
        lo = (member - hi.astype(F32)).astype(BF)
        for i in range(steps):
            at = pl.ds(i * cols, cols)
            q = q_ref[:, at]
            bank_vmem[:, at] = jnp.dot(hi, q, preferred_element_type=F32) + jnp.dot(
                lo, q, preferred_element_type=F32
            )
            copies.append(
                pltpu.make_async_copy(bank_vmem.at[:, at], bank_out.at[:, at], sems.at[i])
            )
            copies[-1].start()
        for copy in copies:
            copy.wait()

    away = pl.BlockSpec(memory_space=pl.ANY)
    return call(
        kernel,
        (
            jax.ShapeDtypeStruct((pas, width), F32),
            jax.ShapeDtypeStruct((bank_rows, width), F32),
        ),
        4 * bank_rows * places * width,
        *parts,
        wanted[None, :],
        q_got,
        in_specs=[VMEM] * (n + 2),
        out_specs=(away, away),
        scratch_shapes=[
            pltpu.VMEM((pas, width), F32),
            pltpu.VMEM((bank_rows, width), F32),
            pltpu.SemaphoreType.DMA((steps + 1,)),
        ],
        compiler_params=ROOMY,
        name="close",
    )


def owns_of(counts, max_pos):
    q_rows = counts.shape[0]
    q_at = jnp.arange(q_rows)
    return jnp.concatenate(
        [
            q_at[:, None] == q_at[None, :],
            (jnp.arange(q_rows // 16 * max_pos)[:, None] // max_pos == q_at[None, :] // 16)
            & (counts[None, :] > 1),
        ]
    )


def body(queries, passages, bank, ids, counts):
    peers = lax.axis_size("dp")
    lines = peers // 2
    me = lax.axis_index("dp")
    odd = me % 2 == 1
    q_rows, width = queries.shape
    bank_rows = bank.shape[0]
    cap = bank_rows // 8
    places = peers * cap
    pas = passages.shape[0]
    pad = -(-(pas + 1) // 8) * 8
    max_pos = ids.shape[1]
    near = lambda x: jnp.where(odd, x[:, 1], x[:, 0])

    block, place = plan(ids.T, passages, peers, bank_rows, pad)
    slots = place.shape[0]
    perm = jnp.arange(places)[:, None] == place[None, :]
    heads = exchange(block)

    notes = jnp.concatenate([place.astype(BF), counts.astype(BF)])
    notes = jnp.pad(notes[None], ((0, 7), (0, width - notes.shape[0])))
    pair_in = to_pair(jnp.concatenate([queries, notes]))
    pair_q = pair_in[:q_rows]
    pair_place = pair_in[q_rows, :slots].astype(jnp.int32)
    pair_counts = pair_in[q_rows, slots : slots + q_rows].astype(jnp.int32)
    pair_perm = jnp.arange(places)[:, None] == pair_place[None, :]
    asks = dot(perm.astype(BF), owns_of(counts, max_pos).astype(BF), 1, 0)
    pair_asks = dot(pair_perm.astype(BF), owns_of(pair_counts, max_pos).astype(BF), 1, 0)
    asks, pair_asks = asks.astype(BF), pair_asks.astype(BF)

    all_pas = heads.reshape(peers * pad, width)
    wanted = heads[:, pas, :cap].astype(F32).reshape(-1)
    pick = (wanted[:, None] == jnp.arange(bank_rows).astype(F32)[None, :]).astype(BF)
    picked = dot(pick, bank, 1, 0).astype(BF)
    fetched = exchange(picked.reshape(peers, cap, width)).reshape(places, width)

    send = []
    for ask, rows in ((asks, queries), (pair_asks, pair_q)):
        ask = near(ask.reshape(lines, 2, cap, q_rows)).reshape(-1, q_rows)
        send.append(dot(ask, rows, 1, 0).astype(BF).reshape(lines, 1, cap, width))
    even_send = jnp.where(odd, send[1], send[0])
    odd_send = jnp.where(odd, send[0], send[1])
    q_send = jnp.concatenate([even_send, odd_send], 1).reshape(lines, 2 * cap, width)
    q_send, fetched = lax.optimization_barrier((q_send, fetched))
    q_got = exchange(q_send, line_groups())
    q_got = q_got.reshape(places, width)

    part = dot(all_pas, queries, 1, 1)
    pos_part = jnp.sum(jnp.where(asks > 0.5, dot(fetched, queries, 1, 1), 0.0), 1)
    mine = sub_sum(jnp.concatenate([part, pos_part.reshape(-1, q_rows)]))
    pair = to_pair(mine)
    spot = lambda source: jnp.stack([me % 2, source]).astype(jnp.int32)
    losses, weights, hi, lo, sent = soften(
        mine, asks, counts.astype(F32)[None], queries, spot(me), pas
    )
    (sent,) = soften(
        pair, pair_asks, pair_counts.astype(F32)[None], pair_q, spot(me ^ 1), pas, sent
    )
    got = scatter_sum(sent)

    query_grad = 50.0 * (
        dot(weights, all_pas, 0, 0) + dot(hi, fetched, 0, 0) + dot(lo, fetched, 0, 0)
    )
    passage_grad, bank_grad = close(got, wanted, q_got, pas, bank_rows)
    return (losses[0], query_grad, passage_grad, bank_grad)


def solution(mesh):
    placed = (P("dp", "sub"), P("dp", "sub"), P("dp", "sub"), P("dp", None), P("dp"))
    return jax.shard_map(
        body,
        mesh=mesh,
        in_specs=placed,
        out_specs=(P("dp"), P("dp", "sub"), P("dp", "sub"), P("dp", "sub")),
        check_vma=False,
    )
```

time: 65.8 us -> 63.9 us (0.971)
  Pallas kernels: 0 us -> 5.62 us
  other arithmetic: 5.69 us -> 2.15 us
  matrix products: 6.06 us -> 4.1 us
  waiting for transfers between devices: 26.8 us -> 25.6 us
    pallas_call x0 -> x4, Pallas kernels: none -> 5.62 us  [call(): pl.pallas_call(kernel, out_shape=outs, cost_estimate=cost, **kw)(*args)]
    ppermute x3, waiting for transfers between devices: 3.51 us -> 6.51 us  [scatter_sum(): lax.ppermute(part, 'dp', [(i, i ^ 2 * k) for i in range(size)])]
    ppermute x3 -> x2, waiting for transfers between devices: 3.21 us -> 1.11 us  [sub_sum(): x = x + lax.ppermute(x, 'sub', [(i, i ^ step) for i in range(size)])]
    dot_general x14 -> x10, matrix products: 6.06 us -> 4.1 us  [dot(): lax.dot_general(a, b, (((ca,), (cb,)), ((), ())), preferred_element_type=...]
    ppermute x2, waiting for transfers between devices: 2.33 us -> 0.65 us  [to_pair(): lax.ppermute(x, 'dp', [(i, i ^ 1) for i in range(lax.axis_size('dp'))])]
    unnamed x10 -> x8, local copies, waits for them, and re-layouts: 0.03 us -> 1.35 us
    reshape x3 -> x0, local copies, waits for them, and re-layouts: 1 us -> none  [the longest x1 0.83 us: body(): rest = jnp.max(ids.reshape(blocks, 16, max_pos), 1)]
    concatenate x1, other arithmetic: 0.84 us -> 0.05 us  [body(): jnp.concatenate([even_send, odd_send], 1).reshape(lines, 2 * cap, width)]
  transfers between devices with their start and end apart: 11 -> 10, of which waited for: 7 -> 5; matrix products, arithmetic and copies ran while one was open for 14% -> 8% of each run, Pallas kernels for 0% -> 4%
where the time goes in v4:
time: 63.9 us; the launch traced here: 63.3 us
  waiting for transfers between devices  25.6 us (40%)
  starting transfers between devices  22.6 us (35%)
  Pallas kernels  5.62 us (9%)
  matrix products  4.1 us (6%)
  local copies, waits for them, and re-layouts  2.4 us (4%)
  other arithmetic  2.15 us (3%)
  between operations  0.86 us (1%)
    all_to_all x3, waiting for transfers between devices, exchange(): lax.all_to_all(x, 'dp', split_axis=0, concat_axis=0, tiled=True, axis_ind...  17.3 us
    all_to_all x3, starting transfers between devices, exchange(): lax.all_to_all(x, 'dp', split_axis=0, concat_axis=0, tiled=True, axis_ind...  12 us
    ppermute x3, waiting for transfers between devices, scatter_sum(): lax.ppermute(part, 'dp', [(i, i ^ 2 * k) for i in range(size)])  6.51 us
    pallas_call x4, Pallas kernels, call(): pl.pallas_call(kernel, out_shape=outs, cost_estimate=cost, **kw)(*args)  5.62 us
    ppermute x2, starting transfers between devices, to_pair(): lax.ppermute(x, 'dp', [(i, i ^ 1) for i in range(lax.axis_size('dp'))])  4.56 us
    ppermute x3, starting transfers between devices, scatter_sum(): lax.ppermute(part, 'dp', [(i, i ^ 2 * k) for i in range(size)])  4.48 us
    dot_general x10, matrix products, dot(): lax.dot_general(a, b, (((ca,), (cb,)), ((), ())), preferred_element_type=...  4.1 us
    ppermute x2, starting transfers between devices, sub_sum(): x = x + lax.ppermute(x, 'sub', [(i, i ^ step) for i in range(size)])  1.59 us
  transfers between devices with their start and end apart: 10, of which 5 were waited for; matrix products, arithmetic and copies ran while one was open for 8% of the time, Pallas kernels for 4%

profile of v4, /device:TPU:0, one launch (start us, length us, event | category | flops | bytes accessed | tf_op | source)
XLA Modules:
  0.0 63.3 jit_solution(17622004673439771045)
XLA Ops:
  0.6 0.7 %convert_bitcast_fusion = (f32[1,128]{1,0:T(1,128)S(1)}, bf16[128]{0:T(256)(128)(2,1)S(1)}) fusion(s32[128]{0:T(128)} %param.9), kind=kLoop, calls=%fused_computation.53 | loop fusion | flops 256 | bytes 1280 | tf_op jit(solution)/shard_map/broadcast_in_dim | solution.py:326
  1.4 1.8 %plan.1 = (bf16[8,8,1024]{2,1,0:T(8,128)(2,1)}, f32[1,256]{1,0:T(1,128)}) custom-call(s32[16,128]{1,0:T(8,128)} %bitcast.63, bf16[6,1024]{1,0:T(8,128)(2,1)} %pas_ref.1), custom_call_target="tpu_custom_call" | custom-call | flops 10000000 | bytes 152576 | tf_op jit(solution)/shard_map/plan/pallas_call | solution.py:62
  3.2 0.7 %copy-done.2 = f32[1,256]{1,0:T(1,128)S(1)} copy-done((f32[1,256]{1,0:T(1,128)S(1)}, f32[1,256]{1,0:T(1,128)}, u32[]{:S(2)}) %copy-start.2) | copy-done | bytes 1048
  3.9 1.0 %fusion.4 = bf16[136,1024]{1,0:T(8,128)(2,1)S(1)} fusion(bf16[1,384]{1,0:T(2,128)(2,1)S(1)} %broadcast_in_dim.7, bf16[128,1024]{1,0:T(8,128)(2,1)} %rows_ref.1), kind=kLoop, calls=%fused_computation.13 | loop fusion | flops 835584 | bytes 541440 | tf_op jit(solution)/shard_map/concatenate | solution.py:294
  4.9 3.0 %collective-permute-start = (bf16[136,1024]{1,0:T(8,128)(2,1)S(1)}, bf16[136,1024]{1,0:T(8,128)(2,1)S(1)}, u32[]{:S(2)}, u32[]{:S(2)}) collective-permute-start(bf16[136,1024]{1,0:T(8,128)(2,1)S(1)} %fusion.4), channel_id=1, source_target_pairs={{0,4},{4,0},{8,12},{12,8},{16,20},{20,16},{24,28},{28,24},{1,5},{5... | collective-permute-start | bytes 835592 | tf_op jit(solution)/shard_map/ppermute | solution.py:24
  8.0 4.9 %all-to-all-start = ((bf16[8,8,1024]{2,1,0:T(8,128)(2,1)}), bf16[8,8,1024]{2,1,0:T(8,128)(2,1)S(1)}, u32[]{:S(2)}, u32[]{:S(2)}) async-start(bf16[8,8,1024]{2,1,0:T(8,128)(2,1)} %get-tuple-element.15), calls=%async_computation | async-start | bytes 262144 | tf_op jit(solution)/shard_map/all_to_all | solution.py:14
  13.0 0.7 %copy-done.3 = s32[128]{0:T(128)S(1)} copy-done((s32[128]{0:T(128)S(1)}, s32[128]{0:T(128)}, u32[]{:S(2)}) %copy-start.3) | copy-done | bytes 536
  13.7 6.5 %all-to-all-done = bf16[8,8,1024]{2,1,0:T(8,128)(2,1)S(1)} async-done(((bf16[8,8,1024]{2,1,0:T(8,128)(2,1)}), bf16[8,8,1024]{2,1,0:T(8,128)(2,1)S(1)}, u32[]{:S(2)}, u32[]{:S(2)}) %all-to-all-start) | async-done | bytes 131104 | tf_op jit(solution)/shard_map/all_to_all | solution.py:14
  20.3 1.1 %convolution_convert_fusion = bf16[256,1024]{1,0:T(8,128)(2,1)} fusion(bf16[256,1024]{1,0:T(8,128)(2,1)S(1)} %copy-done, f32[256]{0:T(256)S(1)} %iota_convert_fusion, f32[256]{0:T(256)S(1)} %reshape.199), kind=kOutput, calls=%fused_computation | convolution fusion | flops 134545408 | bytes 1050624 | tf_op jit(solution)/shard_map/dot_general | solution.py:20
  21.4 3.6 %all-to-all-start.1 = ((bf16[8,32,1024]{2,1,0:T(8,128)(2,1)}), bf16[8,32,1024]{2,1,0:T(8,128)(2,1)S(1)}, u32[]{:S(2)}, u32[]{:S(2)}) async-start(bf16[8,32,1024]{2,1,0:T(8,128)(2,1)} %bitcast.14), calls=%async_computation.1 | async-start | bytes 1048576 | tf_op jit(solution)/shard_map/all_to_all | solution.py:14
  25.1 0.2 fusion.7
  25.4 0.2 convolution_convert_fusion.4.asks_ref
  25.6 0.2 convolution_convert_fusion.3.asks_ref
  25.8 0.2 convolution_convert_fusion.1
  26.1 0.2 broadcast_select_fusion.1
  26.3 0.8 %copy.9 = bf16[4,2,32,1024]{3,2,1,0:T(8,128)(2,1)} copy(bf16[4,2,32,1024]{3,2,0,1:T(8,128)(2,1)S(1)} %pad_maximum_fusion) | data formatting | bytes 1048576 | tf_op jit(solution)/shard_map/concatenate | solution.py:315
  27.2 10.8 %all-to-all-done.1 = bf16[8,32,1024]{2,1,0:T(8,128)(2,1)S(1)} async-done(((bf16[8,32,1024]{2,1,0:T(8,128)(2,1)}), bf16[8,32,1024]{2,1,0:T(8,128)(2,1)S(1)}, u32[]{:S(2)}, u32[]{:S(2)}) %all-to-all-start.1) | async-done | bytes 524320 | tf_op jit(solution)/shard_map/all_to_all | solution.py:14
  38.0 0.4 fusion.2
  38.6 1.1 %collective-permute-done.1 = f32[66,128]{1,0:T(8,128)S(1)} collective-permute-done((f32[66,128]{1,0:T(8,128)S(1)}, f32[66,128]{1,0:T(8,128)S(1)}, u32[]{:S(2)}, u32[]{:S(2)}) %collective-permute-start.1) | collective-permute-done | bytes 33824 | tf_op jit(solution)/shard_map/ppermute | solution.py:31
  39.7 1.5 %collective-permute-start.2 = (f32[66,128]{1,0:T(8,128)S(1)}, f32[66,128]{1,0:T(8,128)S(1)}, u32[]{:S(2)}, u32[]{:S(2)}) collective-permute-start(f32[66,128]{1,0:T(8,128)S(1)} %fusion.19), channel_id=1, source_target_pairs={{0,2},{1,3},{2,0},{3,1},{4,6},{5,7},{6,4},{7,5},{8,10},{9,11},{10,... | collective-permute-start | bytes 101384 | tf_op jit(solution)/shard_map/ppermute | solution.py:31
  41.3 3.5 %all-to-all-start.2 = ((bf16[4,64,1024]{2,1,0:T(8,128)(2,1)}), bf16[4,64,1024]{2,1,0:T(8,128)(2,1)S(1)}, u32[]{:S(2)}, u32[]{:S(2)}) async-start(bf16[4,64,1024]{2,1,0:T(8,128)(2,1)} %bitcast.13), calls=%async_computation.2 | async-start | bytes 1048576 | tf_op jit(solution)/shard_map/all_to_all | solution.py:14
  44.8 1.5 %collective-permute-start.3 = (f32[66,128]{1,0:T(8,128)S(1)}, f32[66,128]{1,0:T(8,128)S(1)}, u32[]{:S(2)}, u32[]{:S(2)}) collective-permute-start(f32[66,128]{1,0:T(8,128)S(1)} %add.48.sums_ref), channel_id=1, source_target_pairs={{0,4},{4,0},{8,12},{12,8},{16,20},{20,16},{24,28},{28,24},{1,5},{5... | collective-permute-start | bytes 101384 | tf_op jit(solution)/shard_map/ppermute | solution.py:24
  46.3 1.3 %soften.1 = (f32[1,128]{1,0:T(1,128)}, bf16[64,128]{1,0:T(8,128)(2,1)S(1)}, bf16[256,128]{1,0:T(8,128)(2,1)S(1)}, bf16[256,128]{1,0:T(8,128)(2,1)S(1)}, f32[4,8,1024]{2,1,0:T(8,128)S(1)}) custom-call(s32[2]{0:T(128)S(1)} %pad_add_fusion.4.where_ref, f32[66,128]{1,0:T(8,128)S(1)} %add.48.sums_ref, bf16[256,128]{1,0:T(8,128)(2,1)S(1)} %convolution_convert_fusion.4.asks_ref, ...), custom_call_target="tpu_custom_call" | custom-call | flops 10000000 | bytes 641032 | tf_op jit(solution)/shard_map/soften/pallas_call | solution.py:62
  47.7 0.2 fusion.22
  47.9 0.3 fusion.21
  48.2 0.6 %collective-permute-done.3.sums_ref = f32[66,128]{1,0:T(8,128)S(1)} collective-permute-done((f32[66,128]{1,0:T(8,128)S(1)}, f32[66,128]{1,0:T(8,128)S(1)}, u32[]{:S(2)}, u32[]{:S(2)}) %collective-permute-start.3) | collective-permute-done | bytes 33824 | tf_op jit(solution)/shard_map/ppermute | solution.py:24
  48.8 1.1 %soften_pair.1 = f32[4,8,1024]{2,1,0:T(8,128)S(1)} custom-call(s32[2]{0:T(128)S(1)} %pad_add_fusion.5.where_ref, f32[66,128]{1,0:T(8,128)S(1)} %collective-permute-done.3.sums_ref, bf16[256,128]{1,0:T(8,128)(2,1)S(1)} %convolution_convert_fusion.3.asks_ref, f32[1,128]{1,0:T(1,128)S(1)} %fusion.15.counts_ref, bf16[128,1024]{1,0:T(8,128)(2,1)S(1)} %slice.36.rows_ref, ...), custom_call_target="tpu_custom_call" | custom-call | flops 10000000 | bytes 624136 | tf_op jit(solution)/shard_map/soften_pair/pallas_call | solution.py:62
  50.0 2.0 %collective-permute-start.4 = (f32[8,1024]{1,0:T(8,128)S(1)}, f32[8,1024]{1,0:T(8,128)S(1)}, u32[]{:S(2)}, u32[]{:S(2)}) collective-permute-start(f32[8,1024]{1,0:T(8,128)S(1)} %get-tuple-element.30), channel_id=1, source_target_pairs={{0,8},{4,12},{8,0},{12,4},{16,24},{20,28},{24,16},{28,20},{1,9},{5... | collective-permute-start | bytes 98312 | tf_op jit(solution)/shard_map/ppermute | solution.py:51
  52.0 2.4 %collective-permute-start.5 = (f32[8,1024]{1,0:T(8,128)S(1)}, f32[8,1024]{1,0:T(8,128)S(1)}, u32[]{:S(2)}, u32[]{:S(2)}) collective-permute-start(f32[8,1024]{1,0:T(8,128)S(1)} %get-tuple-element.29), channel_id=1, source_target_pairs={{0,16},{4,20},{8,24},{12,28},{16,0},{20,4},{24,8},{28,12},{1,17},{... | collective-permute-start | bytes 98312 | tf_op jit(solution)/shard_map/ppermute | solution.py:51
  54.4 1.0 %fusion.1 = f32[128,1024]{1,0:T(8,128)} fusion(f32[128,1024]{1,0:T(8,128)S(1)} %fusion.22, f32[128,1024]{1,0:T(8,128)S(1)} %fusion.21, bf16[64,128]{1,0:T(8,128)(2,1)S(1)} %get-tuple-element.19, bf16[8,8,1024]{2,1,0:T(8,128)(2,1)S(1)} %all-to-all-done), kind=kOutput, calls=%fused_computation.3 | convolution fusion | flops 17170432 | bytes 1720320 | tf_op jit(solution)/shard_map/dot_general | solution.py:20
  55.5 6.5 %collective-permute-done.5.refs_2_ = f32[8,1024]{1,0:T(8,128)S(1)} collective-permute-done((f32[8,1024]{1,0:T(8,128)S(1)}, f32[8,1024]{1,0:T(8,128)S(1)}, u32[]{:S(2)}, u32[]{:S(2)}) %collective-permute-start.5) | collective-permute-done | bytes 32800 | tf_op jit(solution)/shard_map/ppermute | solution.py:51
  62.0 1.3 %close.1 = (f32[6,1024]{1,0:T(8,128)}, f32[256,1024]{1,0:T(8,128)}) custom-call(f32[8,1024]{1,0:T(8,128)S(1)} %get-tuple-element.31.refs_0_, f32[8,1024]{1,0:T(8,128)S(1)} %collective-permute-done.4.refs_1_, f32[8,1024]{1,0:T(8,128)S(1)} %collective-permute-done.5.refs_2_, f32[8,1024]{1,0:T(8,128)S(1)} %collective-permute-done.6.refs_3_, ...), custom_call_target="tpu_custom_call" | custom-call | flops 268435456 | bytes 1729536 | tf_op jit(solution)/shard_map/close/pallas_call | solution.py:62
  (38 shorter events, 0.8 us)
Async XLA Ops:
  0.6 19.6 %copy-start = (bf16[256,1024]{1,0:T(8,128)(2,1)S(1)}, bf16[256,1024]{1,0:T(8,128)(2,1)}, u32[]{:S(2)}) copy-start(bf16[256,1024]{1,0:T(8,128)(2,1)} %param.7) | copy-start | bytes 1572868
  3.2 0.7 %copy-start.2 = (f32[1,256]{1,0:T(1,128)S(1)}, f32[1,256]{1,0:T(1,128)}, u32[]{:S(2)}) copy-start(f32[1,256]{1,0:T(1,128)} %get-tuple-element.16) | copy-start | bytes 3076
  4.9 20.4 %collective-permute-start = (bf16[136,1024]{1,0:T(8,128)(2,1)S(1)}, bf16[136,1024]{1,0:T(8,128)(2,1)S(1)}, u32[]{:S(2)}, u32[]{:S(2)}) collective-permute-start(bf16[136,1024]{1,0:T(8,128)(2,1)S(1)} %fusion.4), channel_id=1, source_target_pairs={{0,4},{4,0},{8,12},{12,8},{16,20},{20,16},{24,28},{28,24},{1,5},{5... | collective-permute-start | bytes 835592 | tf_op jit(solution)/shard_map/ppermute | solution.py:24
  8.0 12.2 %all-to-all-start = ((bf16[8,8,1024]{2,1,0:T(8,128)(2,1)}), bf16[8,8,1024]{2,1,0:T(8,128)(2,1)S(1)}, u32[]{:S(2)}, u32[]{:S(2)}) async-start(bf16[8,8,1024]{2,1,0:T(8,128)(2,1)} %get-tuple-element.15), calls=%async_computation | async-start | bytes 262144 | tf_op jit(solution)/shard_map/all_to_all | solution.py:14
  13.0 0.7 %copy-start.3 = (s32[128]{0:T(128)S(1)}, s32[128]{0:T(128)}, u32[]{:S(2)}) copy-start(s32[128]{0:T(128)} %param.9) | copy-start | bytes 1540
  21.4 3.6 %copy-start.1 = (bf16[128,1024]{1,0:T(8,128)(2,1)S(1)}, bf16[128,1024]{1,0:T(8,128)(2,1)}, u32[]{:S(2)}) copy-start(bf16[128,1024]{1,0:T(8,128)(2,1)} %rows_ref.1) | copy-start | bytes 786436
  21.4 16.6 %all-to-all-start.1 = ((bf16[8,32,1024]{2,1,0:T(8,128)(2,1)}), bf16[8,32,1024]{2,1,0:T(8,128)(2,1)S(1)}, u32[]{:S(2)}, u32[]{:S(2)}) async-start(bf16[8,32,1024]{2,1,0:T(8,128)(2,1)} %bitcast.14), calls=%async_computation.1 | async-start | bytes 1048576 | tf_op jit(solution)/shard_map/all_to_all | solution.py:14
  38.4 1.3 %collective-permute-start.1 = (f32[66,128]{1,0:T(8,128)S(1)}, f32[66,128]{1,0:T(8,128)S(1)}, u32[]{:S(2)}, u32[]{:S(2)}) collective-permute-start(f32[66,128]{1,0:T(8,128)S(1)} %pad_maximum_fusion.1), channel_id=1, source_target_pairs={{0,1},{1,0},{2,3},{3,2},{4,5},{5,4},{6,7},{7,6},{8,9},{9,8},{10,11... | collective-permute-start | bytes 101384 | tf_op jit(solution)/shard_map/ppermute | solution.py:31
  39.7 5.0 %collective-permute-start.2 = (f32[66,128]{1,0:T(8,128)S(1)}, f32[66,128]{1,0:T(8,128)S(1)}, u32[]{:S(2)}, u32[]{:S(2)}) collective-permute-start(f32[66,128]{1,0:T(8,128)S(1)} %fusion.19), channel_id=1, source_target_pairs={{0,2},{1,3},{2,0},{3,1},{4,6},{5,7},{6,4},{7,5},{8,10},{9,11},{10,... | collective-permute-start | bytes 101384 | tf_op jit(solution)/shard_map/ppermute | solution.py:31
  41.3 20.7 %all-to-all-start.2 = ((bf16[4,64,1024]{2,1,0:T(8,128)(2,1)}), bf16[4,64,1024]{2,1,0:T(8,128)(2,1)S(1)}, u32[]{:S(2)}, u32[]{:S(2)}) async-start(bf16[4,64,1024]{2,1,0:T(8,128)(2,1)} %bitcast.13), calls=%async_computation.2 | async-start | bytes 1048576 | tf_op jit(solution)/shard_map/all_to_all | solution.py:14
  44.8 4.0 %collective-permute-start.3 = (f32[66,128]{1,0:T(8,128)S(1)}, f32[66,128]{1,0:T(8,128)S(1)}, u32[]{:S(2)}, u32[]{:S(2)}) collective-permute-start(f32[66,128]{1,0:T(8,128)S(1)} %add.48.sums_ref), channel_id=1, source_target_pairs={{0,4},{4,0},{8,12},{12,8},{16,20},{20,16},{24,28},{28,24},{1,5},{5... | collective-permute-start | bytes 101384 | tf_op jit(solution)/shard_map/ppermute | solution.py:24
  50.0 5.5 %collective-permute-start.4 = (f32[8,1024]{1,0:T(8,128)S(1)}, f32[8,1024]{1,0:T(8,128)S(1)}, u32[]{:S(2)}, u32[]{:S(2)}) collective-permute-start(f32[8,1024]{1,0:T(8,128)S(1)} %get-tuple-element.30), channel_id=1, source_target_pairs={{0,8},{4,12},{8,0},{12,4},{16,24},{20,28},{24,16},{28,20},{1,9},{5... | collective-permute-start | bytes 98312 | tf_op jit(solution)/shard_map/ppermute | solution.py:51
  52.0 10.0 %collective-permute-start.5 = (f32[8,1024]{1,0:T(8,128)S(1)}, f32[8,1024]{1,0:T(8,128)S(1)}, u32[]{:S(2)}, u32[]{:S(2)}) collective-permute-start(f32[8,1024]{1,0:T(8,128)S(1)} %get-tuple-element.29), channel_id=1, source_target_pairs={{0,16},{4,20},{8,24},{12,28},{16,0},{20,4},{24,8},{28,12},{1,17},{... | collective-permute-start | bytes 98312 | tf_op jit(solution)/shard_map/ppermute | solution.py:51
  54.4 7.6 %collective-permute-start.6 = (f32[8,1024]{1,0:T(8,128)S(1)}, f32[8,1024]{1,0:T(8,128)S(1)}, u32[]{:S(2)}, u32[]{:S(2)}) collective-permute-start(f32[8,1024]{1,0:T(8,128)S(1)} %get-tuple-element.28), channel_id=1, source_target_pairs={{0,24},{4,28},{8,16},{12,20},{16,8},{20,12},{24,0},{28,4},{1,25},{... | collective-permute-start | bytes 98312 | tf_op jit(solution)/shard_map/ppermute | solution.py:51

commit v5 on v4

--- a/solution.py
+++ b/solution.py
@@ -10,10 +10,22 @@
 F32 = jnp.float32
 
 
-def exchange(x, groups=None):
+def line_order(lines):
+    return [2, 1, 3, 0] if lines == 4 else list(range(lines))
+
+
+def peer_order(peers):
+    return [2 * line + odd for odd in range(2) for line in line_order(peers // 2)]
+
+
+def exchange(x, groups):
     return lax.all_to_all(
         x, "dp", split_axis=0, concat_axis=0, tiled=True, axis_index_groups=groups
     )
+
+
+def everyone():
+    return [peer_order(lax.axis_size("dp"))]
 
 
 def dot(a, b, ca, cb):
@@ -34,8 +46,12 @@
 
 
 def line_groups():
-    peers = lax.axis_size("dp")
-    return [list(range(odd, peers, 2)) for odd in range(2)]
+    order = line_order(lax.axis_size("dp") // 2)
+    return [[2 * line + odd for line in order] for odd in range(2)]
+
+
+def place_of(order, value):
+    return sum(jnp.where(value == d, order.index(d), 0) for d in order)
 
 
 def scatter_sum(x):
@@ -44,10 +60,11 @@
     if lines > 4 or lines & (lines - 1):
         return [jnp.sum(exchange(x, line_groups()), 0)]
     line = lax.axis_index("dp") // 2
-    total = lax.dynamic_index_in_dim(x, line, 0, False)
+    order = line_order(lines)
+    total = lax.dynamic_index_in_dim(x, place_of(order, line), 0, False)
     parts = []
     for k in range(1, lines):
-        part = lax.dynamic_index_in_dim(x, line ^ k, 0, False)
+        part = lax.dynamic_index_in_dim(x, place_of(order, line ^ k), 0, False)
         parts.append(lax.ppermute(part, "dp", [(i, i ^ (2 * k)) for i in range(size)]))
     return [total] + parts
 
@@ -71,6 +88,7 @@
     pas, width = passages.shape
     cap = bank_rows // 8
     slots, places = 2 * q_rows, peers * cap
+    order = peer_order(peers)
 
     def kernel(ids_ref, pas_ref, block_ref, place_ref):
         ident = (ids_ref[...] + 1).astype(F32)
@@ -89,7 +107,10 @@
         owner_col = jnp.sum(jnp.where(down == along, owner, 0.0), 1, keepdims=True)
         before = (owner_col == owner) & (down < along)
         rank = jnp.sum(before.astype(F32), 0, keepdims=True)
-        place = jnp.where(sid > 0, owner * cap + rank, float(places))
+        spot = jnp.zeros_like(owner)
+        for j, d in enumerate(order):
+            spot = jnp.where(owner == d, float(j), spot)
+        place = jnp.where(sid > 0, spot * cap + rank, float(places))
         place_ref[...] = place
         perm = iota((places, slots), 0).astype(F32) == place
         id_col = jnp.sum(jnp.where(perm, local, 0.0), 1, keepdims=True) - 1
@@ -161,15 +182,15 @@
             lo_ref[...] = (coeffs - hi.astype(F32)).astype(BF)
         else:
             base_ref, sent_ref = refs
-        split_w = weights.reshape(lines, 2, pad, q_rows)
-        near_w = jnp.where(odd, split_w[:, 1], split_w[:, 0]).reshape(lines * pad, q_rows)
+        half = lines * pad
+        near_w = jnp.where(odd, weights[half:], weights[:half])
         part = jnp.dot(near_w.astype(BF), rows_ref[...], preferred_element_type=F32)
         part = part.reshape(lines, pad, width)
         coeff = jnp.sum(coeffs, 1, keepdims=True)
         down, lane = iota((places, places), 0), iota((places, places), 1)
         left = jnp.where(down % cap == lane - source * cap, coeff, 0.0)
         line, at = iota((lines, places), 0), iota((lines, places), 1) // cap
-        pick = (at == 2 * line + where_ref[0]).astype(BF)
+        pick = (at == line + lines * where_ref[0]).astype(BF)
         row = jnp.zeros((lines, places), F32)
         for _ in range(3):
             piece = left.astype(BF)
@@ -282,12 +303,13 @@
     pas = passages.shape[0]
     pad = -(-(pas + 1) // 8) * 8
     max_pos = ids.shape[1]
-    near = lambda x: jnp.where(odd, x[:, 1], x[:, 0])
+    half = places // 2
+    near = lambda x: jnp.where(odd, x[half:], x[:half])
 
     block, place = plan(ids.T, passages, peers, bank_rows, pad)
     slots = place.shape[0]
     perm = jnp.arange(places)[:, None] == place[None, :]
-    heads = exchange(block)
+    heads = exchange(block, everyone())
 
     notes = jnp.concatenate([place.astype(BF), counts.astype(BF)])
     notes = jnp.pad(notes[None], ((0, 7), (0, width - notes.shape[0])))
@@ -304,12 +326,11 @@
     wanted = heads[:, pas, :cap].astype(F32).reshape(-1)
     pick = (wanted[:, None] == jnp.arange(bank_rows).astype(F32)[None, :]).astype(BF)
     picked = dot(pick, bank, 1, 0).astype(BF)
-    fetched = exchange(picked.reshape(peers, cap, width)).reshape(places, width)
+    fetched = exchange(picked.reshape(peers, cap, width), everyone()).reshape(places, width)
 
     send = []
     for ask, rows in ((asks, queries), (pair_asks, pair_q)):
-        ask = near(ask.reshape(lines, 2, cap, q_rows)).reshape(-1, q_rows)
-        send.append(dot(ask, rows, 1, 0).astype(BF).reshape(lines, 1, cap, width))
+        send.append(dot(near(ask), rows, 1, 0).astype(BF).reshape(lines, 1, cap, width))
     even_send = jnp.where(odd, send[1], send[0])
     odd_send = jnp.where(odd, send[0], send[1])
     q_send = jnp.concatenate([even_send, odd_send], 1).reshape(lines, 2 * cap, width)
@@ -321,7 +342,8 @@
     pos_part = jnp.sum(jnp.where(asks > 0.5, dot(fetched, queries, 1, 1), 0.0), 1)
     mine = sub_sum(jnp.concatenate([part, pos_part.reshape(-1, q_rows)]))
     pair = to_pair(mine)
-    spot = lambda source: jnp.stack([me % 2, source]).astype(jnp.int32)
+    at = 2 * place_of(line_order(lines), me // 2)
+    spot = lambda source: jnp.stack([me % 2, at + source % 2]).astype(jnp.int32)
     losses, weights, hi, lo, sent = soften(
         mine, asks, counts.astype(F32)[None], queries, spot(me), pas
     )
@@ -333,6 +355,7 @@
     query_grad = 50.0 * (
         dot(weights, all_pas, 0, 0) + dot(hi, fetched, 0, 0) + dot(lo, fetched, 0, 0)
     )
+    wanted = wanted.reshape(2, lines, cap).swapaxes(0, 1).reshape(-1)
     passage_grad, bank_grad = close(got, wanted, q_got, pas, bank_rows)
     return (losses[0], query_grad, passage_grad, bank_grad)
 

time: 63.9 us -> 60.3 us (0.944)
  waiting for transfers between devices: 25.6 us -> 17.2 us
  starting transfers between devices: 22.6 us -> 27.4 us
    all_to_all x3, waiting for transfers between devices: 17.3 us -> 11.6 us  [exchange(): lax.all_to_all(x, 'dp', split_axis=0, concat_axis=0, tiled=True, axis_ind...]
    all_to_all x3, starting transfers between devices: 12 us -> 17 us  [exchange(): lax.all_to_all(x, 'dp', split_axis=0, concat_axis=0, tiled=True, axis_ind...]
    ppermute x3, waiting for transfers between devices: 6.51 us -> 3.67 us  [scatter_sum(): lax.ppermute(part, 'dp', [(i, i ^ 2 * k) for i in range(size)])]
  transfers between devices with their start and end apart: 10 -> 10, of which waited for: 5 -> 5; matrix products, arithmetic and copies ran while one was open for 8% -> 9% of each run, Pallas kernels for 4% -> 4%
where the time goes in v5:
time: 60.3 us; the launch traced here: 59.8 us
  starting transfers between devices  27.4 us (45%)
  waiting for transfers between devices  17.2 us (29%)
  Pallas kernels  5.62 us (9%)
  matrix products  4.1 us (7%)
  local copies, waits for them, and re-layouts  2.41 us (4%)
  other arithmetic  2.13 us (4%)
  between operations  0.86 us (1%)
    all_to_all x3, starting transfers between devices, exchange(): lax.all_to_all(x, 'dp', split_axis=0, concat_axis=0, tiled=True, axis_ind...  17 us
    all_to_all x3, waiting for transfers between devices, exchange(): lax.all_to_all(x, 'dp', split_axis=0, concat_axis=0, tiled=True, axis_ind...  11.6 us
    pallas_call x4, Pallas kernels, call(): pl.pallas_call(kernel, out_shape=outs, cost_estimate=cost, **kw)(*args)  5.62 us
    ppermute x3, starting transfers between devices, scatter_sum(): lax.ppermute(part, 'dp', [(i, i ^ 2 * k) for i in range(size)])  4.45 us
    ppermute x2, starting transfers between devices, to_pair(): lax.ppermute(x, 'dp', [(i, i ^ 1) for i in range(lax.axis_size('dp'))])  4.36 us
    dot_general x10, matrix products, dot(): lax.dot_general(a, b, (((ca,), (cb,)), ((), ())), preferred_element_type=...  4.1 us
    ppermute x3, waiting for transfers between devices, scatter_sum(): lax.ppermute(part, 'dp', [(i, i ^ 2 * k) for i in range(size)])  3.67 us
    ppermute x2, starting transfers between devices, sub_sum(): x = x + lax.ppermute(x, 'sub', [(i, i ^ step) for i in range(size)])  1.59 us
  transfers between devices with their start and end apart: 10, of which 5 were waited for; matrix products, arithmetic and copies ran while one was open for 9% of the time, Pallas kernels for 4%

profile of v5, /device:TPU:0, one launch (start us, length us, event | category | flops | bytes accessed | tf_op | source)
XLA Modules:
  0.0 59.8 jit_solution(2173612524032079584)
XLA Ops:
  0.6 0.7 %convert_bitcast_fusion = (f32[1,128]{1,0:T(1,128)S(1)}, bf16[128]{0:T(256)(128)(2,1)S(1)}) fusion(s32[128]{0:T(128)} %param.9), kind=kLoop, calls=%fused_computation.58 | loop fusion | flops 256 | bytes 1280 | tf_op jit(solution)/shard_map/broadcast_in_dim | solution.py:348
  1.4 1.8 %plan.1 = (bf16[8,8,1024]{2,1,0:T(8,128)(2,1)}, f32[1,256]{1,0:T(1,128)}) custom-call(s32[16,128]{1,0:T(8,128)} %bitcast.57, bf16[6,1024]{1,0:T(8,128)(2,1)} %pas_ref.1), custom_call_target="tpu_custom_call" | custom-call | flops 10000000 | bytes 152576 | tf_op jit(solution)/shard_map/plan/pallas_call | solution.py:79
  3.2 0.7 %copy-done.2 = f32[1,256]{1,0:T(1,128)S(1)} copy-done((f32[1,256]{1,0:T(1,128)S(1)}, f32[1,256]{1,0:T(1,128)}, u32[]{:S(2)}) %copy-start.2) | copy-done | bytes 1048
  3.9 1.0 %fusion.4 = bf16[136,1024]{1,0:T(8,128)(2,1)S(1)} fusion(bf16[1,384]{1,0:T(2,128)(2,1)S(1)} %broadcast_in_dim.7, bf16[128,1024]{1,0:T(8,128)(2,1)} %rows_ref.1), kind=kLoop, calls=%fused_computation.13 | loop fusion | flops 835584 | bytes 541440 | tf_op jit(solution)/shard_map/concatenate | solution.py:316
  4.9 3.0 %collective-permute-start = (bf16[136,1024]{1,0:T(8,128)(2,1)S(1)}, bf16[136,1024]{1,0:T(8,128)(2,1)S(1)}, u32[]{:S(2)}, u32[]{:S(2)}) collective-permute-start(bf16[136,1024]{1,0:T(8,128)(2,1)S(1)} %fusion.4), channel_id=1, source_target_pairs={{0,4},{4,0},{8,12},{12,8},{16,20},{20,16},{24,28},{28,24},{1,5},{5... | collective-permute-start | bytes 835592 | tf_op jit(solution)/shard_map/ppermute | solution.py:36
  8.0 5.9 %all-to-all-start = ((bf16[8,8,1024]{2,1,0:T(8,128)(2,1)}), bf16[8,8,1024]{2,1,0:T(8,128)(2,1)S(1)}, u32[]{:S(2)}, u32[]{:S(2)}) async-start(bf16[8,8,1024]{2,1,0:T(8,128)(2,1)} %get-tuple-element.15), calls=%async_computation | async-start | bytes 262144 | tf_op jit(solution)/shard_map/all_to_all | solution.py:22
  14.1 0.7 %copy-done.3 = s32[128]{0:T(128)S(1)} copy-done((s32[128]{0:T(128)S(1)}, s32[128]{0:T(128)}, u32[]{:S(2)}) %copy-start.3) | copy-done | bytes 536
  14.7 4.1 %all-to-all-done = bf16[8,8,1024]{2,1,0:T(8,128)(2,1)S(1)} async-done(((bf16[8,8,1024]{2,1,0:T(8,128)(2,1)}), bf16[8,8,1024]{2,1,0:T(8,128)(2,1)S(1)}, u32[]{:S(2)}, u32[]{:S(2)}) %all-to-all-start) | async-done | bytes 131104 | tf_op jit(solution)/shard_map/all_to_all | solution.py:22
  18.9 1.1 %convolution_convert_fusion = bf16[256,1024]{1,0:T(8,128)(2,1)} fusion(bf16[256,1024]{1,0:T(8,128)(2,1)S(1)} %copy-done, f32[256]{0:T(256)S(1)} %iota_convert_fusion, f32[256]{0:T(256)S(1)} %reshape.172), kind=kOutput, calls=%fused_computation | convolution fusion | flops 134545408 | bytes 1050624 | tf_op jit(solution)/shard_map/dot_general | solution.py:32
  20.1 5.2 %all-to-all-start.1 = ((bf16[8,32,1024]{2,1,0:T(8,128)(2,1)}), bf16[8,32,1024]{2,1,0:T(8,128)(2,1)S(1)}, u32[]{:S(2)}, u32[]{:S(2)}) async-start(bf16[8,32,1024]{2,1,0:T(8,128)(2,1)} %bitcast.10), calls=%async_computation.1 | async-start | bytes 1048576 | tf_op jit(solution)/shard_map/all_to_all | solution.py:22
  25.3 0.2 fusion.7
  25.6 0.2 convolution_convert_fusion.4.asks_ref
  26.0 0.2 convolution_convert_fusion.1
  26.2 0.2 broadcast_select_fusion.1
  26.5 0.8 %copy.10 = bf16[4,2,32,1024]{3,2,1,0:T(8,128)(2,1)} copy(bf16[4,2,32,1024]{3,2,0,1:T(8,128)(2,1)S(1)} %pad_maximum_fusion) | data formatting | bytes 1048576 | tf_op jit(solution)/shard_map/concatenate | solution.py:336
  27.4 7.5 %all-to-all-done.1 = bf16[8,32,1024]{2,1,0:T(8,128)(2,1)S(1)} async-done(((bf16[8,32,1024]{2,1,0:T(8,128)(2,1)}), bf16[8,32,1024]{2,1,0:T(8,128)(2,1)S(1)}, u32[]{:S(2)}, u32[]{:S(2)}) %all-to-all-start.1) | async-done | bytes 524320 | tf_op jit(solution)/shard_map/all_to_all | solution.py:22
  34.9 0.4 fusion.2
  35.5 1.1 %collective-permute-done.1 = f32[66,128]{1,0:T(8,128)S(1)} collective-permute-done((f32[66,128]{1,0:T(8,128)S(1)}, f32[66,128]{1,0:T(8,128)S(1)}, u32[]{:S(2)}, u32[]{:S(2)}) %collective-permute-start.1) | collective-permute-done | bytes 33824 | tf_op jit(solution)/shard_map/ppermute | solution.py:43
  36.6 1.5 %collective-permute-start.2 = (f32[66,128]{1,0:T(8,128)S(1)}, f32[66,128]{1,0:T(8,128)S(1)}, u32[]{:S(2)}, u32[]{:S(2)}) collective-permute-start(f32[66,128]{1,0:T(8,128)S(1)} %fusion.23), channel_id=1, source_target_pairs={{0,2},{1,3},{2,0},{3,1},{4,6},{5,7},{6,4},{7,5},{8,10},{9,11},{10,... | collective-permute-start | bytes 101384 | tf_op jit(solution)/shard_map/ppermute | solution.py:43
  38.1 5.9 %all-to-all-start.2 = ((bf16[4,64,1024]{2,1,0:T(8,128)(2,1)}), bf16[4,64,1024]{2,1,0:T(8,128)(2,1)S(1)}, u32[]{:S(2)}, u32[]{:S(2)}) async-start(bf16[4,64,1024]{2,1,0:T(8,128)(2,1)} %bitcast.9), calls=%async_computation.2 | async-start | bytes 1048576 | tf_op jit(solution)/shard_map/all_to_all | solution.py:22
  44.1 1.3 %collective-permute-start.3 = (f32[66,128]{1,0:T(8,128)S(1)}, f32[66,128]{1,0:T(8,128)S(1)}, u32[]{:S(2)}, u32[]{:S(2)}) collective-permute-start(f32[66,128]{1,0:T(8,128)S(1)} %add.92.sums_ref), channel_id=1, source_target_pairs={{0,4},{4,0},{8,12},{12,8},{16,20},{20,16},{24,28},{28,24},{1,5},{5... | collective-permute-start | bytes 101384 | tf_op jit(solution)/shard_map/ppermute | solution.py:36
  45.4 1.3 %soften.1 = (f32[1,128]{1,0:T(1,128)}, bf16[64,128]{1,0:T(8,128)(2,1)S(1)}, bf16[256,128]{1,0:T(8,128)(2,1)S(1)}, bf16[256,128]{1,0:T(8,128)(2,1)S(1)}, f32[4,8,1024]{2,1,0:T(8,128)S(1)}) custom-call(s32[2]{0:T(128)S(1)} %pad_add_fusion.4.where_ref, f32[66,128]{1,0:T(8,128)S(1)} %add.92.sums_ref, bf16[256,128]{1,0:T(8,128)(2,1)S(1)} %convolution_convert_fusion.4.asks_ref, ...), custom_call_target="tpu_custom_call" | custom-call | flops 10000000 | bytes 641032 | tf_op jit(solution)/shard_map/soften/pallas_call | solution.py:79
  46.7 0.2 fusion.26
  47.0 0.3 fusion.25
  47.3 0.8 %collective-permute-done.3.sums_ref = f32[66,128]{1,0:T(8,128)S(1)} collective-permute-done((f32[66,128]{1,0:T(8,128)S(1)}, f32[66,128]{1,0:T(8,128)S(1)}, u32[]{:S(2)}, u32[]{:S(2)}) %collective-permute-start.3) | collective-permute-done | bytes 33824 | tf_op jit(solution)/shard_map/ppermute | solution.py:36
  48.1 1.1 %soften_pair.1 = f32[4,8,1024]{2,1,0:T(8,128)S(1)} custom-call(s32[2]{0:T(128)S(1)} %pad_add_fusion.5.where_ref, f32[66,128]{1,0:T(8,128)S(1)} %collective-permute-done.3.sums_ref, bf16[256,128]{1,0:T(8,128)(2,1)S(1)} %convolution_convert_fusion.3.asks_ref, f32[1,128]{1,0:T(1,128)S(1)} %fusion.19.counts_ref, bf16[128,1024]{1,0:T(8,128)(2,1)S(1)} %slice.36.rows_ref, ...), custom_call_target="tpu_custom_call" | custom-call | flops 10000000 | bytes 624136 | tf_op jit(solution)/shard_map/soften_pair/pallas_call | solution.py:79
  49.3 0.6 %collective-permute-start.4 = (f32[8,1024]{1,0:T(8,128)S(1)}, f32[8,1024]{1,0:T(8,128)S(1)}, u32[]{:S(2)}, u32[]{:S(2)}) collective-permute-start(f32[8,1024]{1,0:T(8,128)S(1)} %get-tuple-element.30), channel_id=1, source_target_pairs={{0,8},{4,12},{8,0},{12,4},{16,24},{20,28},{24,16},{28,20},{1,9},{5... | collective-permute-start | bytes 98312 | tf_op jit(solution)/shard_map/ppermute | solution.py:68
  49.9 1.7 %collective-permute-start.5 = (f32[8,1024]{1,0:T(8,128)S(1)}, f32[8,1024]{1,0:T(8,128)S(1)}, u32[]{:S(2)}, u32[]{:S(2)}) collective-permute-start(f32[8,1024]{1,0:T(8,128)S(1)} %get-tuple-element.29), channel_id=1, source_target_pairs={{0,16},{4,20},{8,24},{12,28},{16,0},{20,4},{24,8},{28,12},{1,17},{... | collective-permute-start | bytes 98312 | tf_op jit(solution)/shard_map/ppermute | solution.py:68
  51.5 2.2 %collective-permute-start.6 = (f32[8,1024]{1,0:T(8,128)S(1)}, f32[8,1024]{1,0:T(8,128)S(1)}, u32[]{:S(2)}, u32[]{:S(2)}) collective-permute-start(f32[8,1024]{1,0:T(8,128)S(1)} %get-tuple-element.28), channel_id=1, source_target_pairs={{0,24},{4,28},{8,16},{12,20},{16,8},{20,12},{24,0},{28,4},{1,25},{... | collective-permute-start | bytes 98312 | tf_op jit(solution)/shard_map/ppermute | solution.py:68
  53.7 1.0 %fusion.1 = f32[128,1024]{1,0:T(8,128)} fusion(f32[128,1024]{1,0:T(8,128)S(1)} %fusion.26, f32[128,1024]{1,0:T(8,128)S(1)} %fusion.25, bf16[64,128]{1,0:T(8,128)(2,1)S(1)} %get-tuple-element.19, bf16[8,8,1024]{2,1,0:T(8,128)(2,1)S(1)} %all-to-all-done), kind=kOutput, calls=%fused_computation.3 | convolution fusion | flops 17170432 | bytes 1720320 | tf_op jit(solution)/shard_map/dot_general | solution.py:32
  54.8 3.7 %collective-permute-done.5.refs_2_ = f32[8,1024]{1,0:T(8,128)S(1)} collective-permute-done((f32[8,1024]{1,0:T(8,128)S(1)}, f32[8,1024]{1,0:T(8,128)S(1)}, u32[]{:S(2)}, u32[]{:S(2)}) %collective-permute-start.5) | collective-permute-done | bytes 32800 | tf_op jit(solution)/shard_map/ppermute | solution.py:68
  58.4 1.3 %close.1 = (f32[6,1024]{1,0:T(8,128)}, f32[256,1024]{1,0:T(8,128)}) custom-call(f32[8,1024]{1,0:T(8,128)S(1)} %get-tuple-element.31.refs_0_, f32[8,1024]{1,0:T(8,128)S(1)} %collective-permute-done.4.refs_1_, f32[8,1024]{1,0:T(8,128)S(1)} %collective-permute-done.5.refs_2_, f32[8,1024]{1,0:T(8,128)S(1)} %collective-permute-done.6.refs_3_, ...), custom_call_target="tpu_custom_call" | custom-call | flops 268435456 | bytes 1729536 | tf_op jit(solution)/shard_map/close/pallas_call | solution.py:79
  (38 shorter events, 0.9 us)
Async XLA Ops:
  0.6 18.3 %copy-start = (bf16[256,1024]{1,0:T(8,128)(2,1)S(1)}, bf16[256,1024]{1,0:T(8,128)(2,1)}, u32[]{:S(2)}) copy-start(bf16[256,1024]{1,0:T(8,128)(2,1)} %param.7) | copy-start | bytes 1572868
  3.2 0.7 %copy-start.2 = (f32[1,256]{1,0:T(1,128)S(1)}, f32[1,256]{1,0:T(1,128)}, u32[]{:S(2)}) copy-start(f32[1,256]{1,0:T(1,128)} %get-tuple-element.16) | copy-start | bytes 3076
  4.9 20.6 %collective-permute-start = (bf16[136,1024]{1,0:T(8,128)(2,1)S(1)}, bf16[136,1024]{1,0:T(8,128)(2,1)S(1)}, u32[]{:S(2)}, u32[]{:S(2)}) collective-permute-start(bf16[136,1024]{1,0:T(8,128)(2,1)S(1)} %fusion.4), channel_id=1, source_target_pairs={{0,4},{4,0},{8,12},{12,8},{16,20},{20,16},{24,28},{28,24},{1,5},{5... | collective-permute-start | bytes 835592 | tf_op jit(solution)/shard_map/ppermute | solution.py:36
  8.0 10.9 %all-to-all-start = ((bf16[8,8,1024]{2,1,0:T(8,128)(2,1)}), bf16[8,8,1024]{2,1,0:T(8,128)(2,1)S(1)}, u32[]{:S(2)}, u32[]{:S(2)}) async-start(bf16[8,8,1024]{2,1,0:T(8,128)(2,1)} %get-tuple-element.15), calls=%async_computation | async-start | bytes 262144 | tf_op jit(solution)/shard_map/all_to_all | solution.py:22
  14.1 0.7 %copy-start.3 = (s32[128]{0:T(128)S(1)}, s32[128]{0:T(128)}, u32[]{:S(2)}) copy-start(s32[128]{0:T(128)} %param.9) | copy-start | bytes 1540
  20.1 5.2 %copy-start.1 = (bf16[128,1024]{1,0:T(8,128)(2,1)S(1)}, bf16[128,1024]{1,0:T(8,128)(2,1)}, u32[]{:S(2)}) copy-start(bf16[128,1024]{1,0:T(8,128)(2,1)} %rows_ref.1) | copy-start | bytes 786436
  20.1 14.8 %all-to-all-start.1 = ((bf16[8,32,1024]{2,1,0:T(8,128)(2,1)}), bf16[8,32,1024]{2,1,0:T(8,128)(2,1)S(1)}, u32[]{:S(2)}, u32[]{:S(2)}) async-start(bf16[8,32,1024]{2,1,0:T(8,128)(2,1)} %bitcast.10), calls=%async_computation.1 | async-start | bytes 1048576 | tf_op jit(solution)/shard_map/all_to_all | solution.py:22
  35.3 1.3 %collective-permute-start.1 = (f32[66,128]{1,0:T(8,128)S(1)}, f32[66,128]{1,0:T(8,128)S(1)}, u32[]{:S(2)}, u32[]{:S(2)}) collective-permute-start(f32[66,128]{1,0:T(8,128)S(1)} %pad_maximum_fusion.1), channel_id=1, source_target_pairs={{0,1},{1,0},{2,3},{3,2},{4,5},{5,4},{6,7},{7,6},{8,9},{9,8},{10,11... | collective-permute-start | bytes 101384 | tf_op jit(solution)/shard_map/ppermute | solution.py:43
  36.6 7.5 %collective-permute-start.2 = (f32[66,128]{1,0:T(8,128)S(1)}, f32[66,128]{1,0:T(8,128)S(1)}, u32[]{:S(2)}, u32[]{:S(2)}) collective-permute-start(f32[66,128]{1,0:T(8,128)S(1)} %fusion.23), channel_id=1, source_target_pairs={{0,2},{1,3},{2,0},{3,1},{4,6},{5,7},{6,4},{7,5},{8,10},{9,11},{10,... | collective-permute-start | bytes 101384 | tf_op jit(solution)/shard_map/ppermute | solution.py:43
  38.1 20.3 %all-to-all-start.2 = ((bf16[4,64,1024]{2,1,0:T(8,128)(2,1)}), bf16[4,64,1024]{2,1,0:T(8,128)(2,1)S(1)}, u32[]{:S(2)}, u32[]{:S(2)}) async-start(bf16[4,64,1024]{2,1,0:T(8,128)(2,1)} %bitcast.9), calls=%async_computation.2 | async-start | bytes 1048576 | tf_op jit(solution)/shard_map/all_to_all | solution.py:22
  44.1 4.0 %collective-permute-start.3 = (f32[66,128]{1,0:T(8,128)S(1)}, f32[66,128]{1,0:T(8,128)S(1)}, u32[]{:S(2)}, u32[]{:S(2)}) collective-permute-start(f32[66,128]{1,0:T(8,128)S(1)} %add.92.sums_ref), channel_id=1, source_target_pairs={{0,4},{4,0},{8,12},{12,8},{16,20},{20,16},{24,28},{28,24},{1,5},{5... | collective-permute-start | bytes 101384 | tf_op jit(solution)/shard_map/ppermute | solution.py:36
  49.3 5.5 %collective-permute-start.4 = (f32[8,1024]{1,0:T(8,128)S(1)}, f32[8,1024]{1,0:T(8,128)S(1)}, u32[]{:S(2)}, u32[]{:S(2)}) collective-permute-start(f32[8,1024]{1,0:T(8,128)S(1)} %get-tuple-element.30), channel_id=1, source_target_pairs={{0,8},{4,12},{8,0},{12,4},{16,24},{20,28},{24,16},{28,20},{1,9},{5... | collective-permute-start | bytes 98312 | tf_op jit(solution)/shard_map/ppermute | solution.py:68
  49.9 8.5 %collective-permute-start.5 = (f32[8,1024]{1,0:T(8,128)S(1)}, f32[8,1024]{1,0:T(8,128)S(1)}, u32[]{:S(2)}, u32[]{:S(2)}) collective-permute-start(f32[8,1024]{1,0:T(8,128)S(1)} %get-tuple-element.29), channel_id=1, source_target_pairs={{0,16},{4,20},{8,24},{12,28},{16,0},{20,4},{24,8},{28,12},{1,17},{... | collective-permute-start | bytes 98312 | tf_op jit(solution)/shard_map/ppermute | solution.py:68
  51.5 6.9 %collective-permute-start.6 = (f32[8,1024]{1,0:T(8,128)S(1)}, f32[8,1024]{1,0:T(8,128)S(1)}, u32[]{:S(2)}, u32[]{:S(2)}) collective-permute-start(f32[8,1024]{1,0:T(8,128)S(1)} %get-tuple-element.28), channel_id=1, source_target_pairs={{0,24},{4,28},{8,16},{12,20},{16,8},{20,12},{24,0},{28,4},{1,25},{... | collective-permute-start | bytes 98312 | tf_op jit(solution)/shard_map/ppermute | solution.py:68

commit v6 on v5

--- a/solution.py
+++ b/solution.py
@@ -11,7 +11,7 @@
 
 
 def line_order(lines):
-    return [2, 1, 3, 0] if lines == 4 else list(range(lines))
+    return [2, 0, 1, 3] if lines == 4 else list(range(lines))
 
 
 def peer_order(peers):
@@ -63,7 +63,7 @@
     order = line_order(lines)
     total = lax.dynamic_index_in_dim(x, place_of(order, line), 0, False)
     parts = []
-    for k in range(1, lines):
+    for k in range(lines - 1, 0, -1):
         part = lax.dynamic_index_in_dim(x, place_of(order, line ^ k), 0, False)
         parts.append(lax.ppermute(part, "dp", [(i, i ^ (2 * k)) for i in range(size)]))
     return [total] + parts
@@ -166,16 +166,16 @@
         top = jnp.maximum(
             jnp.max(scores, 0, keepdims=True), jnp.max(pos_or, 0, keepdims=True)
         )
-        mass = jnp.sum(jnp.exp(scores - top), 0, keepdims=True)
-        mass = mass + jnp.sum(jnp.exp(pos_or - top), 0, keepdims=True)
-        log_total = top + jnp.log(mass)
+        score_mass, pos_mass = jnp.exp(scores - top), jnp.exp(pos_or - top)
+        mass = jnp.sum(score_mass, 0, keepdims=True) + jnp.sum(pos_mass, 0, keepdims=True)
+        inv_mass = 1.0 / mass
         inv_count = 1.0 / counts_ref[...]
-        weights = jnp.exp(scores - log_total)
-        coeffs = jnp.where(asked, jnp.exp(pos_or - log_total) - inv_count, 0.0)
+        weights = score_mass * inv_mass
+        coeffs = jnp.where(asked, pos_mass * inv_mass - inv_count, 0.0)
         if base is None:
             losses_ref, weights_ref, hi_ref, lo_ref, sent_ref = refs
             own = jnp.sum(jnp.where(asked, pos, 0.0), 0, keepdims=True)
-            losses_ref[...] = log_total - own * inv_count
+            losses_ref[...] = top + jnp.log(mass) - own * inv_count
             weights_ref[...] = weights.astype(BF)
             hi = coeffs.astype(BF)
             hi_ref[...] = hi
@@ -187,15 +187,23 @@
         part = jnp.dot(near_w.astype(BF), rows_ref[...], preferred_element_type=F32)
         part = part.reshape(lines, pad, width)
         coeff = jnp.sum(coeffs, 1, keepdims=True)
-        down, lane = iota((places, places), 0), iota((places, places), 1)
-        left = jnp.where(down % cap == lane - source * cap, coeff, 0.0)
-        line, at = iota((lines, places), 0), iota((lines, places), 1) // cap
-        pick = (at == line + lines * where_ref[0]).astype(BF)
-        row = jnp.zeros((lines, places), F32)
-        for _ in range(3):
-            piece = left.astype(BF)
-            left = left - piece.astype(F32)
-            row = row + jnp.dot(pick, piece, preferred_element_type=F32)
+        if cap % 8 == 0 and 128 % cap == 0 and places % 128 == 0:
+            mid = places // 2
+            near_c = jnp.where(odd, coeff[mid:], coeff[:mid])
+            fits = iota((mid, 128), 0) % cap == iota((mid, 128), 1) % cap
+            left = jnp.where(fits, near_c, 0.0).reshape(lines, cap, 128)
+            row = jnp.concatenate([jnp.sum(left, 1)] * (places // 128), 1)
+            row = jnp.where(iota((lines, places), 1) // cap == source, row, 0.0)
+        else:
+            down, lane = iota((places, places), 0), iota((places, places), 1)
+            left = jnp.where(down % cap == lane - source * cap, coeff, 0.0)
+            line, at = iota((lines, places), 0), iota((lines, places), 1) // cap
+            pick = (at == line + lines * where_ref[0]).astype(BF)
+            row = jnp.zeros((lines, places), F32)
+            for _ in range(3):
+                piece = left.astype(BF)
+                left = left - piece.astype(F32)
+                row = row + jnp.dot(pick, piece, preferred_element_type=F32)
         if base is not None:
             part = part + base_ref[...]
             row = row + base_ref[:, pas, :places]

time: 60.3 us -> 59.7 us (0.990)
  starting transfers between devices: 27.4 us -> 25.1 us
  waiting for transfers between devices: 17.2 us -> 19.1 us
    all_to_all x3, starting transfers between devices: 17 us -> 14.7 us  [exchange(): lax.all_to_all(x, 'dp', split_axis=0, concat_axis=0, tiled=True, axis_ind...]
    all_to_all x3, waiting for transfers between devices: 11.6 us -> 13 us  [exchange(): lax.all_to_all(x, 'dp', split_axis=0, concat_axis=0, tiled=True, axis_ind...]
  transfers between devices with their start and end apart: 10 -> 10, of which waited for: 5 -> 6; matrix products, arithmetic and copies ran while one was open for 9% -> 9% of each run, Pallas kernels for 4% -> 4%
where the time goes in v6:
time: 59.7 us; the launch traced here: 59.2 us
  starting transfers between devices  25.1 us (42%)
  waiting for transfers between devices  19.1 us (32%)
  Pallas kernels  5.5 us (9%)
  matrix products  4.1 us (7%)
  local copies, waits for them, and re-layouts  2.41 us (4%)
  other arithmetic  2.13 us (4%)
  between operations  0.86 us (1%)
    all_to_all x3, starting transfers between devices, exchange(): lax.all_to_all(x, 'dp', split_axis=0, concat_axis=0, tiled=True, axis_ind...  14.7 us
    all_to_all x3, waiting for transfers between devices, exchange(): lax.all_to_all(x, 'dp', split_axis=0, concat_axis=0, tiled=True, axis_ind...  13 us
    pallas_call x4, Pallas kernels, call(): pl.pallas_call(kernel, out_shape=outs, cost_estimate=cost, **kw)(*args)  5.5 us
    ppermute x3, starting transfers between devices, scatter_sum(): lax.ppermute(part, 'dp', [(i, i ^ 2 * k) for i in range(size)])  4.45 us
    ppermute x2, starting transfers between devices, to_pair(): lax.ppermute(x, 'dp', [(i, i ^ 1) for i in range(lax.axis_size('dp'))])  4.37 us
    ppermute x3, waiting for transfers between devices, scatter_sum(): lax.ppermute(part, 'dp', [(i, i ^ 2 * k) for i in range(size)])  4.17 us
    dot_general x10, matrix products, dot(): lax.dot_general(a, b, (((ca,), (cb,)), ((), ())), preferred_element_type=...  4.1 us
    ppermute x2, starting transfers between devices, sub_sum(): x = x + lax.ppermute(x, 'sub', [(i, i ^ step) for i in range(size)])  1.59 us
  transfers between devices with their start and end apart: 10, of which 6 were waited for; matrix products, arithmetic and copies ran while one was open for 9% of the time, Pallas kernels for 4%

profile of v6, /device:TPU:0, one launch (start us, length us, event | category | flops | bytes accessed | tf_op | source)
XLA Modules:
  0.0 59.2 jit_solution(17730256773589559811)
XLA Ops:
  0.6 0.7 %convert_bitcast_fusion = (f32[1,128]{1,0:T(1,128)S(1)}, bf16[128]{0:T(256)(128)(2,1)S(1)}) fusion(s32[128]{0:T(128)} %param.9), kind=kLoop, calls=%fused_computation.58 | loop fusion | flops 256 | bytes 1280 | tf_op jit(solution)/shard_map/broadcast_in_dim | solution.py:356
  1.4 1.8 %plan.1 = (bf16[8,8,1024]{2,1,0:T(8,128)(2,1)}, f32[1,256]{1,0:T(1,128)}) custom-call(s32[16,128]{1,0:T(8,128)} %bitcast.57, bf16[6,1024]{1,0:T(8,128)(2,1)} %pas_ref.1), custom_call_target="tpu_custom_call" | custom-call | flops 10000000 | bytes 152576 | tf_op jit(solution)/shard_map/plan/pallas_call | solution.py:79
  3.2 0.7 %copy-done.2 = f32[1,256]{1,0:T(1,128)S(1)} copy-done((f32[1,256]{1,0:T(1,128)S(1)}, f32[1,256]{1,0:T(1,128)}, u32[]{:S(2)}) %copy-start.2) | copy-done | bytes 1048
  3.9 1.0 %fusion.4 = bf16[136,1024]{1,0:T(8,128)(2,1)S(1)} fusion(bf16[1,384]{1,0:T(2,128)(2,1)S(1)} %broadcast_in_dim.7, bf16[128,1024]{1,0:T(8,128)(2,1)} %rows_ref.1), kind=kLoop, calls=%fused_computation.13 | loop fusion | flops 835584 | bytes 541440 | tf_op jit(solution)/shard_map/concatenate | solution.py:324
  4.9 3.0 %collective-permute-start = (bf16[136,1024]{1,0:T(8,128)(2,1)S(1)}, bf16[136,1024]{1,0:T(8,128)(2,1)S(1)}, u32[]{:S(2)}, u32[]{:S(2)}) collective-permute-start(bf16[136,1024]{1,0:T(8,128)(2,1)S(1)} %fusion.4), channel_id=1, source_target_pairs={{0,4},{4,0},{8,12},{12,8},{16,20},{20,16},{24,28},{28,24},{1,5},{5... | collective-permute-start | bytes 835592 | tf_op jit(solution)/shard_map/ppermute | solution.py:36
  8.0 5.9 %all-to-all-start = ((bf16[8,8,1024]{2,1,0:T(8,128)(2,1)}), bf16[8,8,1024]{2,1,0:T(8,128)(2,1)S(1)}, u32[]{:S(2)}, u32[]{:S(2)}) async-start(bf16[8,8,1024]{2,1,0:T(8,128)(2,1)} %get-tuple-element.15), calls=%async_computation | async-start | bytes 262144 | tf_op jit(solution)/shard_map/all_to_all | solution.py:22
  14.1 0.7 %copy-done.3 = s32[128]{0:T(128)S(1)} copy-done((s32[128]{0:T(128)S(1)}, s32[128]{0:T(128)}, u32[]{:S(2)}) %copy-start.3) | copy-done | bytes 536
  14.7 3.9 %all-to-all-done = bf16[8,8,1024]{2,1,0:T(8,128)(2,1)S(1)} async-done(((bf16[8,8,1024]{2,1,0:T(8,128)(2,1)}), bf16[8,8,1024]{2,1,0:T(8,128)(2,1)S(1)}, u32[]{:S(2)}, u32[]{:S(2)}) %all-to-all-start) | async-done | bytes 131104 | tf_op jit(solution)/shard_map/all_to_all | solution.py:22
  18.8 1.1 %convolution_convert_fusion = bf16[256,1024]{1,0:T(8,128)(2,1)} fusion(bf16[256,1024]{1,0:T(8,128)(2,1)S(1)} %copy-done, f32[256]{0:T(256)S(1)} %iota_convert_fusion, f32[256]{0:T(256)S(1)} %reshape.172), kind=kOutput, calls=%fused_computation | convolution fusion | flops 134545408 | bytes 1050624 | tf_op jit(solution)/shard_map/dot_general | solution.py:32
  19.9 4.6 %all-to-all-start.1 = ((bf16[8,32,1024]{2,1,0:T(8,128)(2,1)}), bf16[8,32,1024]{2,1,0:T(8,128)(2,1)S(1)}, u32[]{:S(2)}, u32[]{:S(2)}) async-start(bf16[8,32,1024]{2,1,0:T(8,128)(2,1)} %bitcast.10), calls=%async_computation.1 | async-start | bytes 1048576 | tf_op jit(solution)/shard_map/all_to_all | solution.py:22
  24.5 0.2 fusion.7
  25.3 0.2 convolution_convert_fusion.1
  25.5 0.2 broadcast_select_fusion.1
  25.8 0.8 %copy.10 = bf16[4,2,32,1024]{3,2,1,0:T(8,128)(2,1)} copy(bf16[4,2,32,1024]{3,2,0,1:T(8,128)(2,1)S(1)} %pad_maximum_fusion) | data formatting | bytes 1048576 | tf_op jit(solution)/shard_map/concatenate | solution.py:344
  26.6 9.1 %all-to-all-done.1 = bf16[8,32,1024]{2,1,0:T(8,128)(2,1)S(1)} async-done(((bf16[8,32,1024]{2,1,0:T(8,128)(2,1)}), bf16[8,32,1024]{2,1,0:T(8,128)(2,1)S(1)}, u32[]{:S(2)}, u32[]{:S(2)}) %all-to-all-start.1) | async-done | bytes 524320 | tf_op jit(solution)/shard_map/all_to_all | solution.py:22
  35.7 0.4 fusion.2
  36.3 1.1 %collective-permute-done.1 = f32[66,128]{1,0:T(8,128)S(1)} collective-permute-done((f32[66,128]{1,0:T(8,128)S(1)}, f32[66,128]{1,0:T(8,128)S(1)}, u32[]{:S(2)}, u32[]{:S(2)}) %collective-permute-start.1) | collective-permute-done | bytes 33824 | tf_op jit(solution)/shard_map/ppermute | solution.py:43
  37.4 1.5 %collective-permute-start.2 = (f32[66,128]{1,0:T(8,128)S(1)}, f32[66,128]{1,0:T(8,128)S(1)}, u32[]{:S(2)}, u32[]{:S(2)}) collective-permute-start(f32[66,128]{1,0:T(8,128)S(1)} %fusion.23), channel_id=1, source_target_pairs={{0,2},{1,3},{2,0},{3,1},{4,6},{5,7},{6,4},{7,5},{8,10},{9,11},{10,... | collective-permute-start | bytes 101384 | tf_op jit(solution)/shard_map/ppermute | solution.py:43
  39.0 4.2 %all-to-all-start.2 = ((bf16[4,64,1024]{2,1,0:T(8,128)(2,1)}), bf16[4,64,1024]{2,1,0:T(8,128)(2,1)S(1)}, u32[]{:S(2)}, u32[]{:S(2)}) async-start(bf16[4,64,1024]{2,1,0:T(8,128)(2,1)} %bitcast.9), calls=%async_computation.2 | async-start | bytes 1048576 | tf_op jit(solution)/shard_map/all_to_all | solution.py:22
  43.2 1.3 %collective-permute-start.3 = (f32[66,128]{1,0:T(8,128)S(1)}, f32[66,128]{1,0:T(8,128)S(1)}, u32[]{:S(2)}, u32[]{:S(2)}) collective-permute-start(f32[66,128]{1,0:T(8,128)S(1)} %add.92.sums_ref), channel_id=1, source_target_pairs={{0,4},{4,0},{8,12},{12,8},{16,20},{20,16},{24,28},{28,24},{1,5},{5... | collective-permute-start | bytes 101384 | tf_op jit(solution)/shard_map/ppermute | solution.py:36
  44.5 1.4 %soften.1 = (f32[1,128]{1,0:T(1,128)}, bf16[64,128]{1,0:T(8,128)(2,1)S(1)}, bf16[256,128]{1,0:T(8,128)(2,1)S(1)}, bf16[256,128]{1,0:T(8,128)(2,1)S(1)}, f32[4,8,1024]{2,1,0:T(8,128)S(1)}) custom-call(s32[2]{0:T(128)S(1)} %pad_add_fusion.4.where_ref, f32[66,128]{1,0:T(8,128)S(1)} %add.92.sums_ref, bf16[256,128]{1,0:T(8,128)(2,1)S(1)} %convolution_convert_fusion.4.asks_ref, ...), custom_call_target="tpu_custom_call" | custom-call | flops 10000000 | bytes 641032 | tf_op jit(solution)/shard_map/soften/pallas_call | solution.py:79
  45.9 0.2 fusion.26
  46.2 0.3 fusion.25
  46.4 0.8 %collective-permute-done.3.sums_ref = f32[66,128]{1,0:T(8,128)S(1)} collective-permute-done((f32[66,128]{1,0:T(8,128)S(1)}, f32[66,128]{1,0:T(8,128)S(1)}, u32[]{:S(2)}, u32[]{:S(2)}) %collective-permute-start.3) | collective-permute-done | bytes 33824 | tf_op jit(solution)/shard_map/ppermute | solution.py:36
  47.2 1.0 %soften_pair.1 = f32[4,8,1024]{2,1,0:T(8,128)S(1)} custom-call(s32[2]{0:T(128)S(1)} %pad_add_fusion.5.where_ref, f32[66,128]{1,0:T(8,128)S(1)} %collective-permute-done.3.sums_ref, bf16[256,128]{1,0:T(8,128)(2,1)S(1)} %convolution_convert_fusion.3.asks_ref, f32[1,128]{1,0:T(1,128)S(1)} %fusion.19.counts_ref, bf16[128,1024]{1,0:T(8,128)(2,1)S(1)} %slice.36.rows_ref, ...), custom_call_target="tpu_custom_call" | custom-call | flops 10000000 | bytes 624136 | tf_op jit(solution)/shard_map/soften_pair/pallas_call | solution.py:79
  48.2 1.7 %collective-permute-start.4 = (f32[8,1024]{1,0:T(8,128)S(1)}, f32[8,1024]{1,0:T(8,128)S(1)}, u32[]{:S(2)}, u32[]{:S(2)}) collective-permute-start(f32[8,1024]{1,0:T(8,128)S(1)} %get-tuple-element.30), channel_id=1, source_target_pairs={{0,24},{4,28},{8,16},{12,20},{16,8},{20,12},{24,0},{28,4},{1,25},{... | collective-permute-start | bytes 98312 | tf_op jit(solution)/shard_map/ppermute | solution.py:68
  49.9 0.4 collective-permute-start.5
  50.3 2.4 %collective-permute-start.6 = (f32[8,1024]{1,0:T(8,128)S(1)}, f32[8,1024]{1,0:T(8,128)S(1)}, u32[]{:S(2)}, u32[]{:S(2)}) collective-permute-start(f32[8,1024]{1,0:T(8,128)S(1)} %get-tuple-element.28), channel_id=1, source_target_pairs={{0,8},{4,12},{8,0},{12,4},{16,24},{20,28},{24,16},{28,20},{1,9},{5... | collective-permute-start | bytes 98312 | tf_op jit(solution)/shard_map/ppermute | solution.py:68
  52.7 1.0 %fusion.1 = f32[128,1024]{1,0:T(8,128)} fusion(f32[128,1024]{1,0:T(8,128)S(1)} %fusion.26, f32[128,1024]{1,0:T(8,128)S(1)} %fusion.25, bf16[64,128]{1,0:T(8,128)(2,1)S(1)} %get-tuple-element.19, bf16[8,8,1024]{2,1,0:T(8,128)(2,1)S(1)} %all-to-all-done), kind=kOutput, calls=%fused_computation.3 | convolution fusion | flops 17170432 | bytes 1720320 | tf_op jit(solution)/shard_map/dot_general | solution.py:32
  53.7 1.9 %collective-permute-done.4.refs_1_ = f32[8,1024]{1,0:T(8,128)S(1)} collective-permute-done((f32[8,1024]{1,0:T(8,128)S(1)}, f32[8,1024]{1,0:T(8,128)S(1)}, u32[]{:S(2)}, u32[]{:S(2)}) %collective-permute-start.4) | collective-permute-done | bytes 32800 | tf_op jit(solution)/shard_map/ppermute | solution.py:68
  55.6 2.3 %collective-permute-done.5.refs_2_ = f32[8,1024]{1,0:T(8,128)S(1)} collective-permute-done((f32[8,1024]{1,0:T(8,128)S(1)}, f32[8,1024]{1,0:T(8,128)S(1)}, u32[]{:S(2)}, u32[]{:S(2)}) %collective-permute-start.5) | collective-permute-done | bytes 32800 | tf_op jit(solution)/shard_map/ppermute | solution.py:68
  57.9 1.3 %close.1 = (f32[6,1024]{1,0:T(8,128)}, f32[256,1024]{1,0:T(8,128)}) custom-call(f32[8,1024]{1,0:T(8,128)S(1)} %get-tuple-element.31.refs_0_, f32[8,1024]{1,0:T(8,128)S(1)} %collective-permute-done.4.refs_1_, f32[8,1024]{1,0:T(8,128)S(1)} %collective-permute-done.5.refs_2_, f32[8,1024]{1,0:T(8,128)S(1)} %collective-permute-done.6.refs_3_, ...), custom_call_target="tpu_custom_call" | custom-call | flops 268435456 | bytes 1729536 | tf_op jit(solution)/shard_map/close/pallas_call | solution.py:79
  (38 shorter events, 1.1 us)
Async XLA Ops:
  0.6 18.1 %copy-start = (bf16[256,1024]{1,0:T(8,128)(2,1)S(1)}, bf16[256,1024]{1,0:T(8,128)(2,1)}, u32[]{:S(2)}) copy-start(bf16[256,1024]{1,0:T(8,128)(2,1)} %param.7) | copy-start | bytes 1572868
  3.2 0.7 %copy-start.2 = (f32[1,256]{1,0:T(1,128)S(1)}, f32[1,256]{1,0:T(1,128)}, u32[]{:S(2)}) copy-start(f32[1,256]{1,0:T(1,128)} %get-tuple-element.16) | copy-start | bytes 3076
  4.9 19.8 %collective-permute-start = (bf16[136,1024]{1,0:T(8,128)(2,1)S(1)}, bf16[136,1024]{1,0:T(8,128)(2,1)S(1)}, u32[]{:S(2)}, u32[]{:S(2)}) collective-permute-start(bf16[136,1024]{1,0:T(8,128)(2,1)S(1)} %fusion.4), channel_id=1, source_target_pairs={{0,4},{4,0},{8,12},{12,8},{16,20},{20,16},{24,28},{28,24},{1,5},{5... | collective-permute-start | bytes 835592 | tf_op jit(solution)/shard_map/ppermute | solution.py:36
  8.0 10.7 %all-to-all-start = ((bf16[8,8,1024]{2,1,0:T(8,128)(2,1)}), bf16[8,8,1024]{2,1,0:T(8,128)(2,1)S(1)}, u32[]{:S(2)}, u32[]{:S(2)}) async-start(bf16[8,8,1024]{2,1,0:T(8,128)(2,1)} %get-tuple-element.15), calls=%async_computation | async-start | bytes 262144 | tf_op jit(solution)/shard_map/all_to_all | solution.py:22
  14.1 0.7 %copy-start.3 = (s32[128]{0:T(128)S(1)}, s32[128]{0:T(128)}, u32[]{:S(2)}) copy-start(s32[128]{0:T(128)} %param.9) | copy-start | bytes 1540
  19.9 4.6 %copy-start.1 = (bf16[128,1024]{1,0:T(8,128)(2,1)S(1)}, bf16[128,1024]{1,0:T(8,128)(2,1)}, u32[]{:S(2)}) copy-start(bf16[128,1024]{1,0:T(8,128)(2,1)} %rows_ref.1) | copy-start | bytes 786436
  19.9 15.8 %all-to-all-start.1 = ((bf16[8,32,1024]{2,1,0:T(8,128)(2,1)}), bf16[8,32,1024]{2,1,0:T(8,128)(2,1)S(1)}, u32[]{:S(2)}, u32[]{:S(2)}) async-start(bf16[8,32,1024]{2,1,0:T(8,128)(2,1)} %bitcast.10), calls=%async_computation.1 | async-start | bytes 1048576 | tf_op jit(solution)/shard_map/all_to_all | solution.py:22
  36.1 1.3 %collective-permute-start.1 = (f32[66,128]{1,0:T(8,128)S(1)}, f32[66,128]{1,0:T(8,128)S(1)}, u32[]{:S(2)}, u32[]{:S(2)}) collective-permute-start(f32[66,128]{1,0:T(8,128)S(1)} %pad_maximum_fusion.1), channel_id=1, source_target_pairs={{0,1},{1,0},{2,3},{3,2},{4,5},{5,4},{6,7},{7,6},{8,9},{9,8},{10,11... | collective-permute-start | bytes 101384 | tf_op jit(solution)/shard_map/ppermute | solution.py:43
  37.4 5.8 %collective-permute-start.2 = (f32[66,128]{1,0:T(8,128)S(1)}, f32[66,128]{1,0:T(8,128)S(1)}, u32[]{:S(2)}, u32[]{:S(2)}) collective-permute-start(f32[66,128]{1,0:T(8,128)S(1)} %fusion.23), channel_id=1, source_target_pairs={{0,2},{1,3},{2,0},{3,1},{4,6},{5,7},{6,4},{7,5},{8,10},{9,11},{10,... | collective-permute-start | bytes 101384 | tf_op jit(solution)/shard_map/ppermute | solution.py:43
  39.0 18.9 %all-to-all-start.2 = ((bf16[4,64,1024]{2,1,0:T(8,128)(2,1)}), bf16[4,64,1024]{2,1,0:T(8,128)(2,1)S(1)}, u32[]{:S(2)}, u32[]{:S(2)}) async-start(bf16[4,64,1024]{2,1,0:T(8,128)(2,1)} %bitcast.9), calls=%async_computation.2 | async-start | bytes 1048576 | tf_op jit(solution)/shard_map/all_to_all | solution.py:22
  43.2 4.0 %collective-permute-start.3 = (f32[66,128]{1,0:T(8,128)S(1)}, f32[66,128]{1,0:T(8,128)S(1)}, u32[]{:S(2)}, u32[]{:S(2)}) collective-permute-start(f32[66,128]{1,0:T(8,128)S(1)} %add.92.sums_ref), channel_id=1, source_target_pairs={{0,4},{4,0},{8,12},{12,8},{16,20},{20,16},{24,28},{28,24},{1,5},{5... | collective-permute-start | bytes 101384 | tf_op jit(solution)/shard_map/ppermute | solution.py:36
  48.2 7.4 %collective-permute-start.4 = (f32[8,1024]{1,0:T(8,128)S(1)}, f32[8,1024]{1,0:T(8,128)S(1)}, u32[]{:S(2)}, u32[]{:S(2)}) collective-permute-start(f32[8,1024]{1,0:T(8,128)S(1)} %get-tuple-element.30), channel_id=1, source_target_pairs={{0,24},{4,28},{8,16},{12,20},{16,8},{20,12},{24,0},{28,4},{1,25},{... | collective-permute-start | bytes 98312 | tf_op jit(solution)/shard_map/ppermute | solution.py:68
  49.9 8.0 %collective-permute-start.5 = (f32[8,1024]{1,0:T(8,128)S(1)}, f32[8,1024]{1,0:T(8,128)S(1)}, u32[]{:S(2)}, u32[]{:S(2)}) collective-permute-start(f32[8,1024]{1,0:T(8,128)S(1)} %get-tuple-element.29), channel_id=1, source_target_pairs={{0,16},{4,20},{8,24},{12,28},{16,0},{20,4},{24,8},{28,12},{1,17},{... | collective-permute-start | bytes 98312 | tf_op jit(solution)/shard_map/ppermute | solution.py:68
  50.3 7.6 %collective-permute-start.6 = (f32[8,1024]{1,0:T(8,128)S(1)}, f32[8,1024]{1,0:T(8,128)S(1)}, u32[]{:S(2)}, u32[]{:S(2)}) collective-permute-start(f32[8,1024]{1,0:T(8,128)S(1)} %get-tuple-element.28), channel_id=1, source_target_pairs={{0,8},{4,12},{8,0},{12,4},{16,24},{20,28},{24,16},{28,20},{1,9},{5... | collective-permute-start | bytes 98312 | tf_op jit(solution)/shard_map/ppermute | solution.py:68

commit v7 on v6

--- a/solution.py
+++ b/solution.py
@@ -63,7 +63,7 @@
     order = line_order(lines)
     total = lax.dynamic_index_in_dim(x, place_of(order, line), 0, False)
     parts = []
-    for k in range(lines - 1, 0, -1):
+    for k in ([3, 1, 2] if lines == 4 else range(1, lines)):
         part = lax.dynamic_index_in_dim(x, place_of(order, line ^ k), 0, False)
         parts.append(lax.ppermute(part, "dp", [(i, i ^ (2 * k)) for i in range(size)]))
     return [total] + parts
@@ -139,6 +139,40 @@
         name="plan",
     )
     return block, place[0].astype(jnp.int32)
+
+
+def serve(wanted, bank):
+    places = wanted.shape[0]
+    bank_rows, width = bank.shape
+    steps = 2
+    cols = width // steps
+
+    def kernel(wanted_ref, bank_ref, out, vmem, sems):
+        down, along = iota((places, places), 0), iota((places, places), 1)
+        want = jnp.sum(jnp.where(down == along, wanted_ref[...], 0.0), 1, keepdims=True)
+        pick = (want == iota((places, bank_rows), 1).astype(F32)).astype(BF)
+        copies = []
+        for i in range(steps):
+            at = pl.ds(i * cols, cols)
+            rows = jnp.dot(pick, bank_ref[:, at], preferred_element_type=F32)
+            vmem[:, at] = rows.astype(BF)
+            copies.append(pltpu.make_async_copy(vmem.at[:, at], out.at[:, at], sems.at[i]))
+            copies[-1].start()
+        for copy in copies:
+            copy.wait()
+
+    return call(
+        kernel,
+        (jax.ShapeDtypeStruct((places, width), BF),),
+        2 * places * bank_rows * width,
+        wanted[None, :],
+        bank,
+        in_specs=[VMEM, VMEM],
+        out_specs=(pl.BlockSpec(memory_space=pl.ANY),),
+        scratch_shapes=[pltpu.VMEM((places, width), BF), pltpu.SemaphoreType.DMA((steps,))],
+        compiler_params=ROOMY,
+        name="serve",
+    )[0]
 
 
 def soften(sums, asks, counts, rows, where, pas, base=None):
@@ -332,8 +366,7 @@
 
     all_pas = heads.reshape(peers * pad, width)
     wanted = heads[:, pas, :cap].astype(F32).reshape(-1)
-    pick = (wanted[:, None] == jnp.arange(bank_rows).astype(F32)[None, :]).astype(BF)
-    picked = dot(pick, bank, 1, 0).astype(BF)
+    picked = serve(wanted, bank)
     fetched = exchange(picked.reshape(peers, cap, width), everyone()).reshape(places, width)
 
     send = []

time: 59.7 us -> 59.8 us (level)
  matrix products: 4.1 us -> 2.94 us
  Pallas kernels: 5.5 us -> 6.59 us
  other arithmetic: 2.13 us -> 2.87 us
  waiting for transfers between devices: 19.1 us -> 18.5 us
    dot_general x10 -> x9, matrix products: 4.1 us -> 2.94 us  [dot(): lax.dot_general(a, b, (((ca,), (cb,)), ((), ())), preferred_element_type=...]
    pallas_call x4 -> x5, Pallas kernels: 5.5 us -> 6.59 us  [call(): pl.pallas_call(kernel, out_shape=outs, cost_estimate=cost, **kw)(*args)]
    convert_element_type x1, other arithmetic: 0.02 us -> 0.76 us  [body(): notes = jnp.concatenate([place.astype(BF), counts.astype(BF)])]
  transfers between devices with their start and end apart: 10 -> 10, of which waited for: 6 -> 6; matrix products, arithmetic and copies ran while one was open for 9% -> 7% of each run, Pallas kernels for 4% -> 6%
where the time goes in v7:
time: 59.8 us; the launch traced here: 59.2 us
  starting transfers between devices  25.1 us (42%)
  waiting for transfers between devices  18.5 us (31%)
  Pallas kernels  6.59 us (11%)
  matrix products  2.94 us (5%)
  other arithmetic  2.87 us (5%)
  local copies, waits for them, and re-layouts  2.33 us (4%)
  between operations  0.87 us (1%)
    all_to_all x3, starting transfers between devices, exchange(): lax.all_to_all(x, 'dp', split_axis=0, concat_axis=0, tiled=True, axis_ind...  14.7 us
    all_to_all x3, waiting for transfers between devices, exchange(): lax.all_to_all(x, 'dp', split_axis=0, concat_axis=0, tiled=True, axis_ind...  12.4 us
    pallas_call x5, Pallas kernels, call(): pl.pallas_call(kernel, out_shape=outs, cost_estimate=cost, **kw)(*args)  6.59 us
    ppermute x3, starting transfers between devices, scatter_sum(): lax.ppermute(part, 'dp', [(i, i ^ 2 * k) for i in range(size)])  4.45 us
    ppermute x2, starting transfers between devices, to_pair(): lax.ppermute(x, 'dp', [(i, i ^ 1) for i in range(lax.axis_size('dp'))])  4.36 us
    ppermute x3, waiting for transfers between devices, scatter_sum(): lax.ppermute(part, 'dp', [(i, i ^ 2 * k) for i in range(size)])  4.17 us
    dot_general x9, matrix products, dot(): lax.dot_general(a, b, (((ca,), (cb,)), ((), ())), preferred_element_type=...  2.94 us
    ppermute x2, starting transfers between devices, sub_sum(): x = x + lax.ppermute(x, 'sub', [(i, i ^ step) for i in range(size)])  1.59 us
  transfers between devices with their start and end apart: 10, of which 6 were waited for; matrix products, arithmetic and copies ran while one was open for 7% of the time, Pallas kernels for 6%

profile of v7, /device:TPU:0, one launch (start us, length us, event | category | flops | bytes accessed | tf_op | source)
XLA Modules:
  0.0 59.2 jit_solution(14398500468833055364)
XLA Ops:
  0.6 0.7 %convert_bitcast_fusion = (f32[1,128]{1,0:T(1,128)S(1)}, bf16[128]{0:T(256)(128)(2,1)S(1)}) fusion(s32[128]{0:T(128)} %param.9), kind=kLoop, calls=%fused_computation.53 | loop fusion | flops 256 | bytes 1280 | tf_op jit(solution)/shard_map/broadcast_in_dim | solution.py:389
  1.4 1.8 %plan.1 = (bf16[8,8,1024]{2,1,0:T(8,128)(2,1)}, f32[1,256]{1,0:T(1,128)}) custom-call(s32[16,128]{1,0:T(8,128)} %bitcast.56, bf16[6,1024]{1,0:T(8,128)(2,1)} %pas_ref.1), custom_call_target="tpu_custom_call" | custom-call | flops 10000000 | bytes 152576 | tf_op jit(solution)/shard_map/plan/pallas_call | solution.py:79
  3.2 0.8 %convert_reduce_fusion = bf16[256]{0:T(256)(128)(2,1)S(1)} fusion(f32[1,256]{1,0:T(1,128)} %get-tuple-element.16), kind=kLoop, calls=%fused_computation.46 | loop fusion | flops 512 | bytes 1536 | tf_op jit(solution)/shard_map/convert_element_type | solution.py:356
  4.0 1.0 %fusion.4 = bf16[136,1024]{1,0:T(8,128)(2,1)S(1)} fusion(bf16[1,384]{1,0:T(2,128)(2,1)S(1)} %broadcast_in_dim.7, bf16[128,1024]{1,0:T(8,128)(2,1)} %rows_ref.1), kind=kLoop, calls=%fused_computation.12 | loop fusion | flops 835584 | bytes 541440 | tf_op jit(solution)/shard_map/concatenate | solution.py:358
  5.0 3.0 %collective-permute-start = (bf16[136,1024]{1,0:T(8,128)(2,1)S(1)}, bf16[136,1024]{1,0:T(8,128)(2,1)S(1)}, u32[]{:S(2)}, u32[]{:S(2)}) collective-permute-start(bf16[136,1024]{1,0:T(8,128)(2,1)S(1)} %fusion.4), channel_id=1, source_target_pairs={{0,4},{4,0},{8,12},{12,8},{16,20},{20,16},{24,28},{28,24},{1,5},{5... | collective-permute-start | bytes 835592 | tf_op jit(solution)/shard_map/ppermute | solution.py:36
  8.0 5.9 %all-to-all-start = ((bf16[8,8,1024]{2,1,0:T(8,128)(2,1)}), bf16[8,8,1024]{2,1,0:T(8,128)(2,1)S(1)}, u32[]{:S(2)}, u32[]{:S(2)}) async-start(bf16[8,8,1024]{2,1,0:T(8,128)(2,1)} %get-tuple-element.15), calls=%async_computation | async-start | bytes 262144 | tf_op jit(solution)/shard_map/all_to_all | solution.py:22
  14.1 0.6 %copy-done.2 = f32[1,256]{1,0:T(1,128)S(1)} copy-done((f32[1,256]{1,0:T(1,128)S(1)}, f32[1,256]{1,0:T(1,128)}, u32[]{:S(2)}) %copy-start.2) | copy-done | bytes 1048
  14.7 0.7 %copy-done.3 = s32[128]{0:T(128)S(1)} copy-done((s32[128]{0:T(128)S(1)}, s32[128]{0:T(128)}, u32[]{:S(2)}) %copy-start.3) | copy-done | bytes 536
  15.4 3.3 %all-to-all-done = bf16[8,8,1024]{2,1,0:T(8,128)(2,1)S(1)} async-done(((bf16[8,8,1024]{2,1,0:T(8,128)(2,1)}), bf16[8,8,1024]{2,1,0:T(8,128)(2,1)S(1)}, u32[]{:S(2)}, u32[]{:S(2)}) %all-to-all-start) | async-done | bytes 131104 | tf_op jit(solution)/shard_map/all_to_all | solution.py:22
  18.8 1.1 %serve.1 = bf16[256,1024]{1,0:T(8,128)(2,1)} custom-call(f32[1,256]{1,0:T(1,128)S(1)} %reshape.173.wanted_ref, bf16[256,1024]{1,0:T(8,128)(2,1)S(1)} %copy-done.1), custom_call_target="tpu_custom_call" | custom-call | flops 134217728 | bytes 1049600 | tf_op jit(solution)/shard_map/serve/pallas_call | solution.py:79
  19.9 4.6 %all-to-all-start.1 = ((bf16[8,32,1024]{2,1,0:T(8,128)(2,1)}), bf16[8,32,1024]{2,1,0:T(8,128)(2,1)S(1)}, u32[]{:S(2)}, u32[]{:S(2)}) async-start(bf16[8,32,1024]{2,1,0:T(8,128)(2,1)} %bitcast.10), calls=%async_computation.1 | async-start | bytes 1048576 | tf_op jit(solution)/shard_map/all_to_all | solution.py:22
  24.6 0.2 fusion.6
  25.3 0.2 convolution_convert_fusion
  25.5 0.2 broadcast_select_fusion.1
  25.8 0.8 %copy.10 = bf16[4,2,32,1024]{3,2,1,0:T(8,128)(2,1)} copy(bf16[4,2,32,1024]{3,2,0,1:T(8,128)(2,1)S(1)} %pad_maximum_fusion) | data formatting | bytes 1048576 | tf_op jit(solution)/shard_map/concatenate | solution.py:377
  26.7 9.1 %all-to-all-done.1 = bf16[8,32,1024]{2,1,0:T(8,128)(2,1)S(1)} async-done(((bf16[8,32,1024]{2,1,0:T(8,128)(2,1)}), bf16[8,32,1024]{2,1,0:T(8,128)(2,1)S(1)}, u32[]{:S(2)}, u32[]{:S(2)}) %all-to-all-start.1) | async-done | bytes 524320 | tf_op jit(solution)/shard_map/all_to_all | solution.py:22
  35.8 0.4 fusion.2
  36.3 1.1 %collective-permute-done.1 = f32[66,128]{1,0:T(8,128)S(1)} collective-permute-done((f32[66,128]{1,0:T(8,128)S(1)}, f32[66,128]{1,0:T(8,128)S(1)}, u32[]{:S(2)}, u32[]{:S(2)}) %collective-permute-start.1) | collective-permute-done | bytes 33824 | tf_op jit(solution)/shard_map/ppermute | solution.py:43
  37.4 1.5 %collective-permute-start.2 = (f32[66,128]{1,0:T(8,128)S(1)}, f32[66,128]{1,0:T(8,128)S(1)}, u32[]{:S(2)}, u32[]{:S(2)}) collective-permute-start(f32[66,128]{1,0:T(8,128)S(1)} %fusion.20), channel_id=1, source_target_pairs={{0,2},{1,3},{2,0},{3,1},{4,6},{5,7},{6,4},{7,5},{8,10},{9,11},{10,... | collective-permute-start | bytes 101384 | tf_op jit(solution)/shard_map/ppermute | solution.py:43
  39.0 4.2 %all-to-all-start.2 = ((bf16[4,64,1024]{2,1,0:T(8,128)(2,1)}), bf16[4,64,1024]{2,1,0:T(8,128)(2,1)S(1)}, u32[]{:S(2)}, u32[]{:S(2)}) async-start(bf16[4,64,1024]{2,1,0:T(8,128)(2,1)} %bitcast.9), calls=%async_computation.2 | async-start | bytes 1048576 | tf_op jit(solution)/shard_map/all_to_all | solution.py:22
  43.2 1.3 %collective-permute-start.3 = (f32[66,128]{1,0:T(8,128)S(1)}, f32[66,128]{1,0:T(8,128)S(1)}, u32[]{:S(2)}, u32[]{:S(2)}) collective-permute-start(f32[66,128]{1,0:T(8,128)S(1)} %add.92.sums_ref), channel_id=1, source_target_pairs={{0,4},{4,0},{8,12},{12,8},{16,20},{20,16},{24,28},{28,24},{1,5},{5... | collective-permute-start | bytes 101384 | tf_op jit(solution)/shard_map/ppermute | solution.py:36
  44.5 1.4 %soften.1 = (f32[1,128]{1,0:T(1,128)}, bf16[64,128]{1,0:T(8,128)(2,1)S(1)}, bf16[256,128]{1,0:T(8,128)(2,1)S(1)}, bf16[256,128]{1,0:T(8,128)(2,1)S(1)}, f32[4,8,1024]{2,1,0:T(8,128)S(1)}) custom-call(s32[2]{0:T(128)S(1)} %pad_add_fusion.4.where_ref, f32[66,128]{1,0:T(8,128)S(1)} %add.92.sums_ref, bf16[256,128]{1,0:T(8,128)(2,1)S(1)} %convolution_convert_fusion.3.asks_ref, ...), custom_call_target="tpu_custom_call" | custom-call | flops 10000000 | bytes 641032 | tf_op jit(solution)/shard_map/soften/pallas_call | solution.py:79
  45.9 0.2 fusion.23
  46.2 0.3 fusion.22
  46.4 0.8 %collective-permute-done.3.sums_ref = f32[66,128]{1,0:T(8,128)S(1)} collective-permute-done((f32[66,128]{1,0:T(8,128)S(1)}, f32[66,128]{1,0:T(8,128)S(1)}, u32[]{:S(2)}, u32[]{:S(2)}) %collective-permute-start.3) | collective-permute-done | bytes 33824 | tf_op jit(solution)/shard_map/ppermute | solution.py:36
  47.2 1.0 %soften_pair.1 = f32[4,8,1024]{2,1,0:T(8,128)S(1)} custom-call(s32[2]{0:T(128)S(1)} %pad_add_fusion.5.where_ref, f32[66,128]{1,0:T(8,128)S(1)} %collective-permute-done.3.sums_ref, bf16[256,128]{1,0:T(8,128)(2,1)S(1)} %convolution_convert_fusion.2.asks_ref, f32[1,128]{1,0:T(1,128)S(1)} %fusion.16.counts_ref, bf16[128,1024]{1,0:T(8,128)(2,1)S(1)} %slice.36.rows_ref, ...), custom_call_target="tpu_custom_call" | custom-call | flops 10000000 | bytes 624136 | tf_op jit(solution)/shard_map/soften_pair/pallas_call | solution.py:79
  48.2 1.7 %collective-permute-start.4 = (f32[8,1024]{1,0:T(8,128)S(1)}, f32[8,1024]{1,0:T(8,128)S(1)}, u32[]{:S(2)}, u32[]{:S(2)}) collective-permute-start(f32[8,1024]{1,0:T(8,128)S(1)} %get-tuple-element.30), channel_id=1, source_target_pairs={{0,24},{4,28},{8,16},{12,20},{16,8},{20,12},{24,0},{28,4},{1,25},{... | collective-permute-start | bytes 98312 | tf_op jit(solution)/shard_map/ppermute | solution.py:68
  50.0 2.7 %collective-permute-start.6 = (f32[8,1024]{1,0:T(8,128)S(1)}, f32[8,1024]{1,0:T(8,128)S(1)}, u32[]{:S(2)}, u32[]{:S(2)}) collective-permute-start(f32[8,1024]{1,0:T(8,128)S(1)} %get-tuple-element.28), channel_id=1, source_target_pairs={{0,16},{4,20},{8,24},{12,28},{16,0},{20,4},{24,8},{28,12},{1,17},{... | collective-permute-start | bytes 98312 | tf_op jit(solution)/shard_map/ppermute | solution.py:68
  52.7 1.0 %fusion.1 = f32[128,1024]{1,0:T(8,128)} fusion(f32[128,1024]{1,0:T(8,128)S(1)} %fusion.23, f32[128,1024]{1,0:T(8,128)S(1)} %fusion.22, bf16[64,128]{1,0:T(8,128)(2,1)S(1)} %get-tuple-element.19, bf16[8,8,1024]{2,1,0:T(8,128)(2,1)S(1)} %all-to-all-done), kind=kOutput, calls=%fused_computation.2 | convolution fusion | flops 17170432 | bytes 1720320 | tf_op jit(solution)/shard_map/dot_general | solution.py:32
  53.7 1.9 %collective-permute-done.4.refs_1_ = f32[8,1024]{1,0:T(8,128)S(1)} collective-permute-done((f32[8,1024]{1,0:T(8,128)S(1)}, f32[8,1024]{1,0:T(8,128)S(1)}, u32[]{:S(2)}, u32[]{:S(2)}) %collective-permute-start.4) | collective-permute-done | bytes 32800 | tf_op jit(solution)/shard_map/ppermute | solution.py:68
  55.6 2.3 %collective-permute-done.6.refs_3_ = f32[8,1024]{1,0:T(8,128)S(1)} collective-permute-done((f32[8,1024]{1,0:T(8,128)S(1)}, f32[8,1024]{1,0:T(8,128)S(1)}, u32[]{:S(2)}, u32[]{:S(2)}) %collective-permute-start.6) | collective-permute-done | bytes 32800 | tf_op jit(solution)/shard_map/ppermute | solution.py:68
  57.9 1.3 %close.1 = (f32[6,1024]{1,0:T(8,128)}, f32[256,1024]{1,0:T(8,128)}) custom-call(f32[8,1024]{1,0:T(8,128)S(1)} %get-tuple-element.31.refs_0_, f32[8,1024]{1,0:T(8,128)S(1)} %collective-permute-done.4.refs_1_, f32[8,1024]{1,0:T(8,128)S(1)} %collective-permute-done.5.refs_2_, f32[8,1024]{1,0:T(8,128)S(1)} %collective-permute-done.6.refs_3_, ...), custom_call_target="tpu_custom_call" | custom-call | flops 268435456 | bytes 1729536 | tf_op jit(solution)/shard_map/close/pallas_call | solution.py:79
  (37 shorter events, 1.1 us)
Async XLA Ops:
  3.2 15.6 %copy-start.1 = (bf16[256,1024]{1,0:T(8,128)(2,1)S(1)}, bf16[256,1024]{1,0:T(8,128)(2,1)}, u32[]{:S(2)}) copy-start(bf16[256,1024]{1,0:T(8,128)(2,1)} %bank_ref.1) | copy-start | bytes 1572868
  5.0 19.8 %collective-permute-start = (bf16[136,1024]{1,0:T(8,128)(2,1)S(1)}, bf16[136,1024]{1,0:T(8,128)(2,1)S(1)}, u32[]{:S(2)}, u32[]{:S(2)}) collective-permute-start(bf16[136,1024]{1,0:T(8,128)(2,1)S(1)} %fusion.4), channel_id=1, source_target_pairs={{0,4},{4,0},{8,12},{12,8},{16,20},{20,16},{24,28},{28,24},{1,5},{5... | collective-permute-start | bytes 835592 | tf_op jit(solution)/shard_map/ppermute | solution.py:36
  8.0 10.7 %all-to-all-start = ((bf16[8,8,1024]{2,1,0:T(8,128)(2,1)}), bf16[8,8,1024]{2,1,0:T(8,128)(2,1)S(1)}, u32[]{:S(2)}, u32[]{:S(2)}) async-start(bf16[8,8,1024]{2,1,0:T(8,128)(2,1)} %get-tuple-element.15), calls=%async_computation | async-start | bytes 262144 | tf_op jit(solution)/shard_map/all_to_all | solution.py:22
  14.0 0.7 %copy-start.2 = (f32[1,256]{1,0:T(1,128)S(1)}, f32[1,256]{1,0:T(1,128)}, u32[]{:S(2)}) copy-start(f32[1,256]{1,0:T(1,128)} %get-tuple-element.16) | copy-start | bytes 3076
  14.7 0.7 %copy-start.3 = (s32[128]{0:T(128)S(1)}, s32[128]{0:T(128)}, u32[]{:S(2)}) copy-start(s32[128]{0:T(128)} %param.9) | copy-start | bytes 1540
  19.9 4.7 %copy-start = (bf16[128,1024]{1,0:T(8,128)(2,1)S(1)}, bf16[128,1024]{1,0:T(8,128)(2,1)}, u32[]{:S(2)}) copy-start(bf16[128,1024]{1,0:T(8,128)(2,1)} %rows_ref.1) | copy-start | bytes 786436
  19.9 15.8 %all-to-all-start.1 = ((bf16[8,32,1024]{2,1,0:T(8,128)(2,1)}), bf16[8,32,1024]{2,1,0:T(8,128)(2,1)S(1)}, u32[]{:S(2)}, u32[]{:S(2)}) async-start(bf16[8,32,1024]{2,1,0:T(8,128)(2,1)} %bitcast.10), calls=%async_computation.1 | async-start | bytes 1048576 | tf_op jit(solution)/shard_map/all_to_all | solution.py:22
  36.2 1.3 %collective-permute-start.1 = (f32[66,128]{1,0:T(8,128)S(1)}, f32[66,128]{1,0:T(8,128)S(1)}, u32[]{:S(2)}, u32[]{:S(2)}) collective-permute-start(f32[66,128]{1,0:T(8,128)S(1)} %pad_maximum_fusion.1), channel_id=1, source_target_pairs={{0,1},{1,0},{2,3},{3,2},{4,5},{5,4},{6,7},{7,6},{8,9},{9,8},{10,11... | collective-permute-start | bytes 101384 | tf_op jit(solution)/shard_map/ppermute | solution.py:43
  37.4 5.8 %collective-permute-start.2 = (f32[66,128]{1,0:T(8,128)S(1)}, f32[66,128]{1,0:T(8,128)S(1)}, u32[]{:S(2)}, u32[]{:S(2)}) collective-permute-start(f32[66,128]{1,0:T(8,128)S(1)} %fusion.20), channel_id=1, source_target_pairs={{0,2},{1,3},{2,0},{3,1},{4,6},{5,7},{6,4},{7,5},{8,10},{9,11},{10,... | collective-permute-start | bytes 101384 | tf_op jit(solution)/shard_map/ppermute | solution.py:43
  39.0 18.9 %all-to-all-start.2 = ((bf16[4,64,1024]{2,1,0:T(8,128)(2,1)}), bf16[4,64,1024]{2,1,0:T(8,128)(2,1)S(1)}, u32[]{:S(2)}, u32[]{:S(2)}) async-start(bf16[4,64,1024]{2,1,0:T(8,128)(2,1)} %bitcast.9), calls=%async_computation.2 | async-start | bytes 1048576 | tf_op jit(solution)/shard_map/all_to_all | solution.py:22
  43.2 4.0 %collective-permute-start.3 = (f32[66,128]{1,0:T(8,128)S(1)}, f32[66,128]{1,0:T(8,128)S(1)}, u32[]{:S(2)}, u32[]{:S(2)}) collective-permute-start(f32[66,128]{1,0:T(8,128)S(1)} %add.92.sums_ref), channel_id=1, source_target_pairs={{0,4},{4,0},{8,12},{12,8},{16,20},{20,16},{24,28},{28,24},{1,5},{5... | collective-permute-start | bytes 101384 | tf_op jit(solution)/shard_map/ppermute | solution.py:36
  48.2 7.4 %collective-permute-start.4 = (f32[8,1024]{1,0:T(8,128)S(1)}, f32[8,1024]{1,0:T(8,128)S(1)}, u32[]{:S(2)}, u32[]{:S(2)}) collective-permute-start(f32[8,1024]{1,0:T(8,128)S(1)} %get-tuple-element.30), channel_id=1, source_target_pairs={{0,24},{4,28},{8,16},{12,20},{16,8},{20,12},{24,0},{28,4},{1,25},{... | collective-permute-start | bytes 98312 | tf_op jit(solution)/shard_map/ppermute | solution.py:68
  50.0 5.7 %collective-permute-start.5 = (f32[8,1024]{1,0:T(8,128)S(1)}, f32[8,1024]{1,0:T(8,128)S(1)}, u32[]{:S(2)}, u32[]{:S(2)}) collective-permute-start(f32[8,1024]{1,0:T(8,128)S(1)} %get-tuple-element.29), channel_id=1, source_target_pairs={{0,8},{4,12},{8,0},{12,4},{16,24},{20,28},{24,16},{28,20},{1,9},{5... | collective-permute-start | bytes 98312 | tf_op jit(solution)/shard_map/ppermute | solution.py:68
  50.0 7.9 %collective-permute-start.6 = (f32[8,1024]{1,0:T(8,128)S(1)}, f32[8,1024]{1,0:T(8,128)S(1)}, u32[]{:S(2)}, u32[]{:S(2)}) collective-permute-start(f32[8,1024]{1,0:T(8,128)S(1)} %get-tuple-element.28), channel_id=1, source_target_pairs={{0,16},{4,20},{8,24},{12,28},{16,0},{20,4},{24,8},{28,12},{1,17},{... | collective-permute-start | bytes 98312 | tf_op jit(solution)/shard_map/ppermute | solution.py:68
